TPU v7x, 32 devices: a whole 2x2x4 slice. The times are simulated.
32 devices in a mesh: batch: 4 (over z), expert: 8 (over y, x, core).
Axes of the slice: x: 2, y: 2, z: 4, core: 2. Of those that a mesh axis runs over, the one named last changes fastest.
Arguments:
- tokens: bfloat16 [8192, 1024], P(('batch', 'expert')), may hold values from -6 to 6
- doc_ends: int32 [32, 4], P(('batch', 'expert')), may hold values from 8 to 256, as said below
- routes: int32 [8192, 1], P(('batch', 'expert')), may hold values from 0 to 7, as said below
- w_query: bfloat16 [1024, 1024], replicated, may hold values from -0.1875 to 0.1875
- w_key: bfloat16 [1024, 1024], replicated, may hold values from -0.1875 to 0.1875
- w_value: bfloat16 [1024, 1024], replicated, may hold values from -0.1875 to 0.1875
- w_output: bfloat16 [1024, 1024], replicated, may hold values from -0.5 to 0.5
- attn_gain: float32 [1024], replicated, may hold values from 0.1 to 1.9
- centroids: float32 [8, 1024], replicated, may hold values from -0.15 to 0.15
- up_first: bfloat16 [8, 1024, 4096], P('expert'), may hold values from -0.1875 to 0.1875
- down_first: bfloat16 [8, 4096, 1024], P('expert'), may hold values from -0.09375 to 0.09375
- gain_first: float32 [8, 1024], P('expert'), may hold values from 0.1 to 1.9
- up_second: bfloat16 [8, 1024, 4096], P('expert'), may hold values from -0.1875 to 0.1875
- down_second: bfloat16 [8, 4096, 1024], P('expert'), may hold values from -0.09375 to 0.09375
- gain_second: float32 [8, 1024], P('expert'), may hold values from 0.1 to 1.9
- cotangent: bfloat16 [8192, 1024], P(('batch', 'expert')), may hold values from -6 to 6
Outputs:
- block_out: bfloat16 [8192, 1024], P(('batch', 'expert'))
- grad_tokens: float32 [8192, 1024], P(('batch', 'expert'))
- grad_query: float32 [1024, 1024], P(('batch', 'expert'))
- grad_key: float32 [1024, 1024], P(('batch', 'expert'))
- grad_value: float32 [1024, 1024], P(('batch', 'expert'))
- grad_output: float32 [1024, 1024], P(('batch', 'expert'))
- grad_attn_gain: float32 [1024], replicated
- grad_centroids: float32 [8, 1024], replicated
- grad_up_first: float32 [8, 1024, 4096], P('expert', None, 'batch')
- grad_down_first: float32 [8, 4096, 1024], P('expert', 'batch')
- grad_gain_first: float32 [8, 1024], P('expert', 'batch')
- grad_up_second: float32 [8, 1024, 4096], P('expert', None, 'batch')
- grad_down_second: float32 [8, 4096, 1024], P('expert', 'batch')
- grad_gain_second: float32 [8, 1024], P('expert', 'batch')
Inputs may be any that keep to these rules, and one draw needn't show every extreme that they name: `routes`: each device's 256 slots send at most 44 to any one expert; one expert, chosen by the draw, receives exactly 44 slots from every device. `doc_ends`: each row holds 4 nondecreasing document ends of one device's slots; slots at or past the last end are padding; a document may be empty; on some device the last end is 256, and on some device the first end is 8.
All inputs are finite; a program needn't handle non-finite values.
Results may differ from a plain program's by a relative error of at most 0.014.
Values may be sent and summed in bfloat16 or wider, within the bound.
A program may use at most 256 MiB of HBM per device.

v0:
```python
import jax
import jax.numpy as jnp
from jax import lax
from jax.sharding import PartitionSpec as P

HEADS = 16


EPSILON = 1e-05
MASKED = -1e30
HIGHEST = lax.Precision.HIGHEST


def layer_norm(stream, gain_vec):
    average = jnp.mean(stream, axis=-1, keepdims=True)
    centred = stream - average
    variance = jnp.mean(centred * centred, axis=-1, keepdims=True)
    return centred * lax.rsqrt(variance + EPSILON) * gain_vec


def block_scores(query_blk, key_rows, segment_blk, place_blk, segment, place, factor):
    raw = jnp.einsum("qhd,khd->hqk", query_blk, key_rows, preferred_element_type=jnp.float32)
    allowed = (segment_blk[:, None] == segment[None, :]) & (place[None, :] <= place_blk[:, None])
    return jnp.where(allowed[None], raw * factor, MASKED)


def attend_forward(queries, key_rows, value_rows, segment, place):
    tok_rows, head_count, head_width = queries.shape
    block_rows = min(512, tok_rows)
    factor = head_width ** (-0.5)

    def one_block(block_index):
        scores = block_scores(queries, key_rows, segment, place, segment, place, factor)
        row_peak = jnp.max(scores, axis=-1, keepdims=True)
        raised = jnp.exp(scores - row_peak)
        summed = jnp.sum(raised, axis=-1, keepdims=True)
        shares = (raised / summed).astype(jnp.bfloat16)
        mixed = jnp.einsum("hqk,khd->qhd", shares, value_rows, preferred_element_type=jnp.float32)
        return (mixed.astype(jnp.bfloat16), (row_peak + jnp.log(summed))[..., 0])

    mixed, log_total = lax.map(one_block, jnp.arange(tok_rows // block_rows))
    return (mixed.reshape(tok_rows, head_count * head_width), log_total)


def attend_backward(grad_mixed, queries, key_rows, value_rows, log_total, segment, place):
    tok_rows, head_count, head_width = queries.shape
    block_rows = min(512, tok_rows)
    factor = head_width ** (-0.5)

    def one_block(running, block_index):
        grad_keys, grad_values = running
        scores = block_scores(queries, key_rows, segment, place, segment, place, factor)
        row_total = lax.dynamic_index_in_dim(log_total, block_index, 0, keepdims=False)
        shares = jnp.exp(scores - row_total[..., None])
        shares_low = shares.astype(jnp.bfloat16)
        grad_shares = jnp.einsum(
            "qhd,khd->hqk", grad_mixed, value_rows, preferred_element_type=jnp.float32
        )
        grad_values = grad_values + jnp.einsum(
            "hqk,qhd->khd", shares_low, grad_mixed, preferred_element_type=jnp.float32
        )
        grad_scores = shares * (grad_shares - jnp.sum(shares * grad_shares, axis=-1, keepdims=True))
        grad_raw = (grad_scores * factor).astype(jnp.bfloat16)
        grad_query_blk = jnp.einsum(
            "hqk,khd->qhd", grad_raw, key_rows, preferred_element_type=jnp.float32
        )
        grad_keys = grad_keys + jnp.einsum(
            "hqk,qhd->khd", grad_raw, queries, preferred_element_type=jnp.float32
        )
        return ((grad_keys, grad_values), grad_query_blk)

    empty = jnp.zeros(queries.shape, jnp.float32)
    (grad_keys, grad_values), grad_queries = lax.scan(
        one_block, (empty, empty), jnp.arange(tok_rows // block_rows)
    )
    width_all = head_count * head_width
    return tuple(
        (
            member.reshape(tok_rows, width_all).astype(jnp.bfloat16)
            for member in (grad_queries, grad_keys, grad_values)
        )
    )


def sublayer_forward(stream, up_proj, down_proj, gain_vec):
    normed = layer_norm(stream, gain_vec).astype(jnp.bfloat16)
    pre_act = jnp.dot(normed, up_proj, preferred_element_type=jnp.float32)
    middle = jax.nn.gelu(pre_act).astype(jnp.bfloat16)
    result = stream + jnp.dot(middle, down_proj, preferred_element_type=jnp.float32)
    return (result, (stream, normed, pre_act, middle))


def sublayer_backward(grad_result, kept, up_proj, down_proj, gain_vec):
    stream, normed, pre_act, middle = kept
    grad_low = grad_result.astype(jnp.bfloat16)
    grad_down = jnp.einsum("rf,rd->fd", middle, grad_low, preferred_element_type=jnp.float32)
    grad_middle = jnp.einsum("rd,fd->rf", grad_low, down_proj, preferred_element_type=jnp.float32)
    gelu_pull = jax.vjp(jax.nn.gelu, pre_act)[1]
    grad_pre = gelu_pull(grad_middle)[0].astype(jnp.bfloat16)
    grad_up = jnp.einsum("rd,rf->df", normed, grad_pre, preferred_element_type=jnp.float32)
    grad_normed = jnp.einsum("rf,df->rd", grad_pre, up_proj, preferred_element_type=jnp.float32)
    norm_pull = jax.vjp(layer_norm, stream, gain_vec)[1]
    grad_stream, grad_gain = norm_pull(grad_normed)
    return (grad_result + grad_stream, grad_up, grad_down, grad_gain)


def slot_layout(tokens, routes):
    tok_rows = tokens.shape[0]
    expert_count = lax.axis_size("expert")
    capacity = 11 * tok_rows // (8 * expert_count)
    ones_int = (routes == jnp.arange(expert_count, dtype=jnp.int32)[None, :]).astype(jnp.int32)
    ranking = jnp.sum(jnp.cumsum(ones_int, axis=0) * ones_int, axis=1) - 1
    slot_index = routes[:, 0] * capacity + ranking
    return (expert_count, capacity, ones_int.astype(jnp.float32), slot_index)


def forward_pass(params):
    (
        tokens,
        doc_ends,
        routes,
        w_query,
        w_key,
        w_value,
        w_output,
        attn_gain,
        centroids,
        up_first,
        down_first,
        gain_first,
        up_second,
        down_second,
        gain_second,
    ) = params
    tok_rows, width_all = tokens.shape
    expert_count, capacity, chosen, slot_index = slot_layout(tokens, routes)
    place = jnp.arange(tok_rows, dtype=jnp.int32)
    segment = jnp.sum((place[:, None] >= doc_ends[0][None, :]).astype(jnp.int32), axis=1)
    live_mask = (place < doc_ends[0, -1]).astype(jnp.float32)[:, None]
    stream = tokens.astype(jnp.float32)
    normed = layer_norm(stream, attn_gain).astype(jnp.bfloat16)
    heads_shape = (tok_rows, HEADS, width_all // HEADS)
    queries = (
        jnp.dot(normed, w_query, preferred_element_type=jnp.float32)
        .astype(jnp.bfloat16)
        .reshape(heads_shape)
    )
    key_rows = (
        jnp.dot(normed, w_key, preferred_element_type=jnp.float32)
        .astype(jnp.bfloat16)
        .reshape(heads_shape)
    )
    value_rows = (
        jnp.dot(normed, w_value, preferred_element_type=jnp.float32)
        .astype(jnp.bfloat16)
        .reshape(heads_shape)
    )
    mixed, log_total = attend_forward(queries, key_rows, value_rows, segment, place)
    hidden = stream + jnp.dot(mixed, w_output, preferred_element_type=jnp.float32)
    score = jnp.sum(jnp.dot(hidden, centroids.T, precision=HIGHEST) * chosen, axis=1, keepdims=True)
    gating = jax.nn.sigmoid(score)
    routed = hidden.astype(jnp.bfloat16)
    outgoing = (
        jnp.zeros((expert_count * capacity, width_all), jnp.bfloat16).at[slot_index].set(routed)
    )
    arrived = lax.all_to_all(
        outgoing.reshape(expert_count, capacity, width_all),
        "expert",
        split_axis=0,
        concat_axis=0,
        tiled=True,
    )
    arrived = arrived.reshape(expert_count * capacity, width_all).astype(jnp.float32)
    stream_one, kept_one = sublayer_forward(arrived, up_first[0], down_first[0], gain_first[0])
    stream_two, kept_two = sublayer_forward(
        stream_one, up_second[0], down_second[0], gain_second[0]
    )
    expert_low = stream_two.astype(jnp.bfloat16).reshape(expert_count, capacity, width_all)
    came_back = lax.all_to_all(expert_low, "expert", split_axis=0, concat_axis=0, tiled=True)
    returned = came_back.reshape(expert_count * capacity, width_all)[slot_index].astype(jnp.float32)
    block_out = (live_mask * (gating * returned + (1.0 - gating) * hidden)).astype(jnp.bfloat16)
    kept = (
        stream,
        normed,
        queries,
        key_rows,
        value_rows,
        log_total,
        mixed,
        hidden,
        gating,
        returned,
        kept_one,
        kept_two,
        segment,
        place,
        live_mask,
    )
    return (block_out, kept)


def per_device(
    tokens,
    doc_ends,
    routes,
    w_query,
    w_key,
    w_value,
    w_output,
    attn_gain,
    centroids,
    up_first,
    down_first,
    gain_first,
    up_second,
    down_second,
    gain_second,
    cotangent,
):
    params = (
        tokens,
        doc_ends,
        routes,
        w_query,
        w_key,
        w_value,
        w_output,
        attn_gain,
        centroids,
        up_first,
        down_first,
        gain_first,
        up_second,
        down_second,
        gain_second,
    )
    block_out, kept = forward_pass(params)
    replayed = lax.optimization_barrier((params, block_out))
    kept = forward_pass(replayed[0])[1]
    (
        stream,
        normed,
        queries,
        key_rows,
        value_rows,
        log_total,
        mixed,
        hidden,
        gating,
        returned,
        kept_one,
        kept_two,
        segment,
        place,
        live_mask,
    ) = kept
    tok_rows, width_all = tokens.shape
    expert_count, capacity, chosen, slot_index = slot_layout(tokens, routes)
    grad_block = cotangent.astype(jnp.float32) * live_mask
    grad_sent = (gating * grad_block).astype(jnp.bfloat16)
    grad_gating = jnp.sum(grad_block * (returned - hidden), axis=1, keepdims=True)
    grad_score = grad_gating * gating * (1.0 - gating)
    grad_buffer = (
        jnp.zeros((expert_count * capacity, width_all), jnp.bfloat16).at[slot_index].set(grad_sent)
    )
    grad_rows = lax.all_to_all(
        grad_buffer.reshape(expert_count, capacity, width_all),
        "expert",
        split_axis=0,
        concat_axis=0,
        tiled=True,
    )
    grad_rows = grad_rows.reshape(expert_count * capacity, width_all).astype(jnp.float32)
    grad_stream_one, up_two_grad, down_two_grad, gain_two_grad = sublayer_backward(
        grad_rows, kept_two, up_second[0], down_second[0], gain_second[0]
    )
    grad_arrived, up_one_grad, down_one_grad, gain_one_grad = sublayer_backward(
        grad_stream_one, kept_one, up_first[0], down_first[0], gain_first[0]
    )
    grad_home = lax.all_to_all(
        grad_arrived.astype(jnp.bfloat16).reshape(expert_count, capacity, width_all),
        "expert",
        split_axis=0,
        concat_axis=0,
        tiled=True,
    )
    grad_routed = grad_home.reshape(expert_count * capacity, width_all)[slot_index].astype(
        jnp.float32
    )
    own_centroid = jnp.dot(chosen, centroids, precision=HIGHEST)
    grad_hidden = (1.0 - gating) * grad_block + grad_routed + grad_score * own_centroid
    grad_centroids = jnp.dot(chosen.T, grad_score * hidden, precision=HIGHEST)
    grad_attn_out = grad_hidden.astype(jnp.bfloat16)
    grad_output_w = jnp.einsum(
        "td,te->de", mixed, grad_attn_out, preferred_element_type=jnp.float32
    )
    grad_mixed = jnp.einsum(
        "te,de->td", grad_attn_out, w_output, preferred_element_type=jnp.float32
    ).astype(jnp.bfloat16)
    grad_q, grad_k, grad_v = attend_backward(
        grad_mixed.reshape(queries.shape), queries, key_rows, value_rows, log_total, segment, place
    )
    grad_query_w = jnp.einsum("td,te->de", normed, grad_q, preferred_element_type=jnp.float32)
    grad_key_w = jnp.einsum("td,te->de", normed, grad_k, preferred_element_type=jnp.float32)
    grad_value_w = jnp.einsum("td,te->de", normed, grad_v, preferred_element_type=jnp.float32)
    grad_normed = jnp.einsum("te,de->td", grad_q, w_query, preferred_element_type=jnp.float32)
    grad_normed = grad_normed + jnp.einsum(
        "te,de->td", grad_k, w_key, preferred_element_type=jnp.float32
    )
    grad_normed = grad_normed + jnp.einsum(
        "te,de->td", grad_v, w_value, preferred_element_type=jnp.float32
    )
    norm_pull = jax.vjp(layer_norm, stream, attn_gain)[1]
    grad_input_norm, grad_gain_att = norm_pull(grad_normed)
    grad_tokens = grad_hidden + grad_input_norm
    dense = (
        lax.psum_scatter(grad_query_w, ("batch", "expert"), scatter_dimension=0, tiled=True),
        lax.psum_scatter(grad_key_w, ("batch", "expert"), scatter_dimension=0, tiled=True),
        lax.psum_scatter(grad_value_w, ("batch", "expert"), scatter_dimension=0, tiled=True),
        lax.psum_scatter(grad_output_w, ("batch", "expert"), scatter_dimension=0, tiled=True),
    )
    small = lax.psum((grad_gain_att, grad_centroids), ("batch", "expert"))
    expert_parts = (
        lax.psum_scatter(
            up_one_grad[None].astype(jnp.bfloat16), "batch", scatter_dimension=2, tiled=True
        ).astype(jnp.float32),
        lax.psum_scatter(
            down_one_grad[None].astype(jnp.bfloat16), "batch", scatter_dimension=1, tiled=True
        ).astype(jnp.float32),
        lax.psum_scatter(
            gain_one_grad[None].astype(jnp.bfloat16), "batch", scatter_dimension=1, tiled=True
        ).astype(jnp.float32),
        lax.psum_scatter(
            up_two_grad[None].astype(jnp.bfloat16), "batch", scatter_dimension=2, tiled=True
        ).astype(jnp.float32),
        lax.psum_scatter(
            down_two_grad[None].astype(jnp.bfloat16), "batch", scatter_dimension=1, tiled=True
        ).astype(jnp.float32),
        lax.psum_scatter(
            gain_two_grad[None].astype(jnp.bfloat16), "batch", scatter_dimension=1, tiled=True
        ).astype(jnp.float32),
    )
    return (
        block_out,
        grad_tokens,
        dense[0],
        dense[1],
        dense[2],
        dense[3],
        small[0],
        small[1],
        expert_parts[0],
        expert_parts[1],
        expert_parts[2],
        expert_parts[3],
        expert_parts[4],
        expert_parts[5],
    )


def solution(mesh):
    return jax.shard_map(
        per_device,
        mesh=mesh,
        in_specs=(
            P(("batch", "expert"), None),
            P(("batch", "expert"), None),
            P(("batch", "expert"), None),
            P(),
            P(),
            P(),
            P(),
            P(),
            P(),
            P("expert", None, None),
            P("expert", None, None),
            P("expert", None),
            P("expert", None, None),
            P("expert", None, None),
            P("expert", None),
            P(("batch", "expert"), None),
        ),
        out_specs=(
            P(("batch", "expert"), None),
            P(("batch", "expert"), None),
            P(("batch", "expert"), None),
            P(("batch", "expert"), None),
            P(("batch", "expert"), None),
            P(("batch", "expert"), None),
            P(),
            P(),
            P("expert", None, "batch"),
            P("expert", "batch", None),
            P("expert", "batch"),
            P("expert", None, "batch"),
            P("expert", "batch", None),
            P("expert", "batch"),
        ),
        check_vma=False,
    )
```

profile of v0, /device:TPU:0, one launch (start us, length us, event | category | flops | bytes accessed | tf_op | source)
XLA Modules:
  0.0 1436.5 jit_solution(3034619040677998255)
XLA Ops:
  9.9 2.6 convolution_convert_fusion.6
  14.0 3.2 convolution_convert_fusion.5
  19.2 3.1 convolution_convert_fusion.4
  25.4 4.7 fusion.205
  30.0 2.8 fusion.109
  34.6 2.6 scatter_custom_fusion
  38.2 17.7 %all_to_all.30 = bf16[8,44,1024]{2,1,0:T(8,128)(2,1)S(1)} all-to-all(bf16[8,44,1024]{2,1,0:T(8,128)(2,1)} %reshape.499), channel_id=1, replica_groups=mesh['batch'=4,'expert'=8] {'expert'}, dimensions={0} | all-to-all | bytes 1441792 | tf_op jit(solution)/shard_map/all_to_all | solution.py:166
  57.7 2.2 convert_element_type.323
  61.1 13.9 fusion.206
  76.7 13.1 add_convert_fusion.2
  90.7 4.6 all-to-all-start.1
  96.6 2.2 fusion.124
  98.8 9.2 all-to-all-done.1
  111.2 2.4 multiply_convert_fusion.9
  117.9 3.3 convolution_convert_fusion.2
  121.2 2.1 copy.75
  123.3 3.2 convolution_convert_fusion.1
  126.4 2.1 copy.76
  128.7 2.0 fusion.209
  135.7 3.3 scatter_custom_fusion.2
  141.1 4.2 all-to-all-start.3
  148.1 2.5 scatter_custom_fusion.1
  151.6 6.3 all-to-all-done.3
  157.9 4.2 all-to-all-start.2
  168.9 9.2 fusion.8
  179.4 9.3 fusion.210
  189.9 8.5 fusion.4
  199.7 9.7 fusion.39
  209.4 7.6 multiply_reduce_fusion.3
  220.1 9.8 fusion.32
  230.0 5.1 multiply_reduce_fusion.4
  237.7 10.2 convert_bitcast_fusion.3
  248.4 11.0 convert_bitcast_fusion.2
  259.5 10.2 convert_bitcast_fusion.1
  270.0 11.0 convert_bitcast_fusion
  281.8 2.3 fusion.203
  287.4 4.1 all-to-all-start.4
  291.5 10.1 add_convert_fusion
  304.1 4.2 all-to-all-start.5
  309.9 2.1 gather_fusion.1
  312.0 8.9 all-to-all-done.5
  326.0 2.2 fusion.104
  332.1 2.8 fusion.211
  334.8 8.9 fusion.110
  343.7 4.0 fusion.198
  347.8 8.9 fusion.113
  356.7 3.9 fusion.196
  360.7 3.0 fusion.105
  364.5 2.8 fusion.194
  367.6 4.0 fusion.158
  374.7 2.4 fusion.212
  381.3 45.3 %all-reduce = (f32[1024]{0:T(1024)}, f32[8,1024]{1,0:T(8,128)}) all-reduce(f32[1024]{0:T(1024)S(1)} %get-tuple-element.126, f32[8,1024]{1,0:T(8,128)S(1)} %fusion.133), channel_id=1, replica_groups=mesh['batch'=4,'expert'=8] {'batch','expert'}, use_global_device_ids=true, to_apply=%region_42.43 | all-reduce | flops 9216 | bytes 73728 | tf_op jit(solution)/shard_map/psum | solution.py:322
  426.6 2.9 add_add_fusion.4
  429.5 4.2 convert_element_type.378
  433.7 137.6 %reduce-scatter.25.cloned.1.call-done = bf16[1,1024,1024]{2,1,0:T(8,128)(2,1)} async-done(((bf16[1,4096,1024]{2,1,0:T(8,128)(2,1)}), bf16[1,1024,1024]{2,1,0:T(8,128)(2,1)}) %reduce-scatter.25.cloned.1.call-update) | async-done | bytes 2097168 | tf_op jit(solution)/shard_map/reduce_scatter | solution.py:327
  571.3 4.1 convert_element_type.381
  575.4 143.4 %reduce-scatter.27.cloned.1.call-done = bf16[1,1024,1024]{2,1,0:T(8,128)(2,1)} async-done(((bf16[1,1024,4096]{2,1,0:T(8,128)(2,1)}), bf16[1,1024,1024]{2,1,0:T(8,128)(2,1)}) %reduce-scatter.27.cloned.1.call-update) | async-done | bytes 2097168 | tf_op jit(solution)/shard_map/reduce_scatter | solution.py:333
  718.7 4.1 convert_element_type.387
  722.8 143.4 %reduce-scatter.29.cloned.1.call-done = bf16[1,1024,1024]{2,1,0:T(8,128)(2,1)} async-done(((bf16[1,4096,1024]{2,1,0:T(8,128)(2,1)}), bf16[1,1024,1024]{2,1,0:T(8,128)(2,1)}) %reduce-scatter.29.cloned.1.call-update) | async-done | bytes 2097168 | tf_op jit(solution)/shard_map/reduce_scatter | solution.py:336
  866.2 4.1 convert_element_type.390
  870.3 140.1 %reduce-scatter.15.cloned.1.call-done = f32[32,1024]{1,0:T(8,128)} async-done(((f32[1024,1024]{1,0:T(8,128)}), f32[32,1024]{1,0:T(8,128)}) %reduce-scatter.15.cloned.1.call-update) | async-done | bytes 131088 | tf_op jit(solution)/shard_map/reduce_scatter | solution.py:317
  1010.4 139.7 %reduce-scatter.17.cloned.1.call-done = f32[32,1024]{1,0:T(8,128)} async-done(((f32[1024,1024]{1,0:T(8,128)}), f32[32,1024]{1,0:T(8,128)}) %reduce-scatter.17.cloned.1.call-update) | async-done | bytes 131088 | tf_op jit(solution)/shard_map/reduce_scatter | solution.py:318
  1150.1 139.7 %reduce-scatter.19.cloned.1.call-done = f32[32,1024]{1,0:T(8,128)} async-done(((f32[1024,1024]{1,0:T(8,128)}), f32[32,1024]{1,0:T(8,128)}) %reduce-scatter.19.cloned.1.call-update) | async-done | bytes 131088 | tf_op jit(solution)/shard_map/reduce_scatter | solution.py:319
  1289.7 139.6 %reduce-scatter.21.cloned.1.call-done = f32[32,1024]{1,0:T(8,128)} async-done(((f32[1024,1024]{1,0:T(8,128)}), f32[32,1024]{1,0:T(8,128)}) %reduce-scatter.21.cloned.1.call-update) | async-done | bytes 131088 | tf_op jit(solution)/shard_map/reduce_scatter | solution.py:320
  (264 shorter events, 79.4 us)
Async XLA Ops:
  7.2 6.8 copy-start.1
  7.2 6.8 copy-start.30
  7.2 6.6 copy-start.62
  14.0 10.4 copy-start.32
  34.6 21.9 %copy-start.38 = (f32[1,1024]{1,0:T(1,128)S(1)}, f32[1,1024]{1,0:T(1,128)}, u32[]{:S(2)}) copy-start(f32[1,1024]{1,0:T(1,128)} %param.27) | copy-start | bytes 12292
  61.1 15.6 %copy-start.56 = (f32[1,1024]{1,0:T(1,128)S(1)}, f32[1,1024]{1,0:T(1,128)}, u32[]{:S(2)}) copy-start(f32[1,1024]{1,0:T(1,128)} %param.30) | copy-start | bytes 12292
  76.6 20.0 %copy-start.28 = (f32[8,1024]{1,0:T(8,128)S(1)}, f32[8,1024]{1,0:T(8,128)}, u32[]{:S(2)}) copy-start(f32[8,1024]{1,0:T(8,128)} %param.24) | copy-start | bytes 98308
  90.7 17.2 %all-to-all-start.1 = ((bf16[8,44,1024]{2,1,0:T(8,128)(2,1)}), bf16[8,44,1024]{2,1,0:T(8,128)(2,1)}, u32[]{:S(2)}, u32[]{:S(2)}) async-start(bf16[8,44,1024]{2,1,0:T(8,128)(2,1)} %reshape.500), calls=%async_computation.1 | async-start | bytes 1572864 | tf_op jit(solution)/shard_map/all_to_all | solution.py:179
  96.6 17.0 %copy-start.50 = (s32[1024]{0:T(1024)}, s32[1024]{0:T(1024)S(1)}, u32[]{:S(2)}) copy-start(s32[1024]{0:T(1024)S(1)} %pad_clamp_fusion.1) | copy-start | bytes 12292
  114.6 21.1 %copy-start.60 = (s32[256,1]{0,1:T(1,128)}, s32[256,1]{0,1:T(1,128)S(1)}, u32[]{:S(2)}) copy-start(s32[256,1]{0,1:T(1,128)S(1)} %compare_select_fusion) | copy-start | bytes 3076
  114.7 8.6 copy-start.36
  115.0 6.2 copy-start.51
  115.0 8.2 copy-start.40
  117.9 13.5 copy-start.22
  135.7 10.8 copy-start.4
  141.1 16.8 %all-to-all-start.3 = ((bf16[8,44,1024]{2,1,0:T(8,128)(2,1)}), bf16[8,44,1024]{2,1,0:T(8,128)(2,1)}, u32[]{:S(2)}, u32[]{:S(2)}) async-start(bf16[8,44,1024]{2,1,0:T(8,128)(2,1)} %reshape.509), calls=%async_computation.3 | async-start | bytes 1572864 | tf_op jit(solution)/shard_map/all_to_all | solution.py:166
  146.5 21.4 %copy-start.46 = (f32[256]{0:T(256)}, f32[256]{0:T(256)S(1)}, u32[]{:S(2)}) copy-start(f32[256]{0:T(256)S(1)} %compare_convert_fusion) | copy-start | bytes 3076
  148.0 20.9 %copy-start.48 = (f32[256]{0:T(256)}, f32[256]{0:T(256)S(1)}, u32[]{:S(2)}) copy-start(f32[256]{0:T(256)S(1)} %get-tuple-element.131) | copy-start | bytes 3076
  157.9 40.5 %all-to-all-start.2 = ((bf16[8,44,1024]{2,1,0:T(8,128)(2,1)}), bf16[8,44,1024]{2,1,0:T(8,128)(2,1)}, u32[]{:S(2)}, u32[]{:S(2)}) async-start(bf16[8,44,1024]{2,1,0:T(8,128)(2,1)} %reshape.506), calls=%async_computation.2 | async-start | bytes 1572864 | tf_op jit(solution)/shard_map/all_to_all | solution.py:266
  162.1 209.6 %reduce-scatter.31.cloned.1.call-start = ((), (), s32[]{:S(2)}) async-start(), calls=%async_computation.24 | async-start | bytes 327680
  179.4 9.4 copy-start.16
  179.4 10.5 copy-start.57
  188.8 20.6 %copy-start.44 = (f32[352]{0:T(512)}, f32[352]{0:T(512)S(1)}, u32[]{:S(2)}) copy-start(f32[352]{0:T(512)S(1)} %broadcast_multiply_fusion.2) | copy-start | bytes 4228
  189.1 20.3 %copy-start.55 = (f32[352]{0:T(512)}, f32[352]{0:T(512)S(1)}, u32[]{:S(2)}) copy-start(f32[352]{0:T(512)S(1)} %fusion.173) | copy-start | bytes 4228
  199.7 9.7 copy-start.11
  199.7 9.7 copy-start.15
  199.7 9.7 copy-start.58
  209.4 7.6 copy-start.63
  217.0 12.9 slice-start
  220.1 9.8 copy-start.17
  220.1 9.8 copy-start.39
  220.1 9.8 copy-start.53
  220.1 9.8 copy-start.54
  220.1 9.8 slice-start.1
  230.0 5.1 copy-start.64
  236.0 137.2 %reduce-scatter.33.cloned.1.call-start = ((), (), s32[]{:S(2)}) async-start(), calls=%async_computation.25 | async-start | bytes 327680
  237.7 191.8 %reduce-scatter.23.cloned.1.call-start = ((), (), s32[]{:S(2)}) async-start(), calls=%async_computation.20 | async-start | bytes 10485760 | tf_op jit(solution)/shard_map/reduce_scatter | solution.py:324
  248.0 323.3 %reduce-scatter.25.cloned.1.call-start = ((), (), s32[]{:S(2)}) async-start(), calls=%async_computation.21 | async-start | bytes 10485760 | tf_op jit(solution)/shard_map/reduce_scatter | solution.py:327
  259.5 459.3 %reduce-scatter.27.cloned.1.call-start = ((), (), s32[]{:S(2)}) async-start(), calls=%async_computation.22 | async-start | bytes 10485760 | tf_op jit(solution)/shard_map/reduce_scatter | solution.py:333
  269.7 596.4 %reduce-scatter.29.cloned.1.call-start = ((), (), s32[]{:S(2)}) async-start(), calls=%async_computation.23 | async-start | bytes 10485760 | tf_op jit(solution)/shard_map/reduce_scatter | solution.py:336
  281.0 3.1 copy-start.13
  287.4 16.7 %all-to-all-start.4 = ((bf16[8,44,1024]{2,1,0:T(8,128)(2,1)}), bf16[8,44,1024]{2,1,0:T(8,128)(2,1)S(1)}, u32[]{:S(2)}, u32[]{:S(2)}) async-start(bf16[8,44,1024]{2,1,0:T(8,128)(2,1)} %reshape.510), calls=%async_computation.4 | async-start | bytes 1572864 | tf_op jit(solution)/shard_map/all_to_all | solution.py:280
  291.5 17.1 %copy-start.61 = (s32[256,1]{0,1:T(1,128)S(1)}, s32[256,1]{0,1:T(1,128)}, u32[]{:S(2)}) copy-start(s32[256,1]{0,1:T(1,128)} %copy-done.60) | copy-start | bytes 3076
  291.5 17.1 %copy-start.35 = (f32[16,256]{1,0:T(8,128)S(1)}, f32[16,256]{1,0:T(8,128)}, u32[]{:S(2)}) copy-start(f32[16,256]{1,0:T(8,128)} %copy-done.34) | copy-start | bytes 49156
  304.1 4.5 copy-start.21
  304.1 16.8 %all-to-all-start.5 = ((bf16[8,44,1024]{2,1,0:T(8,128)(2,1)}), bf16[8,44,1024]{2,1,0:T(8,128)(2,1)}, u32[]{:S(2)}, u32[]{:S(2)}) async-start(bf16[8,44,1024]{2,1,0:T(8,128)(2,1)} %reshape.512), calls=%async_computation.5 | async-start | bytes 1572864 | tf_op jit(solution)/shard_map/all_to_all | solution.py:179
  308.3 702.1 %reduce-scatter.15.cloned.1.call-start = ((), (), s32[]{:S(2)}) async-start(), calls=%async_computation.16 | async-start | bytes 4325376 | tf_op jit(solution)/shard_map/reduce_scatter | solution.py:317
  312.0 12.1 copy-start.18
  312.0 12.1 copy-start.47
  312.0 14.0 copy-start.49
  312.0 14.0 copy-start.29
  312.0 14.1 copy-start.33
  312.0 14.0 copy-start.59
  324.1 5.2 copy-start.8
  324.1 8.0 copy-start.23
  334.8 8.9 copy-start.2
  334.8 8.9 copy-start.31
  334.8 8.9 copy-start.37
  334.8 8.9 copy-start.41
  347.8 802.3 %reduce-scatter.17.cloned.1.call-start = ((), (), s32[]{:S(2)}) async-start(), calls=%async_computation.17 | async-start | bytes 4325376 | tf_op jit(solution)/shard_map/reduce_scatter | solution.py:318
  360.6 929.1 %reduce-scatter.19.cloned.1.call-start = ((), (), s32[]{:S(2)}) async-start(), calls=%async_computation.18 | async-start | bytes 4325376 | tf_op jit(solution)/shard_map/reduce_scatter | solution.py:319
  367.3 7.4 copy-start.25
  367.3 1062.1 %reduce-scatter.21.cloned.1.call-start = ((), (), s32[]{:S(2)}) async-start(), calls=%async_computation.19 | async-start | bytes 4325376 | tf_op jit(solution)/shard_map/reduce_scatter | solution.py:320
  374.7 4.3 copy-start.20
  (18 other events, 35.9 us)
Sparse Core Ops, SparseCore 0:
  236.1 21.2 reduce-scatter.30
  259.8 17.8 reduce-scatter.32
  280.0 143.7 reduce-scatter.22
  426.0 145.2 reduce-scatter.24
  573.5 145.1 reduce-scatter.26
  720.9 145.1 reduce-scatter.28
  869.0 141.2 reduce-scatter.14
  1013.2 136.8 reduce-scatter.16
  1152.9 136.7 reduce-scatter.18
  1292.4 136.8 reduce-scatter.20
where the time goes:
time: 1440 us
  waiting for transfers between devices  1010 us (70%)
  matrix products  220 us (15%)
  blocking collectives  63 us (4%)
  other arithmetic  55.1 us (4%)
  local copies, waits for them, and re-layouts  51 us (4%)
  starting transfers between devices  22.9 us (2%)
  between operations  15.5 us (1%)
    reduce_scatter x1, waiting for transfers between devices, per_device(): lax.psum_scatter(down_two_grad[None].astype(jnp.bfloat16), 'batch', scatt...  143 us
    reduce_scatter x1, waiting for transfers between devices, per_device(): lax.psum_scatter(up_two_grad[None].astype(jnp.bfloat16), 'batch', scatter...  143 us
    reduce_scatter x1, waiting for transfers between devices, per_device(): lax.psum_scatter(grad_query_w, ('batch', 'expert'), scatter_dimension=0,...  140 us
    reduce_scatter x1, waiting for transfers between devices, per_device(): lax.psum_scatter(grad_key_w, ('batch', 'expert'), scatter_dimension=0, ti...  140 us
    reduce_scatter x1, waiting for transfers between devices, per_device(): lax.psum_scatter(grad_value_w, ('batch', 'expert'), scatter_dimension=0,...  140 us
    reduce_scatter x1, waiting for transfers between devices, per_device(): lax.psum_scatter(grad_output_w, ('batch', 'expert'), scatter_dimension=0,...  140 us
    reduce_scatter x1, waiting for transfers between devices, per_device(): lax.psum_scatter(down_one_grad[None].astype(jnp.bfloat16), 'batch', scatt...  138 us
    dot_general x4, matrix products, sublayer_forward(): jnp.dot(middle, down_proj, preferred_element_type=jnp.float32)  46.4 us
  transfers between devices with their start and end apart: 15, of which 11 were waited for; matrix products, arithmetic and copies ran while one was open for 13% of the time, Pallas kernels for 0%

commit v1 on v0

--- a/solution.py
+++ b/solution.py
@@ -93,15 +93,72 @@
 def sublayer_backward(grad_result, kept, up_proj, down_proj, gain_vec):
     stream, normed, pre_act, middle = kept
     grad_low = grad_result.astype(jnp.bfloat16)
-    grad_down = jnp.einsum("rf,rd->fd", middle, grad_low, preferred_element_type=jnp.float32)
     grad_middle = jnp.einsum("rd,fd->rf", grad_low, down_proj, preferred_element_type=jnp.float32)
     gelu_pull = jax.vjp(jax.nn.gelu, pre_act)[1]
     grad_pre = gelu_pull(grad_middle)[0].astype(jnp.bfloat16)
-    grad_up = jnp.einsum("rd,rf->df", normed, grad_pre, preferred_element_type=jnp.float32)
     grad_normed = jnp.einsum("rf,df->rd", grad_pre, up_proj, preferred_element_type=jnp.float32)
     norm_pull = jax.vjp(layer_norm, stream, gain_vec)[1]
     grad_stream, grad_gain = norm_pull(grad_normed)
-    return (grad_result + grad_stream, grad_up, grad_down, grad_gain)
+    return (grad_result + grad_stream, grad_low, grad_gain)
+
+
+def ring_rows(rows, axis):
+    count = lax.axis_size(axis)
+    back = [(i, (i - 1) % count) for i in range(count)]
+    held = [rows]
+    for _ in range(count - 1):
+        held.append(lax.ppermute(held[-1], axis, back))
+    return jnp.concatenate(held, axis=0)
+
+
+def weight_grads(normed_rows, grad_rows, up_proj, down_proj):
+    count = lax.axis_size("batch")
+    width = up_proj.shape[1] // count
+    first = lax.axis_index("batch") * width
+    up_part = lax.dynamic_slice_in_dim(up_proj, first, width, 1)
+    down_part = lax.dynamic_slice_in_dim(down_proj, first, width, 0)
+    pre_act = jnp.dot(normed_rows, up_part, preferred_element_type=jnp.float32)
+    middle, gelu_pull = jax.vjp(jax.nn.gelu, pre_act)
+    grad_middle = jnp.einsum("rd,fd->rf", grad_rows, down_part, preferred_element_type=jnp.float32)
+    grad_pre = gelu_pull(grad_middle)[0].astype(jnp.bfloat16)
+    grad_down = jnp.einsum(
+        "rf,rd->fd", middle.astype(jnp.bfloat16), grad_rows, preferred_element_type=jnp.float32
+    )
+    grad_up = jnp.einsum("rd,rf->df", normed_rows, grad_pre, preferred_element_type=jnp.float32)
+    return grad_up, grad_down
+
+
+def halve(blocks, axis, bit, dim):
+    count = lax.axis_size(axis)
+    mine = (lax.axis_index(axis) // bit) % 2
+    kept = lax.dynamic_index_in_dim(blocks, mine, dim, keepdims=False)
+    sent = lax.dynamic_index_in_dim(blocks, 1 - mine, dim, keepdims=False)
+    got = lax.ppermute(sent, axis, [(i, i ^ bit) for i in range(count)])
+    return (kept.astype(jnp.float32) + got.astype(jnp.float32)).astype(blocks.dtype)
+
+
+def scatter_sum(parts):
+    experts, groups = lax.axis_size("expert"), lax.axis_size("batch")
+    kinds, rows, width = parts.shape
+    bits_e = experts.bit_length() - 1
+    bits_b = groups.bit_length() - 1
+    shape = (kinds,) + (2,) * (bits_b + bits_e) + (rows // (experts * groups), width)
+    blocks = parts.reshape(shape)
+    for k in range(bits_e):
+        blocks = halve(blocks, "expert", 1 << k, bits_b + bits_e - k)
+    for k in range(bits_b):
+        blocks = halve(blocks, "batch", 1 << k, bits_b - k)
+    return blocks
+
+
+def all_sum(value):
+    for axis in ("expert", "batch"):
+        count = lax.axis_size(axis)
+        bit = 1
+        while bit < count:
+            value = value + lax.ppermute(value, axis, [(i, i ^ bit) for i in range(count)])
+            bit *= 2
+    return value
 
 
 def slot_layout(tokens, routes):
@@ -235,8 +292,6 @@
         gain_second,
     )
     block_out, kept = forward_pass(params)
-    replayed = lax.optimization_barrier((params, block_out))
-    kept = forward_pass(replayed[0])[1]
     (
         stream,
         normed,
@@ -271,10 +326,10 @@
         tiled=True,
     )
     grad_rows = grad_rows.reshape(expert_count * capacity, width_all).astype(jnp.float32)
-    grad_stream_one, up_two_grad, down_two_grad, gain_two_grad = sublayer_backward(
+    grad_stream_one, low_two, gain_two_grad = sublayer_backward(
         grad_rows, kept_two, up_second[0], down_second[0], gain_second[0]
     )
-    grad_arrived, up_one_grad, down_one_grad, gain_one_grad = sublayer_backward(
+    grad_arrived, low_one, gain_one_grad = sublayer_backward(
         grad_stream_one, kept_one, up_first[0], down_first[0], gain_first[0]
     )
     grad_home = lax.all_to_all(
@@ -313,32 +368,28 @@
     norm_pull = jax.vjp(layer_norm, stream, attn_gain)[1]
     grad_input_norm, grad_gain_att = norm_pull(grad_normed)
     grad_tokens = grad_hidden + grad_input_norm
-    dense = (
-        lax.psum_scatter(grad_query_w, ("batch", "expert"), scatter_dimension=0, tiled=True),
-        lax.psum_scatter(grad_key_w, ("batch", "expert"), scatter_dimension=0, tiled=True),
-        lax.psum_scatter(grad_value_w, ("batch", "expert"), scatter_dimension=0, tiled=True),
-        lax.psum_scatter(grad_output_w, ("batch", "expert"), scatter_dimension=0, tiled=True),
-    )
-    small = lax.psum((grad_gain_att, grad_centroids), ("batch", "expert"))
+    dense = scatter_sum(
+        jnp.stack((grad_query_w, grad_key_w, grad_value_w, grad_output_w)).astype(jnp.bfloat16)
+    ).astype(jnp.float32)
+    small = all_sum(jnp.concatenate((grad_gain_att[None], grad_centroids), axis=0))
+    up_two_grad, down_two_grad = weight_grads(
+        ring_rows(kept_two[1], "batch"), ring_rows(low_two, "batch"), up_second[0], down_second[0]
+    )
+    up_one_grad, down_one_grad = weight_grads(
+        ring_rows(kept_one[1], "batch"), ring_rows(low_one, "batch"), up_first[0], down_first[0]
+    )
+    gains = lax.all_gather(jnp.stack((gain_one_grad, gain_two_grad)), "batch")
+    gain_part = gain_one_grad.shape[0] // lax.axis_size("batch")
+    gains = lax.dynamic_slice_in_dim(
+        jnp.sum(gains, axis=0), lax.axis_index("batch") * gain_part, gain_part, 1
+    )
     expert_parts = (
-        lax.psum_scatter(
-            up_one_grad[None].astype(jnp.bfloat16), "batch", scatter_dimension=2, tiled=True
-        ).astype(jnp.float32),
-        lax.psum_scatter(
-            down_one_grad[None].astype(jnp.bfloat16), "batch", scatter_dimension=1, tiled=True
-        ).astype(jnp.float32),
-        lax.psum_scatter(
-            gain_one_grad[None].astype(jnp.bfloat16), "batch", scatter_dimension=1, tiled=True
-        ).astype(jnp.float32),
-        lax.psum_scatter(
-            up_two_grad[None].astype(jnp.bfloat16), "batch", scatter_dimension=2, tiled=True
-        ).astype(jnp.float32),
-        lax.psum_scatter(
-            down_two_grad[None].astype(jnp.bfloat16), "batch", scatter_dimension=1, tiled=True
-        ).astype(jnp.float32),
-        lax.psum_scatter(
-            gain_two_grad[None].astype(jnp.bfloat16), "batch", scatter_dimension=1, tiled=True
-        ).astype(jnp.float32),
+        up_one_grad[None],
+        down_one_grad[None],
+        gains[0:1],
+        up_two_grad[None],
+        down_two_grad[None],
+        gains[1:2],
     )
     return (
         block_out,
@@ -348,7 +399,7 @@
         dense[2],
         dense[3],
         small[0],
-        small[1],
+        small[1:],
         expert_parts[0],
         expert_parts[1],
         expert_parts[2],

time: 1440 us -> 546 us (0.38)
  waiting for transfers between devices: 1010 us -> 182 us
  matrix products: 220 us -> 173 us
  starting transfers between devices: 22.9 us -> 43.4 us
  blocking collectives: 63 us -> 42.8 us
  other arithmetic: 55.1 us -> 37.6 us
    reduce_scatter x8 -> x0, waiting for transfers between devices: 983 us -> none  [the longest x1 143 us: per_device(): lax.psum_scatter(down_two_grad[None].astype(jnp.bfloat16), 'batch', scatt...]
    ppermute x0 -> x22, waiting for transfers between devices: none -> 147 us  [the longest x12 81.3 us: ring_rows(): held.append(lax.ppermute(held[-1], axis, back))]
    psum x1 -> x0, blocking collectives: 45.3 us -> none  [per_device(): small = lax.psum((grad_gain_att, grad_centroids), ('batch', 'expert'))]
    dot_general x4 -> x2, matrix products: 46.4 us -> 13.8 us  [sublayer_forward(): jnp.dot(middle, down_proj, preferred_element_type=jnp.float32)]
    ppermute x0 -> x22, starting transfers between devices: none -> 30.4 us  [the longest x12 27.1 us: ring_rows(): held.append(lax.ppermute(held[-1], axis, back))]
    all_gather x0 -> x1, blocking collectives: none -> 24.9 us  [per_device(): gains = lax.all_gather(jnp.stack((gain_one_grad, gain_two_grad)), 'batch')]
    dot_general x2, matrix products: 12.7 us -> 31 us  [sublayer_backward(): jnp.einsum('rf,df->rd', grad_pre, up_proj, preferred_element_type=jnp.flo...]
  transfers between devices with their start and end apart: 15 -> 25, of which waited for: 11 -> 17; matrix products, arithmetic and copies ran while one was open for 13% -> 14% of each run, Pallas kernels for 0% -> 0%
where the time goes in v1:
time: 546 us; the launch traced here: 539 us
  waiting for transfers between devices  182 us (33%)
  matrix products  173 us (32%)
  local copies, waits for them, and re-layouts  58.2 us (11%)
  starting transfers between devices  43.4 us (8%)
  blocking collectives  42.8 us (8%)
  other arithmetic  37.6 us (7%)
    ppermute x12, waiting for transfers between devices, ring_rows(): held.append(lax.ppermute(held[-1], axis, back))  81.3 us
    ppermute x5, waiting for transfers between devices, all_sum(): lax.ppermute(value, axis, [(i, i ^ bit) for i in range(count)])  45.6 us
    dot_general x2, matrix products, sublayer_backward(): jnp.einsum('rf,df->rd', grad_pre, up_proj, preferred_element_type=jnp.flo...  31 us
    dot_general x2, matrix products, weight_grads(): jnp.einsum('rd,rf->df', normed_rows, grad_pre, preferred_element_type=jnp...  30.6 us
    ppermute x12, starting transfers between devices, ring_rows(): held.append(lax.ppermute(held[-1], axis, back))  27.1 us
    all_gather x1, blocking collectives, per_device(): gains = lax.all_gather(jnp.stack((gain_one_grad, gain_two_grad)), 'batch')  24.9 us
    ppermute x5, waiting for transfers between devices, halve(): got = lax.ppermute(sent, axis, [(i, i ^ bit) for i in range(count)])  20.1 us
    all_to_all x1, blocking collectives, forward_pass(): lax.all_to_all(outgoing.reshape(expert_count, capacity, width_all), 'expe...  17.9 us
  transfers between devices with their start and end apart: 25, of which 17 were waited for; matrix products, arithmetic and copies ran while one was open for 14% of the time, Pallas kernels for 0%

profile of v1, /device:TPU:0, one launch (start us, length us, event | category | flops | bytes accessed | tf_op | source)
XLA Modules:
  0.0 538.8 jit_solution(13143295100545646052)
XLA Ops:
  6.4 2.6 convolution_convert_fusion.3
  10.3 3.3 convolution_convert_fusion.2
  15.6 3.2 convolution_convert_fusion.1
  26.3 2.6 scatter_custom_fusion
  30.9 17.9 %all_to_all.20 = bf16[8,44,1024]{2,1,0:T(8,128)(2,1)S(1)} all-to-all(bf16[8,44,1024]{2,1,0:T(8,128)(2,1)} %reshape.361), channel_id=1, replica_groups=mesh['batch'=4,'expert'=8] {'expert'}, dimensions={0} | all-to-all | bytes 1441792 | tf_op jit(solution)/shard_map/all_to_all | solution.py:223
  52.9 9.3 %fusion.16 = f32[352,4096]{1,0:T(8,128)} fusion(bf16[352,1024]{1,0:T(8,128)(2,1)} %convert_element_type.255, bf16[1,1024,4096]{2,1,0:T(8,128)(2,1)} %param.25), kind=kOutput, calls=%fused_computation.22 | convolution fusion | flops 2952790016 | bytes 14876672 | tf_op jit(solution)/shard_map/dot_general | solution.py:87
  62.2 2.3 reshape.374
  64.4 9.1 %fusion.270 = (f32[352]{0:T(512)S(1)}, f32[352,1024]{1,0:T(8,128)S(1)}) fusion(f32[352,1024]{1,0:T(8,128)} %reshape.374, bf16[1,4096,1024]{2,1,0:T(8,128)(2,1)} %param.26, f32[352,4096]{1,0:T(8,128)} %fusion.16), kind=kOutput, calls=%fused_computation.329 | convolution fusion | flops 2966486784 | bytes 17040768 | tf_op jit(solution)/shard_map/dot_general | solution.py:89
  75.1 6.1 %fusion.8 = f32[352,4096]{1,0:T(8,128)S(1)} fusion(bf16[352,1024]{1,0:T(8,128)(2,1)S(1)} %multiply_convert_fusion.15, bf16[1,1024,4096]{2,1,0:T(8,128)(2,1)} %param.28), kind=kOutput, calls=%fused_computation.14 | convolution fusion | flops 2952790016 | bytes 14876672 | tf_op jit(solution)/shard_map/dot_general | solution.py:87
  81.2 2.5 copy-done.48
  83.7 4.7 add_convert_fusion.1
  90.4 4.6 all-to-all-start.1
  97.3 10.4 %all-to-all-done.1 = bf16[8,44,1024]{2,1,0:T(8,128)(2,1)} async-done(((bf16[8,44,1024]{2,1,0:T(8,128)(2,1)}), bf16[8,44,1024]{2,1,0:T(8,128)(2,1)}, u32[]{:S(2)}, u32[]{:S(2)}) %all-to-all-start.1) | async-done | bytes 720928 | tf_op jit(solution)/shard_map/all_to_all | solution.py:236
  109.7 3.6 gather_fusion
  114.8 3.2 scatter_custom_fusion.1
  120.0 4.2 all-to-all-start.2
  124.4 12.4 %all-to-all-done.2 = bf16[8,44,1024]{2,1,0:T(8,128)(2,1)} async-done(((bf16[8,44,1024]{2,1,0:T(8,128)(2,1)}), bf16[8,44,1024]{2,1,0:T(8,128)(2,1)}, u32[]{:S(2)}, u32[]{:S(2)}) %all-to-all-start.2) | async-done | bytes 720928 | tf_op jit(solution)/shard_map/all_to_all | solution.py:321
  136.9 2.0 reshape.365
  138.9 15.3 %multiply_reduce_fusion.2 = (f32[1024]{0:T(1024)S(1)}, f32[352]{0:T(512)S(1)}, f32[352,1024]{1,0:T(8,128)}) fusion(f32[352,1024]{1,0:T(8,128)} %copy-done.13, f32[352]{0:T(512)S(1)} %fusion.208, f32[352]{0:T(512)S(1)} %broadcast_multiply_fusion.1, f32[1024]{0:T(1024)S(1)} %bitcast.230, bf16[1,1024,4096]{2,1,0:T(8,128)(2,1)} %param.28, ...), kind=kOutput, calls=%fused_computation.155 | convolution fusion | flops 5936937472 | bytes 26161280 | tf_op jit(solution)/shard_map/rf,df->rd/dot_general | solution.py:99
  154.3 2.4 fusion.267
  158.8 15.6 %multiply_reduce_fusion.3 = (f32[1024]{0:T(1024)S(1)}, f32[352]{0:T(512)S(1)}, bf16[352,1024]{1,0:T(8,128)(2,1)}, f32[352,1024]{1,0:T(8,128)}) fusion(f32[352,1024]{1,0:T(8,128)} %reshape.374, f32[352]{0:T(512)S(1)} %div.124, f32[352]{0:T(512)S(1)} %rsqrt.39, f32[1024]{0:T(1024)S(1)} %bitcast.233, bf16[1,1024,4096]{2,1,0:T(8,128)(2,1)} %param.25, ...), kind=kOutput, calls=%fused_computation.156 | convolution fusion | flops 5937658368 | bytes 26882176 | tf_op jit(solution)/shard_map/rf,df->rd/dot_general | solution.py:99
  174.5 2.5 fusion.266
  180.2 4.2 all-to-all-start.3
  184.5 12.6 %all-to-all-done.3 = bf16[8,44,1024]{2,1,0:T(8,128)(2,1)} async-done(((bf16[8,44,1024]{2,1,0:T(8,128)(2,1)}), bf16[8,44,1024]{2,1,0:T(8,128)(2,1)}, u32[]{:S(2)}, u32[]{:S(2)}) %all-to-all-start.3) | async-done | bytes 720928 | tf_op jit(solution)/shard_map/all_to_all | solution.py:335
  197.1 2.2 reshape.367
  199.3 3.6 gather_fusion.1
  202.8 2.4 fusion.152
  206.2 3.2 convolution_convert_fusion
  211.4 4.0 fusion.275
  215.3 8.5 %fusion.157 = bf16[16,64,256]{2,1,0:T(8,128)(2,1)} fusion(bf16[256,16,64]{0,2,1:T(8,128)(2,1)} %bitcast.221, f32[16,256,256]{1,2,0:T(8,128)} %fusion.275, f32[16,256,256]{1,2,0:T(8,128)} %copy-done.2, f32[16,256]{1,0:T(8,128)S(1)} %log_add_fusion), kind=kOutput, calls=%fused_computation.178 | convolution fusion | flops 141824256 | bytes 9453568 | tf_op jit(solution)/shard_map/while/body/eval_jaxpr/hqk,khd->qhd/dot_general | solution.py:64
  223.9 8.6 %fusion.160 = bf16[16,64,256]{2,1,0:T(8,128)(2,1)} fusion(bf16[256,16,64]{0,2,1:T(8,128)(2,1)} %bitcast.219, f32[16,256,256]{1,2,0:T(8,128)} %fusion.275, f32[16,256,256]{1,2,0:T(8,128)} %copy-done.2, f32[16,256]{1,0:T(8,128)S(1)} %log_add_fusion), kind=kOutput, calls=%fused_computation.179 | convolution fusion | flops 141824256 | bytes 9453568 | tf_op jit(solution)/shard_map/while/body/eval_jaxpr/hqk,qhd->khd/dot_general | solution.py:67
  232.5 3.3 fusion.153
  240.5 2.0 convert_bitcast_fusion
  247.6 2.5 dynamic-slice_bitcast_fusion
  250.1 2.5 copy-done.3
  252.6 3.6 collective-permute-start.16
  256.2 16.1 %collective-permute-done.16 = bf16[352,1024]{1,0:T(8,128)(2,1)S(1)} collective-permute-done((bf16[352,1024]{1,0:T(8,128)(2,1)S(1)}, bf16[352,1024]{1,0:T(8,128)(2,1)S(1)}, u32[]{:S(2)}, u32[]{:S(2)}) %collective-permute-start.16) | collective-permute-done | bytes 720928 | tf_op jit(solution)/shard_map/ppermute | solution.py:110
  272.2 4.3 collective-permute-start.17
  279.2 3.8 collective-permute-done.6
  283.0 25.5 %collective-permute-done.10 = bf16[352,1024]{1,0:T(8,128)(2,1)} collective-permute-done((bf16[352,1024]{1,0:T(8,128)(2,1)S(1)}, bf16[352,1024]{1,0:T(8,128)(2,1)}, u32[]{:S(2)}, u32[]{:S(2)}) %collective-permute-start.10) | collective-permute-done | bytes 720928 | tf_op jit(solution)/shard_map/ppermute | solution.py:110
  309.1 3.7 collective-permute-done.7
  312.8 4.4 collective-permute-start.11
  318.1 36.9 %collective-permute-done.8 = f32[9,1024]{1,0:T(8,128)S(1)} collective-permute-done((f32[9,1024]{1,0:T(8,128)S(1)}, f32[9,1024]{1,0:T(8,128)S(1)}, u32[]{:S(2)}, u32[]{:S(2)}) %collective-permute-start.8) | collective-permute-done | bytes 36896 | tf_op jit(solution)/shard_map/ppermute | solution.py:159
  355.0 4.3 collective-permute-start.18
  361.4 24.9 %all-gather.1 = f32[4,2,1024]{2,1,0:T(2,128)S(1)} all-gather(f32[1,2,1024]{2,1,0:T(2,128)S(1)} %maximum_bitcast_fusion), channel_id=2, replica_groups=mesh['batch'=4,'expert'=8] {'batch'}, dimensions={0}, use_global_device_ids=true | all-gather | bytes 40960 | tf_op jit(solution)/shard_map/all_gather | solution.py:381
  389.9 2.1 constant_dynamic-update-slice_fusion.2
  393.2 8.0 %fusion.113 = f32[1408,1024]{1,0:T(8,128)} fusion(bf16[1,1024,4096]{2,1,0:T(8,128)(2,1)} %param.28, s32[]{:T(128)S(6)} %select_n.116, bf16[352,1024]{1,0:T(8,128)(2,1)} %collective-permute-done.18, bf16[352,1024]{1,0:T(8,128)(2,1)} %copy-done.43, bf16[352,1024]{1,0:T(8,128)(2,1)} %copy-done.42, bf16[352,1024]{1,0:T(8,128)(2,1)S(1)} %copy-done.33), kind=kOutput, calls=%fused_computation.122 | convolution fusion | flops 2964324352 | bytes 10747908 | tf_op jit(solution)/shard_map/dot_general | solution.py:120
  401.3 4.4 collective-permute-done.14
  405.7 3.6 collective-permute-start.15
  409.2 11.9 %collective-permute-done.20 = bf16[352,1024]{1,0:T(8,128)(2,1)S(1)} collective-permute-done((bf16[352,1024]{1,0:T(8,128)(2,1)}, bf16[352,1024]{1,0:T(8,128)(2,1)S(1)}, u32[]{:S(2)}, u32[]{:S(2)}) %collective-permute-start.20) | collective-permute-done | bytes 720928 | tf_op jit(solution)/shard_map/ppermute | solution.py:110
  421.1 4.0 collective-permute-start.21
  426.0 10.5 %collective-permute-done.12 = bf16[352,1024]{1,0:T(8,128)(2,1)S(1)} collective-permute-done((bf16[352,1024]{1,0:T(8,128)(2,1)}, bf16[352,1024]{1,0:T(8,128)(2,1)S(1)}, u32[]{:S(2)}, u32[]{:S(2)}) %collective-permute-start.12) | collective-permute-done | bytes 720928 | tf_op jit(solution)/shard_map/ppermute | solution.py:110
  436.6 7.9 %fusion.121 = f32[1408,1024]{1,0:T(8,128)} fusion(bf16[1,1024,4096]{2,1,0:T(8,128)(2,1)} %param.25, s32[]{:T(128)S(6)} %select_n.116, bf16[352,1024]{1,0:T(8,128)(2,1)S(1)} %collective-permute-done.12, bf16[352,1024]{1,0:T(8,128)(2,1)} %collective-permute-done.11, bf16[352,1024]{1,0:T(8,128)(2,1)} %collective-permute-done.10, ...), kind=kOutput, calls=%fused_computation.126 | convolution fusion | flops 2964324352 | bytes 10747908 | tf_op jit(solution)/shard_map/dot_general | solution.py:120
  444.5 4.3 fusion.1
  451.5 12.8 %collective-permute-done.21 = bf16[352,1024]{1,0:T(8,128)(2,1)S(1)} collective-permute-done((bf16[352,1024]{1,0:T(8,128)(2,1)S(1)}, bf16[352,1024]{1,0:T(8,128)(2,1)S(1)}, u32[]{:S(2)}, u32[]{:S(2)}) %collective-permute-start.21) | collective-permute-done | bytes 720928 | tf_op jit(solution)/shard_map/ppermute | solution.py:110
  465.2 15.2 %fusion.102 = f32[1,1024,1024]{2,1,0:T(8,128)} fusion(f32[1408,1024]{1,0:T(8,128)} %fusion.121, bf16[1,4096,1024]{2,1,0:T(8,128)(2,1)} %param.26, s32[]{:T(128)S(6)} %select_n.116, bf16[352,1024]{1,0:T(8,128)(2,1)} %collective-permute-done.15, bf16[352,1024]{1,0:T(8,128)(2,1)S(1)} %collective-permute-done.14, ...), kind=kOutput, calls=%fused_computation.115 | convolution fusion | flops 5957484544 | bytes 17825796 | tf_op jit(solution)/shard_map/rd,rf->df/dot_general | solution.py:127
  480.4 12.1 %collective-permute-done.1 = bf16[4,2,2,2,32,1024]{5,4,3,2,1,0:T(8,128)(2,1)} collective-permute-done((bf16[4,2,2,2,32,1024]{5,4,3,2,1,0:T(8,128)(2,1)S(1)}, bf16[4,2,2,2,32,1024]{5,4,3,2,1,0:T(8,128)(2,1)}, u32[]{:S(2)}, u32[]{:S(2)}) %collective-permute-start.1) | collective-permute-done | bytes 2097184 | tf_op jit(solution)/shard_map/ppermute | solution.py:136
  492.5 3.3 fusion.46
  496.6 15.4 %fusion.105 = f32[1,1024,1024]{2,1,0:T(8,128)} fusion(f32[1408,1024]{1,0:T(8,128)} %fusion.113, bf16[1408,1024]{1,0:T(8,128)(2,1)} %constant_dynamic-update-slice_fusion, bf16[1,4096,1024]{2,1,0:T(8,128)(2,1)} %param.29, s32[]{:T(128)S(6)} %select_n.116, bf16[352,1024]{1,0:T(8,128)(2,1)} %collective-permute-done.18, bf16[352,1024]{1,0:T(8,128)(2,1)} %copy-done.43, ...), kind=kOutput, calls=%fused_computation.116 | convolution fusion | flops 5945950208 | bytes 17825796 | tf_op jit(solution)/shard_map/rd,rf->df/dot_general | solution.py:127
  512.0 2.1 collective-permute-done.2
  515.9 9.6 %fusion.109 = f32[1,1024,1024]{2,1,0:T(8,128)} fusion(f32[1408,1024]{1,0:T(8,128)} %fusion.121, bf16[352,1024]{1,0:T(8,128)(2,1)} %collective-permute-done.15, bf16[352,1024]{1,0:T(8,128)(2,1)S(1)} %copy-done.45, bf16[352,1024]{1,0:T(8,128)(2,1)} %collective-permute-done.13, bf16[352,1024]{1,0:T(8,128)(2,1)} %fusion.178), kind=kOutput, calls=%fused_computation.118 | convolution fusion | flops 2977300480 | bytes 12845056 | tf_op jit(solution)/shard_map/rf,rd->fd/dot_general | solution.py:124
  525.4 2.4 collective-permute-done.3
  528.9 5.3 fusion.108
  534.2 3.5 collective-permute-done.4
  (226 shorter events, 71.9 us)
Async XLA Ops:
  0.6 5.7 %copy-start = (bf16[1024,1024]{1,0:T(8,128)(2,1)S(1)}, bf16[1024,1024]{1,0:T(8,128)(2,1)}, u32[]{:S(2)}) copy-start(bf16[1024,1024]{1,0:T(8,128)(2,1)} %param.21) | copy-start | bytes 6291460
  0.7 9.6 %copy-start.5 = (bf16[256,1024]{1,0:T(8,128)(2,1)S(1)}, bf16[256,1024]{1,0:T(8,128)(2,1)}, u32[]{:S(2)}) copy-start(bf16[256,1024]{1,0:T(8,128)(2,1)} %param.16) | copy-start | bytes 1572868
  0.7 9.5 %copy-start.37 = (f32[1024]{0:T(1024)S(1)}, f32[1024]{0:T(1024)}, u32[]{:S(2)}) copy-start(f32[1024]{0:T(1024)} %param.23) | copy-start | bytes 12292
  10.2 12.5 %copy-start.23 = (bf16[256,1024]{0,1:T(8,128)(2,1)}, bf16[256,1024]{0,1:T(8,128)(2,1)S(1)}, u32[]{:S(2)}) copy-start(bf16[256,1024]{0,1:T(8,128)(2,1)S(1)} %copy.72) | copy-start | bytes 1572868
  10.2 9.8 %copy-start.47 = (s32[1,4]{1,0:T(1,128)S(1)}, s32[1,4]{1,0:T(1,128)}, u32[]{:S(2)}) copy-start(s32[1,4]{1,0:T(1,128)} %param.17) | copy-start | bytes 52
  20.0 2.7 copy-start.31
  22.8 2.8 copy-start.17
  26.3 23.4 %copy-start.39 = (f32[1,1024]{1,0:T(1,128)S(1)}, f32[1,1024]{1,0:T(1,128)}, u32[]{:S(2)}) copy-start(f32[1,1024]{1,0:T(1,128)} %param.27) | copy-start | bytes 12292
  64.4 9.5 %copy-start.38 = (f32[1,1024]{1,0:T(1,128)S(1)}, f32[1,1024]{1,0:T(1,128)}, u32[]{:S(2)}) copy-start(f32[1,1024]{1,0:T(1,128)} %param.30) | copy-start | bytes 12292
  73.6 7.6 %copy-start.13 = (f32[352,1024]{1,0:T(8,128)}, f32[352,1024]{1,0:T(8,128)S(1)}, u32[]{:S(2)}) copy-start(f32[352,1024]{1,0:T(8,128)S(1)} %get-tuple-element.97) | copy-start | bytes 4325380
  73.9 9.8 %slice-start.2 = ((s8[8388608]{0:T(1024)(128)(4,1)}), s8[4194304]{0:T(1024)(128)(4,1)S(1)}, s32[]{:S(2)}) async-start(s8[8388608]{0:T(1024)(128)(4,1)} %bitcast.242), calls=%async_computation.6 | async-start | bytes 8388608
  75.1 8.7 %slice-start.3 = ((s8[8388608]{0:T(1024)(128)(4,1)}), s8[4194304]{0:T(1024)(128)(4,1)S(1)}, s32[]{:S(2)}) async-start(s8[8388608]{0:T(1024)(128)(4,1)} %bitcast.242), calls=%async_computation.7 | async-start | bytes 8388608
  81.2 2.5 copy-start.48
  83.7 12.6 %copy-start.35 = (f32[8,1024]{1,0:T(8,128)S(1)}, f32[8,1024]{1,0:T(8,128)}, u32[]{:S(2)}) copy-start(f32[8,1024]{1,0:T(8,128)} %param.24) | copy-start | bytes 98308
  83.7 12.6 %copy-start.36 = (s32[256,1]{0,1:T(1,128)S(1)}, s32[256,1]{0,1:T(1,128)}, u32[]{:S(2)}) copy-start(s32[256,1]{0,1:T(1,128)} %param.18) | copy-start | bytes 3076
  90.4 17.2 %all-to-all-start.1 = ((bf16[8,44,1024]{2,1,0:T(8,128)(2,1)}), bf16[8,44,1024]{2,1,0:T(8,128)(2,1)}, u32[]{:S(2)}, u32[]{:S(2)}) async-start(bf16[8,44,1024]{2,1,0:T(8,128)(2,1)} %reshape.362), calls=%async_computation.1 | async-start | bytes 1572864 | tf_op jit(solution)/shard_map/all_to_all | solution.py:236
  120.0 16.8 %all-to-all-start.2 = ((bf16[8,44,1024]{2,1,0:T(8,128)(2,1)}), bf16[8,44,1024]{2,1,0:T(8,128)(2,1)}, u32[]{:S(2)}, u32[]{:S(2)}) async-start(bf16[8,44,1024]{2,1,0:T(8,128)(2,1)} %reshape.364), calls=%async_computation.2 | async-start | bytes 1572864 | tf_op jit(solution)/shard_map/all_to_all | solution.py:321
  154.2 3.5 copy-start.14
  180.2 16.8 %all-to-all-start.3 = ((bf16[8,44,1024]{2,1,0:T(8,128)(2,1)}), bf16[8,44,1024]{2,1,0:T(8,128)(2,1)}, u32[]{:S(2)}, u32[]{:S(2)}) async-start(bf16[8,44,1024]{2,1,0:T(8,128)(2,1)} %reshape.366), calls=%async_computation.3 | async-start | bytes 1572864 | tf_op jit(solution)/shard_map/all_to_all | solution.py:335
  232.5 3.3 copy-start.22
  232.5 3.3 copy-start.25
  232.5 4.1 copy-start.24
  232.5 4.1 copy-start.27
  238.9 5.0 copy-start.21
  240.5 4.4 copy-start.28
  242.6 3.1 copy-start.26
  247.5 5.0 copy-start.3
  247.6 5.0 copy-start.33
  247.6 29.0 %copy-start.40 = (bf16[352,1024]{1,0:T(8,128)(2,1)S(1)}, bf16[352,1024]{1,0:T(8,128)(2,1)}, u32[]{:S(2)}) copy-start(bf16[352,1024]{1,0:T(8,128)(2,1)} %get-tuple-element.83) | copy-start | bytes 2162692
  247.6 35.4 %copy-start.16 = (bf16[352,1024]{1,0:T(8,128)(2,1)S(1)}, bf16[352,1024]{1,0:T(8,128)(2,1)}, u32[]{:S(2)}) copy-start(bf16[352,1024]{1,0:T(8,128)(2,1)} %reshape.365) | copy-start | bytes 2162692
  247.6 111.7 %copy-start.19 = (bf16[256,1024]{1,0:T(8,128)(2,1)S(1)}, bf16[256,1024]{1,0:T(8,128)(2,1)}, u32[]{:S(2)}) copy-start(bf16[256,1024]{1,0:T(8,128)(2,1)} %gather_fusion) | copy-start | bytes 1572868
  252.6 191.9 %collective-permute-start = (bf16[4,2,2,2,2,32,1024]{6,5,4,3,2,1,0:T(8,128)(2,1)}, bf16[4,2,2,2,2,32,1024]{6,5,4,3,2,1,0:T(8,128)(2,1)}, u32[]{:S(2)}, u32[]{:S(2)}) collective-permute-start(bf16[4,2,2,2,2,32,1024]{6,5,4,3,2,1,0:T(8,128)(2,1)} %dynamic-slice_bitcast_fusion), channel_id=1, source_target_pairs={{0,1},{1,0},{2,3},{3,2},{4,5},{5,4},{6,7},{7,6},{8,9},{9,8},{10,11... | collective-permute-start | bytes 12582920 | tf_op jit(solution)/shard_map/ppermute | solution.py:136
  252.6 19.7 %collective-permute-start.16 = (bf16[352,1024]{1,0:T(8,128)(2,1)S(1)}, bf16[352,1024]{1,0:T(8,128)(2,1)S(1)}, u32[]{:S(2)}, u32[]{:S(2)}) collective-permute-start(bf16[352,1024]{1,0:T(8,128)(2,1)S(1)} %copy-done.33), channel_id=1, source_target_pairs={{0,24},{8,0},{16,8},{24,16},{1,25},{9,1},{17,9},{25,17},{2,26},{10... | collective-permute-start | bytes 2162696 | tf_op jit(solution)/shard_map/ppermute | solution.py:110
  272.2 45.0 %copy-start.42 = (bf16[352,1024]{1,0:T(8,128)(2,1)}, bf16[352,1024]{1,0:T(8,128)(2,1)S(1)}, u32[]{:S(2)}) copy-start(bf16[352,1024]{1,0:T(8,128)(2,1)S(1)} %collective-permute-done.16) | copy-start | bytes 2162692
  272.2 45.0 %collective-permute-start.17 = (bf16[352,1024]{1,0:T(8,128)(2,1)S(1)}, bf16[352,1024]{1,0:T(8,128)(2,1)S(1)}, u32[]{:S(2)}, u32[]{:S(2)}) collective-permute-start(bf16[352,1024]{1,0:T(8,128)(2,1)S(1)} %collective-permute-done.16), channel_id=1, source_target_pairs={{0,24},{8,0},{16,8},{24,16},{1,25},{9,1},{17,9},{25,17},{2,26},{10... | collective-permute-start | bytes 2162696 | tf_op jit(solution)/shard_map/ppermute | solution.py:110
  276.5 32.0 %collective-permute-start.10 = (bf16[352,1024]{1,0:T(8,128)(2,1)S(1)}, bf16[352,1024]{1,0:T(8,128)(2,1)}, u32[]{:S(2)}, u32[]{:S(2)}) collective-permute-start(bf16[352,1024]{1,0:T(8,128)(2,1)S(1)} %copy-done.40), channel_id=1, source_target_pairs={{0,24},{8,0},{16,8},{24,16},{1,25},{9,1},{17,9},{25,17},{2,26},{10... | collective-permute-start | bytes 2162696 | tf_op jit(solution)/shard_map/ppermute | solution.py:110
  277.3 1.3 collective-permute-start.5
  277.4 83.9 %collective-permute-start.13 = (bf16[352,1024]{1,0:T(8,128)(2,1)}, bf16[352,1024]{1,0:T(8,128)(2,1)}, u32[]{:S(2)}, u32[]{:S(2)}) collective-permute-start(bf16[352,1024]{1,0:T(8,128)(2,1)} %fusion.178), channel_id=1, source_target_pairs={{0,24},{8,0},{16,8},{24,16},{1,25},{9,1},{17,9},{25,17},{2,26},{10... | collective-permute-start | bytes 2162696 | tf_op jit(solution)/shard_map/ppermute | solution.py:110
  278.6 4.3 collective-permute-start.6
  283.0 103.3 %collective-permute-start.19 = (bf16[352,1024]{1,0:T(8,128)(2,1)S(1)}, bf16[352,1024]{1,0:T(8,128)(2,1)}, u32[]{:S(2)}, u32[]{:S(2)}) collective-permute-start(bf16[352,1024]{1,0:T(8,128)(2,1)S(1)} %copy-done.16), channel_id=1, source_target_pairs={{0,24},{8,0},{16,8},{24,16},{1,25},{9,1},{17,9},{25,17},{2,26},{10... | collective-permute-start | bytes 2162696 | tf_op jit(solution)/shard_map/ppermute | solution.py:110
  308.5 4.3 collective-permute-start.7
  312.8 76.2 %collective-permute-start.11 = (bf16[352,1024]{1,0:T(8,128)(2,1)}, bf16[352,1024]{1,0:T(8,128)(2,1)}, u32[]{:S(2)}, u32[]{:S(2)}) collective-permute-start(bf16[352,1024]{1,0:T(8,128)(2,1)} %collective-permute-done.10), channel_id=1, source_target_pairs={{0,24},{8,0},{16,8},{24,16},{1,25},{9,1},{17,9},{25,17},{2,26},{10... | collective-permute-start | bytes 2162696 | tf_op jit(solution)/shard_map/ppermute | solution.py:110
  318.1 36.9 %collective-permute-start.8 = (f32[9,1024]{1,0:T(8,128)S(1)}, f32[9,1024]{1,0:T(8,128)S(1)}, u32[]{:S(2)}, u32[]{:S(2)}) collective-permute-start(f32[9,1024]{1,0:T(8,128)S(1)} %add.303), channel_id=1, source_target_pairs={{0,8},{8,0},{16,24},{24,16},{1,9},{9,1},{17,25},{25,17},{2,10},{10... | collective-permute-start | bytes 110600 | tf_op jit(solution)/shard_map/ppermute | solution.py:159
  355.0 38.2 %collective-permute-start.18 = (bf16[352,1024]{1,0:T(8,128)(2,1)}, bf16[352,1024]{1,0:T(8,128)(2,1)}, u32[]{:S(2)}, u32[]{:S(2)}) collective-permute-start(bf16[352,1024]{1,0:T(8,128)(2,1)} %copy-done.43), channel_id=1, source_target_pairs={{0,24},{8,0},{16,8},{24,16},{1,25},{9,1},{17,9},{25,17},{2,26},{10... | collective-permute-start | bytes 2162696 | tf_op jit(solution)/shard_map/ppermute | solution.py:110
  361.3 26.9 %collective-permute-start.9 = (f32[9,1024]{1,0:T(8,128)S(1)}, f32[9,1024]{1,0:T(8,128)S(1)}, u32[]{:S(2)}, u32[]{:S(2)}) collective-permute-start(f32[9,1024]{1,0:T(8,128)S(1)} %add.304), channel_id=1, source_target_pairs={{0,16},{8,24},{16,0},{24,8},{1,17},{9,25},{17,1},{25,9},{2,18},{10... | collective-permute-start | bytes 110600 | tf_op jit(solution)/shard_map/ppermute | solution.py:159
  386.3 19.3 %collective-permute-start.14 = (bf16[352,1024]{1,0:T(8,128)(2,1)}, bf16[352,1024]{1,0:T(8,128)(2,1)S(1)}, u32[]{:S(2)}, u32[]{:S(2)}) collective-permute-start(bf16[352,1024]{1,0:T(8,128)(2,1)} %collective-permute-done.13), channel_id=1, source_target_pairs={{0,24},{8,0},{16,8},{24,16},{1,25},{9,1},{17,9},{25,17},{2,26},{10... | collective-permute-start | bytes 2162696 | tf_op jit(solution)/shard_map/ppermute | solution.py:110
  388.2 33.0 %collective-permute-start.20 = (bf16[352,1024]{1,0:T(8,128)(2,1)}, bf16[352,1024]{1,0:T(8,128)(2,1)S(1)}, u32[]{:S(2)}, u32[]{:S(2)}) collective-permute-start(bf16[352,1024]{1,0:T(8,128)(2,1)} %collective-permute-done.19), channel_id=1, source_target_pairs={{0,24},{8,0},{16,8},{24,16},{1,25},{9,1},{17,9},{25,17},{2,26},{10... | collective-permute-start | bytes 2162696 | tf_op jit(solution)/shard_map/ppermute | solution.py:110
  389.0 47.6 %collective-permute-start.12 = (bf16[352,1024]{1,0:T(8,128)(2,1)}, bf16[352,1024]{1,0:T(8,128)(2,1)S(1)}, u32[]{:S(2)}, u32[]{:S(2)}) collective-permute-start(bf16[352,1024]{1,0:T(8,128)(2,1)} %collective-permute-done.11), channel_id=1, source_target_pairs={{0,24},{8,0},{16,8},{24,16},{1,25},{9,1},{17,9},{25,17},{2,26},{10... | collective-permute-start | bytes 2162696 | tf_op jit(solution)/shard_map/ppermute | solution.py:110
  393.2 43.3 %copy-start.41 = (bf16[352,1024]{1,0:T(8,128)(2,1)S(1)}, bf16[352,1024]{1,0:T(8,128)(2,1)}, u32[]{:S(2)}) copy-start(bf16[352,1024]{1,0:T(8,128)(2,1)} %get-tuple-element.83) | copy-start | bytes 2162692
  405.7 59.6 %copy-start.44 = (bf16[352,1024]{1,0:T(8,128)(2,1)}, bf16[352,1024]{1,0:T(8,128)(2,1)S(1)}, u32[]{:S(2)}) copy-start(bf16[352,1024]{1,0:T(8,128)(2,1)S(1)} %collective-permute-done.14) | copy-start | bytes 2162692
  405.7 59.5 %collective-permute-start.15 = (bf16[352,1024]{1,0:T(8,128)(2,1)S(1)}, bf16[352,1024]{1,0:T(8,128)(2,1)}, u32[]{:S(2)}, u32[]{:S(2)}) collective-permute-start(bf16[352,1024]{1,0:T(8,128)(2,1)S(1)} %collective-permute-done.14), channel_id=1, source_target_pairs={{0,24},{8,0},{16,8},{24,16},{1,25},{9,1},{17,9},{25,17},{2,26},{10... | collective-permute-start | bytes 2162696 | tf_op jit(solution)/shard_map/ppermute | solution.py:110
  421.1 43.2 %collective-permute-start.21 = (bf16[352,1024]{1,0:T(8,128)(2,1)S(1)}, bf16[352,1024]{1,0:T(8,128)(2,1)S(1)}, u32[]{:S(2)}, u32[]{:S(2)}) collective-permute-start(bf16[352,1024]{1,0:T(8,128)(2,1)S(1)} %collective-permute-done.20), channel_id=1, source_target_pairs={{0,24},{8,0},{16,8},{24,16},{1,25},{9,1},{17,9},{25,17},{2,26},{10... | collective-permute-start | bytes 2162696 | tf_op jit(solution)/shard_map/ppermute | solution.py:110
  425.1 19.4 %slice-start = ((s8[8388608]{0:T(1024)(128)(4,1)}), s8[4194304]{0:T(1024)(128)(4,1)S(1)}, s32[]{:S(2)}) async-start(s8[8388608]{0:T(1024)(128)(4,1)} %bitcast.201), calls=%async_computation.4 | async-start | bytes 8388608
  426.0 18.4 %slice-start.1 = ((s8[8388608]{0:T(1024)(128)(4,1)}), s8[4194304]{0:T(1024)(128)(4,1)S(1)}, s32[]{:S(2)}) async-start(s8[8388608]{0:T(1024)(128)(4,1)} %bitcast.201), calls=%async_computation.5 | async-start | bytes 8388608
  436.6 7.9 %copy-start.46 = (bf16[352,1024]{1,0:T(8,128)(2,1)}, bf16[352,1024]{1,0:T(8,128)(2,1)S(1)}, u32[]{:S(2)}) copy-start(bf16[352,1024]{1,0:T(8,128)(2,1)S(1)} %collective-permute-done.12) | copy-start | bytes 2162692
  451.0 41.5 %collective-permute-start.1 = (bf16[4,2,2,2,32,1024]{5,4,3,2,1,0:T(8,128)(2,1)S(1)}, bf16[4,2,2,2,32,1024]{5,4,3,2,1,0:T(8,128)(2,1)}, u32[]{:S(2)}, u32[]{:S(2)}) collective-permute-start(bf16[4,2,2,2,32,1024]{5,4,3,2,1,0:T(8,128)(2,1)S(1)} %dynamic-slice_bitcast_fusion.1), channel_id=1, source_target_pairs={{0,2},{1,3},{2,0},{3,1},{4,6},{5,7},{6,4},{7,5},{8,10},{9,11},{10,... | collective-permute-start | bytes 6291464 | tf_op jit(solution)/shard_map/ppermute | solution.py:136
  495.9 18.1 %collective-permute-start.2 = (bf16[4,2,2,32,1024]{4,3,2,1,0:T(8,128)(2,1)S(1)}, bf16[4,2,2,32,1024]{4,3,2,1,0:T(8,128)(2,1)}, u32[]{:S(2)}, u32[]{:S(2)}) collective-permute-start(bf16[4,2,2,32,1024]{4,3,2,1,0:T(8,128)(2,1)S(1)} %dynamic-slice_bitcast_fusion.2), channel_id=1, source_target_pairs={{0,4},{1,5},{2,6},{3,7},{4,0},{5,1},{6,2},{7,3},{8,12},{9,13},{10,... | collective-permute-start | bytes 3145736 | tf_op jit(solution)/shard_map/ppermute | solution.py:136
  512.0 3.9 copy-start.45
  515.7 13.2 %slice-start.4 = ((s8[5767168]{0:T(1024)(128)(4,1)}), s8[4194304]{0:T(1024)(128)(4,1)S(1)}, s32[]{:S(2)}) async-start(s8[5767168]{0:T(1024)(128)(4,1)} %bitcast.245), calls=%async_computation.8 | async-start | bytes 8388608
  515.8 13.1 %copy-start.34 = (bf16[1408,1024]{1,0:T(8,128)(2,1)S(1)}, bf16[1408,1024]{1,0:T(8,128)(2,1)}, u32[]{:S(2)}) copy-start(bf16[1408,1024]{1,0:T(8,128)(2,1)} %constant_dynamic-update-slice_fusion) | copy-start | bytes 8650756
  515.8 13.1 %slice-start.5 = ((s8[5767168]{0:T(1024)(128)(4,1)}), s8[1572864]{0:T(1024)(128)(4,1)S(1)}, s32[]{:S(2)}) async-start(s8[5767168]{0:T(1024)(128)(4,1)} %bitcast.245), calls=%async_computation.9 | async-start | bytes 3145728
  515.8 12.1 %collective-permute-start.3 = (bf16[4,2,32,1024]{3,2,1,0:T(8,128)(2,1)S(1)}, bf16[4,2,32,1024]{3,2,1,0:T(8,128)(2,1)S(1)}, u32[]{:S(2)}, u32[]{:S(2)}) collective-permute-start(bf16[4,2,32,1024]{3,2,1,0:T(8,128)(2,1)S(1)} %dynamic-slice_bitcast_fusion.3), channel_id=1, source_target_pairs={{0,8},{8,0},{16,24},{24,16},{1,9},{9,1},{17,25},{25,17},{2,10},{10... | collective-permute-start | bytes 1572872 | tf_op jit(solution)/shard_map/ppermute | solution.py:136
  528.1 9.6 %collective-permute-start.4 = (bf16[4,32,1024]{2,1,0:T(8,128)(2,1)S(1)}, bf16[4,32,1024]{2,1,0:T(8,128)(2,1)S(1)}, u32[]{:S(2)}, u32[]{:S(2)}) collective-permute-start(bf16[4,32,1024]{2,1,0:T(8,128)(2,1)S(1)} %dynamic-slice_bitcast_fusion.4), channel_id=1, source_target_pairs={{0,16},{8,24},{16,0},{24,8},{1,17},{9,25},{17,1},{25,9},{2,18},{10... | collective-permute-start | bytes 786440 | tf_op jit(solution)/shard_map/ppermute | solution.py:136
  528.9 9.7 %copy-start.1 = (bf16[1024,1024]{1,0:T(8,128)(2,1)S(1)}, bf16[1024,1024]{1,0:T(8,128)(2,1)}, u32[]{:S(2)}) copy-start(bf16[1024,1024]{1,0:T(8,128)(2,1)} %param.21) | copy-start | bytes 6291460
  (16 other events, 26.8 us)

commit v2 on v1

--- a/solution.py
+++ b/solution.py
@@ -1,6 +1,9 @@
-import jax
-import jax.numpy as jnp
+import functools
+import jax, jax.numpy as jnp
 from jax import lax
+from jax.experimental import pallas as pl
+from jax.experimental.pallas import tpu as pltpu
+
 from jax.sharding import PartitionSpec as P
 
 HEADS = 16
@@ -159,6 +162,276 @@
             value = value + lax.ppermute(value, axis, [(i, i ^ bit) for i in range(count)])
             bit *= 2
     return value
+
+
+MESH = pl.DeviceIdType.MESH
+BF = jnp.bfloat16
+F32 = jnp.float32
+GELU_A = 0.7978845608028654
+GELU_B = 0.044715
+
+
+def gelu_pair(v):
+    square = v * v
+    bent = jnp.tanh(GELU_A * v * (1.0 + GELU_B * square))
+    half = 0.5 * (1.0 + bent)
+    slope = half + 0.5 * v * (1.0 - bent * bent) * (GELU_A * (1.0 + 3.0 * GELU_B * square))
+    return v * half, slope
+
+
+def dot(a, b, dims=((1,), (0,))):
+    return lax.dot_general(a, b, (dims, ((), ())), preferred_element_type=F32)
+
+
+def finish_kernel(
+    groups, width,
+    rows_in, up_first, down_first, up_second, down_second, dense_in, small_in, gains_in,
+    up_out, down_out, dense_out, small_out, gains_out,
+    rows, ups, downs, up_acc, down_acc, turned, part, d_one, d_two, d_three, d_four, d_five, keep, s_got, g_got,
+    ring_send, ring_recv, dense_send, dense_recv, small_send, small_recv, gain_send, gain_recv, local_sem, out_sem,
+):
+    b, e = lax.axis_index("batch"), lax.axis_index("expert")
+    steps = 2 * groups
+    before = lax.rem(b + groups - 1, groups)
+    after = lax.rem(b + 1, groups)
+    core, x, y = lax.rem(e, 2), lax.rem(e // 2, 2), lax.rem(e // 4, 2)
+    b0, b1 = lax.rem(b, 2), lax.rem(b // 2, 2)
+    e_core = e + 1 - 2 * core
+    e_x = e + 2 - 4 * x
+    e_y = e + 4 - 8 * y
+    b_lo = b + 1 - 2 * b0
+    b_hi = b + 2 - 4 * b1
+    peers = [(b, e_core), (b, e_x), (b, e_y), (before, e), (after, e), (b_hi, e)]
+    barrier = pltpu.get_barrier_semaphore()
+    for peer in peers:
+        pl.semaphore_signal(barrier, inc=1, device_id=peer, device_id_type=MESH)
+
+    loads = []
+    col = pl.multiple_of(b * width, width)
+    for s, (up, down) in enumerate(((up_first, down_first), (up_second, down_second))):
+        loads.append(pltpu.make_async_copy(up.at[0, :, pl.ds(col, width)], ups.at[s], local_sem.at[0, s]))
+        loads.append(pltpu.make_async_copy(down.at[0, pl.ds(col, width), :], downs.at[s], local_sem.at[1, s]))
+    for s in range(2):
+        for kind in range(2):
+            loads.append(pltpu.make_async_copy(rows_in.at[kind, s], rows.at[kind, s, 0], local_sem.at[2 + kind, s]))
+    mine = pltpu.make_async_copy(dense_in.at[core], part, local_sem.at[4, 0])
+    for load in loads:
+        load.start()
+    mine.start()
+    pl.semaphore_wait(barrier, len(peers))
+
+    def remote(src, dst, send, recv, peer):
+        return pltpu.make_async_remote_copy(
+            src_ref=src, dst_ref=dst, send_sem=send, recv_sem=recv, device_id=peer, device_id_type=MESH
+        )
+
+    first_dense = remote(dense_in.at[1 - core], d_one, dense_send.at[0], dense_recv.at[0], (b, e_core))
+    first_dense.start()
+
+    def ring(kind, s, k):
+        return remote(
+            rows.at[kind, s, k - 1], rows.at[kind, s, k], ring_send.at[kind, s, k], ring_recv.at[kind, s, k], (before, e)
+        )
+
+    for s in (1, 0):
+        for kind in range(2):
+            pltpu.make_async_copy(rows_in.at[kind, s], rows.at[kind, s, 0], local_sem.at[2 + kind, s]).wait()
+            ring(kind, s, 1).start()
+    for s in range(2):
+        loads[2 * s].wait()
+        loads[2 * s + 1].wait()
+    up_acc[...] = jnp.zeros_like(up_acc)
+    down_acc[...] = jnp.zeros_like(down_acc)
+
+    def small_step(level, peer):
+        return remote(keep.at[level], s_got.at[level], small_send.at[level], small_recv.at[level], peer)
+
+    def gain_step(level, peer):
+        return remote(
+            keep.at[5 + level, pl.ds(0, 8)], g_got.at[level], gain_send.at[level], gain_recv.at[level], peer
+        )
+
+    def second(m):
+        if m < 2:
+            return remote(part.at[m, 1 - x], d_two.at[m], dense_send.at[1 + m], dense_recv.at[1 + m], (b, e_x))
+        return remote(part.at[m, :, 1 - y], d_two.at[m], dense_send.at[1 + m], dense_recv.at[1 + m], (b, e_y))
+
+    def third(m):
+        if m < 2:
+            return remote(part.at[m, x, 1 - y], d_three.at[m], dense_send.at[5 + m], dense_recv.at[5 + m], (b, e_y))
+        return remote(part.at[m, 1 - x, y], d_three.at[m], dense_send.at[5 + m], dense_recv.at[5 + m], (b, e_x))
+
+    fourth = remote(d_four.at[:, 1 - b0], d_four.at[:, 2], dense_send.at[9], dense_recv.at[9], (b_lo, e))
+    fifth = remote(d_five.at[:, 1 - b1], d_five.at[:, 2], dense_send.at[10], dense_recv.at[10], (b_hi, e))
+
+    keep[0] = small_in[...]
+    keep[5, pl.ds(0, 8)] = gains_in[...]
+    small_step(0, (b, e_core)).start()
+    gain_step(0, (b_lo, e)).start()
+
+    def weight_step(i, carry):
+        k, s = i // 2, 1 - lax.rem(i, 2)
+
+        @pl.when(k > 0)
+        def _():
+            for kind in range(2):
+                ring(kind, s, k).wait_recv()
+
+        @pl.when((k > 0) & (k < groups - 1))
+        def _():
+            for kind in range(2):
+                ring(kind, s, k + 1).start()
+
+        turned[...] = rows[0, s, k].T
+
+        def chunk(c, carry):
+            cols = pl.ds(pl.multiple_of(c * 256, 256), 256)
+            pre = dot(rows[0, s, k], ups[s, :, cols])
+            grad_mid = dot(rows[1, s, k], downs[s, cols, :], ((1,), (1,)))
+            mid, slope = gelu_pair(pre)
+            down_acc[s, cols, :] += dot(mid.astype(BF), rows[1, s, k], ((0,), (0,)))
+            up_acc[s, :, cols] += dot(turned[...], (grad_mid * slope).astype(BF))
+            return carry
+
+        lax.fori_loop(0, width // 256, chunk, 0)
+
+        @pl.when(i == 0)
+        def _():
+            mine.wait()
+            first_dense.wait()
+            small_step(0, (b, e_core)).wait()
+            gain_step(0, (b_lo, e)).wait()
+            keep[1] = keep[0] + s_got[0]
+            keep[6, pl.ds(0, 8)] = keep[5, pl.ds(0, 8)] + g_got[0]
+            small_step(1, (b, e_x)).start()
+            gain_step(1, (b_hi, e)).start()
+            for m in range(4):
+                for xx in range(2):
+                    part[m, xx] = (part[m, xx].astype(F32) + d_one[m, xx].astype(F32)).astype(BF)
+            for m in range(4):
+                second(m).start()
+
+        @pl.when(i == 2)
+        def _():
+            small_step(1, (b, e_x)).wait()
+            gain_step(1, (b_hi, e)).wait()
+            gains_out[...] = keep[6, pl.ds(0, 8)] + g_got[1]
+            keep[2] = keep[1] + s_got[1]
+            small_step(2, (b, e_y)).start()
+            for m in range(4):
+                second(m).wait()
+            for m in range(4):
+                if m < 2:
+                    part[m, x] = (part[m, x].astype(F32) + d_two[m].astype(F32)).astype(BF)
+                else:
+                    for xx in range(2):
+                        part[m, xx, y] = (part[m, xx, y].astype(F32) + d_two[m, xx].astype(F32)).astype(BF)
+            for m in range(4):
+                third(m).start()
+
+        @pl.when(i == 3)
+        def _():
+            small_step(2, (b, e_y)).wait()
+            keep[3] = keep[2] + s_got[2]
+            small_step(3, (b_lo, e)).start()
+            for m in range(4):
+                third(m).wait()
+            for m in range(4):
+                for g in range(4):
+                    d_four[m, g % 2, g // 2] = (part[m, x, y, g].astype(F32) + d_three[m, g].astype(F32)).astype(BF)
+            fourth.start()
+
+        @pl.when(i == 4)
+        def _():
+            small_step(3, (b_lo, e)).wait()
+            keep[4] = keep[3] + s_got[3]
+            small_step(4, (b_hi, e)).start()
+            fourth.wait()
+            for m in range(4):
+                for g in range(2):
+                    d_five[m, g] = (d_four[m, b0, g].astype(F32) + d_four[m, 2, g].astype(F32)).astype(BF)
+            fifth.start()
+
+        @pl.when(i == 5)
+        def _():
+            small_step(4, (b_hi, e)).wait()
+            small_out[...] = keep[4] + s_got[4]
+            fifth.wait()
+            for m in range(4):
+                dense_out[m] = d_five[m, b1].astype(F32) + d_five[m, 2].astype(F32)
+
+        @pl.when(i == steps - 2)
+        def _():
+            pltpu.make_async_copy(up_acc.at[1], up_out.at[1], out_sem.at[0, 1]).start()
+            pltpu.make_async_copy(down_acc.at[1], down_out.at[1], out_sem.at[1, 1]).start()
+
+        return carry
+
+    lax.fori_loop(0, steps, weight_step, 0)
+    for s in range(2):
+        for kind in range(2):
+            for k in range(1, groups):
+                ring(kind, s, k).wait_send()
+    finals = [
+        pltpu.make_async_copy(up_acc.at[s], up_out.at[s], out_sem.at[0, s]) for s in range(2)
+    ] + [pltpu.make_async_copy(down_acc.at[s], down_out.at[s], out_sem.at[1, s]) for s in range(2)]
+    finals[0].start()
+    finals[2].start()
+    for final in finals:
+        final.wait()
+
+
+def finish(rows, up_first, down_first, up_second, down_second, dense, small, gains):
+    groups = lax.axis_size("batch")
+    count, width_all = rows.shape[2], rows.shape[3]
+    width = up_first.shape[2] // groups
+    block = dense.shape[5]
+    any_spec = pl.BlockSpec(memory_space=pl.ANY)
+    vmem = pl.BlockSpec(memory_space=pltpu.VMEM)
+    wide = width_all
+    return pl.pallas_call(
+        functools.partial(finish_kernel, groups, width),
+        out_shape=(
+            jax.ShapeDtypeStruct((2, wide, width), F32),
+            jax.ShapeDtypeStruct((2, width, wide), F32),
+            jax.ShapeDtypeStruct((4, block, wide), F32),
+            jax.ShapeDtypeStruct(small.shape, F32),
+            jax.ShapeDtypeStruct(gains.shape, F32),
+        ),
+        in_specs=[any_spec] * 6 + [vmem] * 2,
+        out_specs=(any_spec, any_spec, vmem, vmem, vmem),
+        scratch_shapes=[
+            pltpu.VMEM((2, 2, groups, count, wide), BF),
+            pltpu.VMEM((2, wide, width), BF),
+            pltpu.VMEM((2, width, wide), BF),
+            pltpu.VMEM((2, wide, width), F32),
+            pltpu.VMEM((2, width, wide), F32),
+            pltpu.VMEM((wide, count), BF),
+            pltpu.VMEM((4, 2, 2, 4, block, wide), BF),
+            pltpu.VMEM((4, 2, 2, 4, block, wide), BF),
+            pltpu.VMEM((4, 2, 4, block, wide), BF),
+            pltpu.VMEM((4, 4, block, wide), BF),
+            pltpu.VMEM((4, 3, 2, block, wide), BF),
+            pltpu.VMEM((4, 3, block, wide), BF),
+            pltpu.VMEM((7,) + small.shape, F32),
+            pltpu.VMEM((5,) + small.shape, F32),
+            pltpu.VMEM((2,) + gains.shape, F32),
+            pltpu.SemaphoreType.DMA((2, 2, groups)),
+            pltpu.SemaphoreType.DMA((2, 2, groups)),
+            pltpu.SemaphoreType.DMA((11,)),
+            pltpu.SemaphoreType.DMA((11,)),
+            pltpu.SemaphoreType.DMA((5,)),
+            pltpu.SemaphoreType.DMA((5,)),
+            pltpu.SemaphoreType.DMA((2,)),
+            pltpu.SemaphoreType.DMA((2,)),
+            pltpu.SemaphoreType.DMA((5, 2)),
+            pltpu.SemaphoreType.DMA((2, 2)),
+        ],
+        compiler_params=pltpu.CompilerParams(
+            collective_id=1, has_side_effects=True, vmem_limit_bytes=64 * 1024 * 1024 - 65536
+        ),
+        name="finish",
+    )(rows, up_first, down_first, up_second, down_second, dense, small, gains)
 
 
 def slot_layout(tokens, routes):
@@ -368,29 +641,50 @@
     norm_pull = jax.vjp(layer_norm, stream, attn_gain)[1]
     grad_input_norm, grad_gain_att = norm_pull(grad_normed)
     grad_tokens = grad_hidden + grad_input_norm
-    dense = scatter_sum(
-        jnp.stack((grad_query_w, grad_key_w, grad_value_w, grad_output_w)).astype(jnp.bfloat16)
-    ).astype(jnp.float32)
-    small = all_sum(jnp.concatenate((grad_gain_att[None], grad_centroids), axis=0))
-    up_two_grad, down_two_grad = weight_grads(
-        ring_rows(kept_two[1], "batch"), ring_rows(low_two, "batch"), up_second[0], down_second[0]
-    )
-    up_one_grad, down_one_grad = weight_grads(
-        ring_rows(kept_one[1], "batch"), ring_rows(low_one, "batch"), up_first[0], down_first[0]
-    )
-    gains = lax.all_gather(jnp.stack((gain_one_grad, gain_two_grad)), "batch")
-    gain_part = gain_one_grad.shape[0] // lax.axis_size("batch")
-    gains = lax.dynamic_slice_in_dim(
-        jnp.sum(gains, axis=0), lax.axis_index("batch") * gain_part, gain_part, 1
-    )
-    expert_parts = (
-        up_one_grad[None],
-        down_one_grad[None],
-        gains[0:1],
-        up_two_grad[None],
-        down_two_grad[None],
-        gains[1:2],
-    )
+    grads = (grad_query_w, grad_key_w, grad_value_w, grad_output_w)
+    if lax.axis_size("batch") == 4 and expert_count == 8:
+        stacked = jnp.stack(grads).astype(jnp.bfloat16)
+        pieces = stacked.reshape(4, 4, 2, 2, 2, width_all // 32, width_all).transpose(4, 0, 3, 2, 1, 5, 6)
+        small_in = jnp.concatenate(
+            (grad_gain_att[None], grad_centroids, jnp.zeros((7, width_all), jnp.float32)), axis=0
+        )
+        gains_in = jnp.concatenate(
+            (gain_one_grad[None], gain_two_grad[None], jnp.zeros((6, width_all), jnp.float32)), axis=0
+        )
+        rows = jnp.stack((kept_one[1], kept_two[1], low_one, low_two)).reshape(2, 2, -1, width_all)
+        up_parts, down_parts, dense, small, gains = finish(
+            rows, up_first, down_first, up_second, down_second, pieces, small_in, gains_in
+        )
+        gain_part = width_all // 4
+        gains = lax.dynamic_slice_in_dim(gains, lax.axis_index("batch") * gain_part, gain_part, 1)
+        small = small[:9]
+        expert_parts = (
+            up_parts[0:1], down_parts[0:1], gains[0:1], up_parts[1:2], down_parts[1:2], gains[1:2],
+        )
+    else:
+        dense = scatter_sum(
+            jnp.stack((grad_query_w, grad_key_w, grad_value_w, grad_output_w)).astype(jnp.bfloat16)
+        ).astype(jnp.float32)
+        small = all_sum(jnp.concatenate((grad_gain_att[None], grad_centroids), axis=0))
+        up_two_grad, down_two_grad = weight_grads(
+            ring_rows(kept_two[1], "batch"), ring_rows(low_two, "batch"), up_second[0], down_second[0]
+        )
+        up_one_grad, down_one_grad = weight_grads(
+            ring_rows(kept_one[1], "batch"), ring_rows(low_one, "batch"), up_first[0], down_first[0]
+        )
+        gains = lax.all_gather(jnp.stack((gain_one_grad, gain_two_grad)), "batch")
+        gain_part = gain_one_grad.shape[0] // lax.axis_size("batch")
+        gains = lax.dynamic_slice_in_dim(
+            jnp.sum(gains, axis=0), lax.axis_index("batch") * gain_part, gain_part, 1
+        )
+        expert_parts = (
+            up_one_grad[None],
+            down_one_grad[None],
+            gains[0:1],
+            up_two_grad[None],
+            down_two_grad[None],
+            gains[1:2],
+        )
     return (
         block_out,
         grad_tokens,

time: 546 us -> 480 us (0.88)
  the two profiles are of different devices: /device:TPU:0 before, /device:TPU:26 now
where the time goes in v2:
time: 480 us; the launch traced here: 474 us
  Pallas kernels  242 us (50%)
  matrix products  103 us (21%)
  local copies, waits for them, and re-layouts  39.3 us (8%)
  other arithmetic  34.9 us (7%)
  waiting for transfers between devices  21.4 us (4%)
  starting transfers between devices  15.9 us (3%)
  blocking collectives  15.3 us (3%)
    pallas_call x1, Pallas kernels, finish(): pl.pallas_call(functools.partial(finish_kernel, groups, width), out_shape...  242 us
    dot_general x2, matrix products, sublayer_backward(): jnp.einsum('rf,df->rd', grad_pre, up_proj, preferred_element_type=jnp.flo...  30.5 us
    dot_general x2, matrix products, sublayer_forward(): pre_act = jnp.dot(normed, up_proj, preferred_element_type=jnp.float32)  15.7 us
    all_to_all x1, blocking collectives, forward_pass(): lax.all_to_all(outgoing.reshape(expert_count, capacity, width_all), 'expe...  15.3 us
    dot_general x2, matrix products, sublayer_forward(): jnp.dot(middle, down_proj, preferred_element_type=jnp.float32)  12.9 us
    slice x1, local copies, waits for them, and re-layouts, per_device(): down_parts[1:2]  12.4 us
  transfers between devices with their start and end apart: 3, of which 3 were waited for; matrix products, arithmetic and copies ran while one was open for 3% of the time, Pallas kernels for 0%

profile of v2, /device:TPU:26, one launch (start us, length us, event | category | flops | bytes accessed | tf_op | source)
XLA Modules:
  0.0 473.6 jit_solution(11242376441769994609)
XLA Ops:
  0.7 0.8 convert_reduce_fusion.2
  1.5 1.2 convert_reduce_fusion
  2.7 1.3 fusion.112
  5.5 0.8 fusion.133
  7.1 2.5 convolution_convert_fusion.1
  9.9 2.5 convolution_convert_fusion.2
  12.6 2.5 convolution_convert_fusion.3
  15.4 0.8 fusion.179
  16.9 0.9 fusion.95
  18.3 1.2 copy-done.5
  20.3 1.9 scatter_custom_fusion
  22.3 15.3 %all_to_all.20 = bf16[8,44,1024]{2,1,0:T(8,128)(2,1)S(1)} all-to-all(bf16[8,44,1024]{2,1,0:T(8,128)(2,1)S(1)} %reshape.437), channel_id=1, replica_groups=mesh['batch'=4,'expert'=8] {'expert'}, dimensions={0} | all-to-all | bytes 1441792 | tf_op jit(solution)/shard_map/all_to_all | solution.py:496
  38.5 1.0 convert_element_type.199
  39.5 9.2 %fusion.15 = f32[352,4096]{1,0:T(8,128)} fusion(bf16[352,1024]{1,0:T(8,128)(2,1)} %convert_element_type.199, bf16[1,1024,4096]{2,1,0:T(8,128)(2,1)} %up_first.1), kind=kOutput, calls=%fused_computation.20 | convolution fusion | flops 2952790016 | bytes 14876672 | tf_op jit(solution)/shard_map/dot_general | solution.py:90
  48.8 1.2 reshape.451
  50.0 9.1 %fusion.180 = (f32[352]{0:T(512)S(1)}, f32[352,1024]{1,0:T(8,128)S(1)}) fusion(f32[352,1024]{1,0:T(8,128)} %reshape.451, bf16[1,4096,1024]{2,1,0:T(8,128)(2,1)} %down_first.1, f32[352,4096]{1,0:T(8,128)} %fusion.15), kind=kOutput, calls=%fused_computation.236 | convolution fusion | flops 2966486784 | bytes 17040768 | tf_op jit(solution)/shard_map/dot_general | solution.py:92
  59.5 6.4 %fusion.7 = f32[352,4096]{1,0:T(8,128)S(1)} fusion(bf16[1,1024,4096]{2,1,0:T(8,128)(2,1)} %up_second.1, f32[352,1024]{1,0:T(8,128)S(1)} %get-tuple-element.111, f32[1024]{0:T(1024)S(1)} %bitcast.191, f32[352]{0:T(512)S(1)} %fusion.141, f32[352]{0:T(512)S(1)} %broadcast_multiply_fusion.1), kind=kOutput, calls=%fused_computation.12 | convolution fusion | flops 2954231808 | bytes 15604480 | tf_op jit(solution)/shard_map/dot_general | solution.py:90
  66.0 2.5 copy-done.24
  68.5 3.8 add_convert_fusion.1
  72.3 1.0 reshape.438
  73.4 5.6 %all-to-all-start.1 = ((bf16[8,44,1024]{2,1,0:T(8,128)(2,1)}), bf16[8,44,1024]{2,1,0:T(8,128)(2,1)}, u32[]{:S(2)}, u32[]{:S(2)}) async-start(bf16[8,44,1024]{2,1,0:T(8,128)(2,1)} %reshape.438), calls=%async_computation.1 | async-start | bytes 1572864 | tf_op jit(solution)/shard_map/all_to_all | solution.py:509
  80.4 0.9 fusion.104
  81.5 1.2 reshape.452
  82.7 7.4 %all-to-all-done.1 = bf16[8,44,1024]{2,1,0:T(8,128)(2,1)} async-done(((bf16[8,44,1024]{2,1,0:T(8,128)(2,1)}), bf16[8,44,1024]{2,1,0:T(8,128)(2,1)}, u32[]{:S(2)}, u32[]{:S(2)}) %all-to-all-start.1) | async-done | bytes 720928 | tf_op jit(solution)/shard_map/all_to_all | solution.py:509
  90.1 1.2 reshape.439
  91.4 1.2 gather_fusion
  92.9 2.0 scatter_custom_fusion.1
  95.0 1.0 reshape.440
  96.0 5.4 %all-to-all-start.2 = ((bf16[8,44,1024]{2,1,0:T(8,128)(2,1)}), bf16[8,44,1024]{2,1,0:T(8,128)(2,1)S(1)}, u32[]{:S(2)}, u32[]{:S(2)}) async-start(bf16[8,44,1024]{2,1,0:T(8,128)(2,1)} %reshape.440), calls=%async_computation.2 | async-start | bytes 1572864 | tf_op jit(solution)/shard_map/all_to_all | solution.py:594
  101.4 2.5 multiply_convert_fusion.6
  103.9 1.1 fusion.109
  104.9 7.5 %all-to-all-done.2 = bf16[8,44,1024]{2,1,0:T(8,128)(2,1)S(1)} async-done(((bf16[8,44,1024]{2,1,0:T(8,128)(2,1)}), bf16[8,44,1024]{2,1,0:T(8,128)(2,1)S(1)}, u32[]{:S(2)}, u32[]{:S(2)}) %all-to-all-start.2) | async-done | bytes 720928 | tf_op jit(solution)/shard_map/all_to_all | solution.py:594
  112.6 15.1 %multiply_reduce_fusion.2 = (f32[1024]{0:T(1024)S(1)}, f32[352]{0:T(512)S(1)}, f32[352,1024]{1,0:T(8,128)}) fusion(f32[352,1024]{1,0:T(8,128)} %copy-done.7, f32[352]{0:T(512)S(1)} %fusion.141, f32[352]{0:T(512)S(1)} %broadcast_multiply_fusion.1, f32[1024]{0:T(1024)S(1)} %bitcast.192, bf16[1,1024,4096]{2,1,0:T(8,128)(2,1)} %up_second.1, ...), kind=kOutput, calls=%fused_computation.97 | convolution fusion | flops 5936937472 | bytes 26161280 | tf_op jit(solution)/shard_map/rf,df->rd/dot_general | solution.py:102
  127.8 3.2 fusion.175
  131.0 1.1 copy-done.3
  132.1 1.1 fusion.116
  133.2 15.3 %multiply_reduce_fusion.3 = (f32[1024]{0:T(1024)S(1)}, f32[352]{0:T(512)S(1)}, f32[352,1024]{1,0:T(8,128)}) fusion(f32[352,1024]{1,0:T(8,128)} %reshape.451, f32[352]{0:T(512)S(1)} %div.100, f32[352]{0:T(512)S(1)} %rsqrt.39, f32[1024]{0:T(1024)S(1)} %bitcast.176, bf16[1,1024,4096]{2,1,0:T(8,128)(2,1)} %up_first.1, f32[352,4096]{1,0:T(8,128)} %fusion.15, ...), kind=kOutput, calls=%fused_computation.98 | convolution fusion | flops 5936937472 | bytes 26161280 | tf_op jit(solution)/shard_map/rf,df->rd/dot_general | solution.py:102
  148.5 2.4 fusion.174
  151.0 1.2 add_convert_fusion
  152.2 2.0 reshape.442
  154.2 5.0 %all-to-all-start.3 = ((bf16[8,44,1024]{2,1,0:T(8,128)(2,1)}), bf16[8,44,1024]{2,1,0:T(8,128)(2,1)S(1)}, u32[]{:S(2)}, u32[]{:S(2)}) async-start(bf16[8,44,1024]{2,1,0:T(8,128)(2,1)} %reshape.442), calls=%async_computation.3 | async-start | bytes 1572864 | tf_op jit(solution)/shard_map/all_to_all | solution.py:608
  160.7 3.1 pad_maximum_fusion
  163.9 6.4 %all-to-all-done.3 = bf16[8,44,1024]{2,1,0:T(8,128)(2,1)S(1)} async-done(((bf16[8,44,1024]{2,1,0:T(8,128)(2,1)}), bf16[8,44,1024]{2,1,0:T(8,128)(2,1)S(1)}, u32[]{:S(2)}, u32[]{:S(2)}) %all-to-all-start.3) | async-done | bytes 720928 | tf_op jit(solution)/shard_map/all_to_all | solution.py:608
  170.4 1.2 gather_fusion.1
  171.6 1.2 fusion.91
  172.8 2.3 convolution_convert_fusion
  175.4 2.9 fusion.185
  178.7 0.8 fusion.92
  179.5 7.6 %fusion.96 = bf16[16,64,256]{2,1,0:T(8,128)(2,1)S(1)} fusion(bf16[256,16,64]{0,2,1:T(8,128)(2,1)S(1)} %bitcast.171, f32[16,256,256]{1,2,0:T(8,128)} %fusion.185, f32[16,256,256]{1,2,0:T(8,128)} %copy-done, f32[16,256]{1,0:T(8,128)S(1)} %log_add_fusion), kind=kOutput, calls=%fused_computation.120 | convolution fusion | flops 141824256 | bytes 9453568 | tf_op jit(solution)/shard_map/while/body/eval_jaxpr/hqk,khd->qhd/dot_general | solution.py:67
  187.1 7.8 %fusion.99 = bf16[16,64,256]{2,1,0:T(8,128)(2,1)S(1)} fusion(bf16[256,16,64]{0,2,1:T(8,128)(2,1)} %bitcast.173, f32[16,256,256]{1,2,0:T(8,128)} %fusion.185, f32[16,256,256]{1,2,0:T(8,128)} %copy-done, f32[16,256]{1,0:T(8,128)S(1)} %log_add_fusion), kind=kOutput, calls=%fused_computation.121 | convolution fusion | flops 141824256 | bytes 9453568 | tf_op jit(solution)/shard_map/while/body/eval_jaxpr/hqk,qhd->khd/dot_general | solution.py:70
  194.9 3.2 convert_bitcast_fusion
  198.1 2.5 fusion.186
  200.6 0.8 convolution_add_fusion.1
  201.5 1.0 fusion.113
  203.0 1.6 fusion.170
  204.6 1.2 copy.76
  205.9 1.0 convert_bitcast_fusion.2
  209.0 3.8 maximum_bitcast_fusion.dense_in
  212.9 241.9 %finish.1 = (f32[2,1024,1024]{2,1,0:T(8,128)}, f32[2,1024,1024]{2,1,0:T(8,128)}, f32[4,32,1024]{2,1,0:T(8,128)}, f32[16,1024]{1,0:T(8,128)}, f32[8,1024]{1,0:T(8,128)}) custom-call(bf16[2,2,352,1024]{3,2,1,0:T(8,128)(2,1)} %bitcast.151, bf16[1,1024,4096]{2,1,0:T(8,128)(2,1)} %up_first.1, bf16[1,4096,1024]{2,1,0:T(8,128)(2,1)} %down_first.1, ...), custom_call_target="tpu_custom_call" | custom-call | tf_op jit(solution)/shard_map/finish/pallas_call | solution.py:392
  454.8 1.4 slice.55
  456.2 1.5 slice.56
  457.6 1.9 slice_bitcast_fusion
  459.5 12.4 %fusion.176 = (f32[1,1024,1024]{2,1,0:T(8,128)}, f32[1,1024,1024]{2,1,0:T(8,128)}, f32[1,1024,1024]{2,1,0:T(8,128)}, f32[1,1024,1024]{2,1,0:T(8,128)}) fusion(f32[2,1024,1024]{2,1,0:T(8,128)} %get-tuple-element.79, f32[2,1024,1024]{2,1,0:T(8,128)} %get-tuple-element.78), kind=kLoop, calls=%fused_computation.232 | loop fusion | bytes 33554432 | tf_op jit(solution)/shard_map/slice | solution.py:662
  471.9 1.4 fusion.178
  (106 shorter events, 13.3 us)
Async XLA Ops:
  0.6 9.2 %copy-start.2 = (bf16[256,1024]{1,0:T(8,128)(2,1)S(1)}, bf16[256,1024]{1,0:T(8,128)(2,1)}, u32[]{:S(2)}) copy-start(bf16[256,1024]{1,0:T(8,128)(2,1)} %param.16) | copy-start | bytes 1572868
  0.7 9.2 %copy-start.21 = (f32[1024]{0:T(1024)S(1)}, f32[1024]{0:T(1024)}, u32[]{:S(2)}) copy-start(f32[1024]{0:T(1024)} %param.23) | copy-start | bytes 12292
  9.9 5.6 %copy-start.15 = (bf16[256,1024]{0,1:T(8,128)(2,1)}, bf16[256,1024]{0,1:T(8,128)(2,1)S(1)}, u32[]{:S(2)}) copy-start(bf16[256,1024]{0,1:T(8,128)(2,1)S(1)} %copy.70) | copy-start | bytes 1572868
  12.6 3.7 copy-start.17
  15.4 1.5 copy-start.10
  16.3 2.0 copy-start
  16.9 2.7 copy-start.5
  18.3 2.0 copy-start.14
  20.3 17.9 %copy-start.19 = (f32[1,1024]{1,0:T(1,128)S(1)}, f32[1,1024]{1,0:T(1,128)}, u32[]{:S(2)}) copy-start(f32[1,1024]{1,0:T(1,128)} %param.27) | copy-start | bytes 12292
  50.0 9.5 %copy-start.22 = (f32[1,1024]{1,0:T(1,128)S(1)}, f32[1,1024]{1,0:T(1,128)}, u32[]{:S(2)}) copy-start(f32[1,1024]{1,0:T(1,128)} %param.30) | copy-start | bytes 12292
  59.1 6.8 %copy-start.7 = (f32[352,1024]{1,0:T(8,128)}, f32[352,1024]{1,0:T(8,128)S(1)}, u32[]{:S(2)}) copy-start(f32[352,1024]{1,0:T(8,128)S(1)} %get-tuple-element.111) | copy-start | bytes 4325380
  59.2 9.3 %slice-start = ((s8[8388608]{0:T(1024)(128)(4,1)}), s8[4194304]{0:T(1024)(128)(4,1)S(1)}, s32[]{:S(2)}) async-start(s8[8388608]{0:T(1024)(128)(4,1)} %bitcast.152), calls=%async_computation.4 | async-start | bytes 8388608
  59.5 9.0 %slice-start.1 = ((s8[8388608]{0:T(1024)(128)(4,1)}), s8[4194304]{0:T(1024)(128)(4,1)S(1)}, s32[]{:S(2)}) async-start(s8[8388608]{0:T(1024)(128)(4,1)} %bitcast.152), calls=%async_computation.5 | async-start | bytes 8388608
  66.0 2.6 copy-start.24
  68.5 10.4 %copy-start.23 = (s32[1,4]{1,0:T(1,128)S(1)}, s32[1,4]{1,0:T(1,128)}, u32[]{:S(2)}) copy-start(s32[1,4]{1,0:T(1,128)} %param.17) | copy-start | bytes 52
  68.5 11.8 %copy-start.18 = (f32[8,1024]{1,0:T(8,128)S(1)}, f32[8,1024]{1,0:T(8,128)}, u32[]{:S(2)}) copy-start(f32[8,1024]{1,0:T(8,128)} %param.24) | copy-start | bytes 98308
  68.5 11.8 %copy-start.20 = (s32[256,1]{0,1:T(1,128)S(1)}, s32[256,1]{0,1:T(1,128)}, u32[]{:S(2)}) copy-start(s32[256,1]{0,1:T(1,128)} %param.18) | copy-start | bytes 3076
  73.4 16.8 %all-to-all-start.1 = ((bf16[8,44,1024]{2,1,0:T(8,128)(2,1)}), bf16[8,44,1024]{2,1,0:T(8,128)(2,1)}, u32[]{:S(2)}, u32[]{:S(2)}) async-start(bf16[8,44,1024]{2,1,0:T(8,128)(2,1)} %reshape.438), calls=%async_computation.1 | async-start | bytes 1572864 | tf_op jit(solution)/shard_map/all_to_all | solution.py:509
  81.5 11.1 %copy-start.8 = (bf16[256,1024]{1,0:T(8,128)(2,1)S(1)}, bf16[256,1024]{1,0:T(8,128)(2,1)}, u32[]{:S(2)}) copy-start(bf16[256,1024]{1,0:T(8,128)(2,1)} %param.31) | copy-start | bytes 1572868
  96.0 16.5 %all-to-all-start.2 = ((bf16[8,44,1024]{2,1,0:T(8,128)(2,1)}), bf16[8,44,1024]{2,1,0:T(8,128)(2,1)S(1)}, u32[]{:S(2)}, u32[]{:S(2)}) async-start(bf16[8,44,1024]{2,1,0:T(8,128)(2,1)} %reshape.440), calls=%async_computation.2 | async-start | bytes 1572864 | tf_op jit(solution)/shard_map/all_to_all | solution.py:594
  131.0 1.1 copy-start.3
  148.5 2.4 copy-start.4
  154.2 16.1 %all-to-all-start.3 = ((bf16[8,44,1024]{2,1,0:T(8,128)(2,1)}), bf16[8,44,1024]{2,1,0:T(8,128)(2,1)S(1)}, u32[]{:S(2)}, u32[]{:S(2)}) async-start(bf16[8,44,1024]{2,1,0:T(8,128)(2,1)} %reshape.442), calls=%async_computation.3 | async-start | bytes 1572864 | tf_op jit(solution)/shard_map/all_to_all | solution.py:608
  163.8 7.8 %copy-start.9 = (bf16[256,1024]{1,0:T(8,128)(2,1)S(1)}, bf16[256,1024]{1,0:T(8,128)(2,1)}, u32[]{:S(2)}) copy-start(bf16[256,1024]{1,0:T(8,128)(2,1)} %param.31) | copy-start | bytes 1572868
  171.6 3.8 copy-start.11
  175.4 3.3 copy-start.1
  175.4 4.1 copy-start.16
  194.9 5.7 %copy-start.12 = (bf16[1024,1024]{1,0:T(8,128)(2,1)S(1)}, bf16[1024,1024]{1,0:T(8,128)(2,1)}, u32[]{:S(2)}) copy-start(bf16[1024,1024]{1,0:T(8,128)(2,1)} %param.20) | copy-start | bytes 6291460
  198.1 3.3 copy-start.13
  205.9 3.2 copy-start.6

commit v3 on v2

v3 whole, which is shorter than its diff:
```python
import functools
import jax, jax.numpy as jnp
from jax import lax
from jax.experimental import pallas as pl
from jax.experimental.pallas import tpu as pltpu
from jax.sharding import PartitionSpec as P


MESH = pl.DeviceIdType.MESH
BF = jnp.bfloat16
F32 = jnp.float32
GELU_A = 0.7978845608028654
GELU_B = 0.044715


def gelu_pair(v):
    square = v * v
    bent = jnp.tanh(GELU_A * v * (1.0 + GELU_B * square))
    half = 0.5 * (1.0 + bent)
    slope = half + 0.5 * v * (1.0 - bent * bent) * (GELU_A * (1.0 + 3.0 * GELU_B * square))
    return v * half, slope


def dot(a, b, dims=((1,), (0,))):
    return lax.dot_general(a, b, (dims, ((), ())), preferred_element_type=F32)


def finish_kernel(
    groups, width,
    rows_in, up_first, down_first, up_second, down_second, dense_in, small_in, gains_in,
    up_one, down_one, up_two, down_two, dense_out, small_out, gains_out,
    rows, ups, downs, up_acc, down_acc, turned, part, d_one, d_two, d_three, d_four, d_five, keep, s_got, g_got,
    ring_send, ring_recv, dense_send, dense_recv, small_send, small_recv, gain_send, gain_recv, local_sem, out_sem,
):
    b, e = lax.axis_index("batch"), lax.axis_index("expert")
    steps = 2 * groups
    before = lax.rem(b + groups - 1, groups)
    after = lax.rem(b + 1, groups)
    core, x, y = lax.rem(e, 2), lax.rem(e // 2, 2), lax.rem(e // 4, 2)
    b0, b1 = lax.rem(b, 2), lax.rem(b // 2, 2)
    e_core = e + 1 - 2 * core
    e_x = e + 2 - 4 * x
    e_y = e + 4 - 8 * y
    b_lo = b + 1 - 2 * b0
    b_hi = b + 2 - 4 * b1
    peers = [(b, e_core), (b, e_x), (b, e_y), (before, e), (after, e), (b_hi, e)]
    barrier = pltpu.get_barrier_semaphore()
    for peer in peers:
        pl.semaphore_signal(barrier, inc=1, device_id=peer, device_id_type=MESH)

    loads = []
    col = pl.multiple_of(b * width, width)
    for s, (up, down) in enumerate(((up_first, down_first), (up_second, down_second))):
        loads.append(pltpu.make_async_copy(up.at[0, :, pl.ds(col, width)], ups.at[s], local_sem.at[0, s]))
        loads.append(pltpu.make_async_copy(down.at[0, pl.ds(col, width), :], downs.at[s], local_sem.at[1, s]))
    for s in range(2):
        for kind in range(2):
            loads.append(pltpu.make_async_copy(rows_in.at[kind, s], rows.at[kind, s, 0], local_sem.at[2 + kind, s]))
    mine = pltpu.make_async_copy(dense_in.at[core], part, local_sem.at[4, 0])
    for load in loads:
        load.start()
    mine.start()
    pl.semaphore_wait(barrier, len(peers))

    def remote(src, dst, send, recv, peer):
        return pltpu.make_async_remote_copy(
            src_ref=src, dst_ref=dst, send_sem=send, recv_sem=recv, device_id=peer, device_id_type=MESH
        )

    first_dense = remote(dense_in.at[1 - core], d_one, dense_send.at[0], dense_recv.at[0], (b, e_core))
    first_dense.start()

    def ring(kind, s, k):
        return remote(
            rows.at[kind, s, k - 1], rows.at[kind, s, k], ring_send.at[kind, s, k], ring_recv.at[kind, s, k], (before, e)
        )

    for s in (1, 0):
        for kind in range(2):
            pltpu.make_async_copy(rows_in.at[kind, s], rows.at[kind, s, 0], local_sem.at[2 + kind, s]).wait()
            ring(kind, s, 1).start()
    for s in range(2):
        loads[2 * s].wait()
        loads[2 * s + 1].wait()
    up_acc[...] = jnp.zeros_like(up_acc)
    down_acc[...] = jnp.zeros_like(down_acc)

    def small_step(level, peer):
        return remote(keep.at[level], s_got.at[level], small_send.at[level], small_recv.at[level], peer)

    def gain_step(level, peer):
        return remote(
            keep.at[5 + level, pl.ds(0, 8)], g_got.at[level], gain_send.at[level], gain_recv.at[level], peer
        )

    def second(m):
        if m < 2:
            return remote(part.at[m, 1 - x], d_two.at[m], dense_send.at[1 + m], dense_recv.at[1 + m], (b, e_x))
        return remote(part.at[m, :, 1 - y], d_two.at[m], dense_send.at[1 + m], dense_recv.at[1 + m], (b, e_y))

    def third(m):
        if m < 2:
            return remote(part.at[m, x, 1 - y], d_three.at[m], dense_send.at[5 + m], dense_recv.at[5 + m], (b, e_y))
        return remote(part.at[m, 1 - x, y], d_three.at[m], dense_send.at[5 + m], dense_recv.at[5 + m], (b, e_x))

    fourth = remote(d_four.at[:, 1 - b0], d_four.at[:, 2], dense_send.at[9], dense_recv.at[9], (b_lo, e))
    fifth = remote(d_five.at[:, 1 - b1], d_five.at[:, 2], dense_send.at[10], dense_recv.at[10], (b_hi, e))

    keep[0] = small_in[...]
    keep[5, pl.ds(0, 8)] = gains_in[...]
    small_step(0, (b, e_core)).start()
    gain_step(0, (b_lo, e)).start()

    def results(s):
        up_out, down_out = ((up_one, down_one), (up_two, down_two))[s]
        return (
            pltpu.make_async_copy(up_acc.at[s], up_out.at[0], out_sem.at[0, s]),
            pltpu.make_async_copy(down_acc.at[s], down_out.at[0], out_sem.at[1, s]),
        )

    def weight_step(i, carry):
        k, s = i // 2, 1 - lax.rem(i, 2)

        @pl.when(k > 0)
        def _():
            for kind in range(2):
                ring(kind, s, k).wait_recv()

        @pl.when((k > 0) & (k < groups - 1))
        def _():
            for kind in range(2):
                ring(kind, s, k + 1).start()

        turned[...] = rows[0, s, k].T

        def chunk(c, carry):
            cols = pl.ds(pl.multiple_of(c * 256, 256), 256)
            pre = dot(rows[0, s, k], ups[s, :, cols])
            grad_mid = dot(rows[1, s, k], downs[s, cols, :], ((1,), (1,)))
            mid, slope = gelu_pair(pre)
            down_acc[s, cols, :] += dot(mid.astype(BF), rows[1, s, k], ((0,), (0,)))
            up_acc[s, :, cols] += dot(turned[...], (grad_mid * slope).astype(BF))
            return carry

        lax.fori_loop(0, width // 256, chunk, 0)

        @pl.when(i == 0)
        def _():
            mine.wait()
            first_dense.wait()
            small_step(0, (b, e_core)).wait()
            gain_step(0, (b_lo, e)).wait()
            keep[1] = keep[0] + s_got[0]
            keep[6, pl.ds(0, 8)] = keep[5, pl.ds(0, 8)] + g_got[0]
            small_step(1, (b, e_x)).start()
            gain_step(1, (b_hi, e)).start()
            for m in range(4):
                for xx in range(2):
                    part[m, xx] = (part[m, xx].astype(F32) + d_one[m, xx].astype(F32)).astype(BF)
            for m in range(4):
                second(m).start()

        @pl.when(i == 2)
        def _():
            small_step(1, (b, e_x)).wait()
            gain_step(1, (b_hi, e)).wait()
            gains_out[...] = keep[6, pl.ds(0, 8)] + g_got[1]
            keep[2] = keep[1] + s_got[1]
            small_step(2, (b, e_y)).start()
            for m in range(4):
                second(m).wait()
            for m in range(4):
                if m < 2:
                    part[m, x] = (part[m, x].astype(F32) + d_two[m].astype(F32)).astype(BF)
                else:
                    for xx in range(2):
                        part[m, xx, y] = (part[m, xx, y].astype(F32) + d_two[m, xx].astype(F32)).astype(BF)
            for m in range(4):
                third(m).start()

        @pl.when(i == 3)
        def _():
            small_step(2, (b, e_y)).wait()
            keep[3] = keep[2] + s_got[2]
            small_step(3, (b_lo, e)).start()
            for m in range(4):
                third(m).wait()
            for m in range(4):
                for g in range(4):
                    d_four[m, g % 2, g // 2] = (part[m, x, y, g].astype(F32) + d_three[m, g].astype(F32)).astype(BF)
            fourth.start()

        @pl.when(i == 4)
        def _():
            small_step(3, (b_lo, e)).wait()
            keep[4] = keep[3] + s_got[3]
            small_step(4, (b_hi, e)).start()
            fourth.wait()
            for m in range(4):
                for g in range(2):
                    d_five[m, g] = (d_four[m, b0, g].astype(F32) + d_four[m, 2, g].astype(F32)).astype(BF)
            fifth.start()

        @pl.when(i == 5)
        def _():
            small_step(4, (b_hi, e)).wait()
            small_out[...] = keep[4] + s_got[4]
            fifth.wait()
            for m in range(4):
                dense_out[m] = d_five[m, b1].astype(F32) + d_five[m, 2].astype(F32)

        @pl.when(i == steps - 2)
        def _():
            for copy in results(1):
                copy.start()

        return carry

    lax.fori_loop(0, steps, weight_step, 0)
    for s in range(2):
        for kind in range(2):
            for k in range(1, groups):
                ring(kind, s, k).wait_send()
    for copy in results(0):
        copy.start()
    for copy in results(1) + results(0):
        copy.wait()


def finish(rows, up_first, down_first, up_second, down_second, dense, small, gains):
    groups = lax.axis_size("batch")
    count, width_all = rows.shape[2], rows.shape[3]
    width = up_first.shape[2] // groups
    block = dense.shape[5]
    any_spec = pl.BlockSpec(memory_space=pl.ANY)
    vmem = pl.BlockSpec(memory_space=pltpu.VMEM)
    wide = width_all
    return pl.pallas_call(
        functools.partial(finish_kernel, groups, width),
        out_shape=(
            jax.ShapeDtypeStruct((1, wide, width), F32),
            jax.ShapeDtypeStruct((1, width, wide), F32),
            jax.ShapeDtypeStruct((1, wide, width), F32),
            jax.ShapeDtypeStruct((1, width, wide), F32),
            jax.ShapeDtypeStruct((4, block, wide), F32),
            jax.ShapeDtypeStruct(small.shape, F32),
            jax.ShapeDtypeStruct(gains.shape, F32),
        ),
        in_specs=[any_spec] * 6 + [vmem] * 2,
        out_specs=(any_spec,) * 4 + (vmem,) * 3,
        scratch_shapes=[
            pltpu.VMEM((2, 2, groups, count, wide), BF),
            pltpu.VMEM((2, wide, width), BF),
            pltpu.VMEM((2, width, wide), BF),
            pltpu.VMEM((2, wide, width), F32),
            pltpu.VMEM((2, width, wide), F32),
            pltpu.VMEM((wide, count), BF),
            pltpu.VMEM((4, 2, 2, 4, block, wide), BF),
            pltpu.VMEM((4, 2, 2, 4, block, wide), BF),
            pltpu.VMEM((4, 2, 4, block, wide), BF),
            pltpu.VMEM((4, 4, block, wide), BF),
            pltpu.VMEM((4, 3, 2, block, wide), BF),
            pltpu.VMEM((4, 3, block, wide), BF),
            pltpu.VMEM((7,) + small.shape, F32),
            pltpu.VMEM((5,) + small.shape, F32),
            pltpu.VMEM((2,) + gains.shape, F32),
            pltpu.SemaphoreType.DMA((2, 2, groups)),
            pltpu.SemaphoreType.DMA((2, 2, groups)),
            pltpu.SemaphoreType.DMA((11,)),
            pltpu.SemaphoreType.DMA((11,)),
            pltpu.SemaphoreType.DMA((5,)),
            pltpu.SemaphoreType.DMA((5,)),
            pltpu.SemaphoreType.DMA((2,)),
            pltpu.SemaphoreType.DMA((2,)),
            pltpu.SemaphoreType.DMA((5, 2)),
            pltpu.SemaphoreType.DMA((2, 2)),
        ],
        compiler_params=pltpu.CompilerParams(
            collective_id=1, has_side_effects=True, vmem_limit_bytes=64 * 1024 * 1024 - 65536
        ),
        name="finish",
    )(rows, up_first, down_first, up_second, down_second, dense, small, gains)


MASKED = -1e30
EPSILON = 1e-05


def split_three(value):
    high = value.astype(BF)
    rest = value - high.astype(F32)
    middle = rest.astype(BF)
    return high, middle, (rest - middle.astype(F32)).astype(BF)


def select_rows(marks, value, dims):
    return sum(dot(marks, term, dims) for term in split_three(value))


def norm_parts(stream):
    average = jnp.mean(stream, axis=-1, keepdims=True)
    centred = stream - average
    variance = jnp.mean(centred * centred, axis=-1, keepdims=True)
    scale = lax.rsqrt(variance + EPSILON)
    return centred * scale, scale


def norm_pull(grad, stream, gain):
    unit, scale = norm_parts(stream)
    inner = grad * gain
    mean_inner = jnp.mean(inner, axis=-1, keepdims=True)
    mean_product = jnp.mean(inner * unit, axis=-1, keepdims=True)
    return scale * (inner - mean_inner - unit * mean_product), jnp.sum(grad * unit, axis=0, keepdims=True)


def route_marks(routes_row, experts, slots):
    count = routes_row.shape[1]
    ids = lax.broadcasted_iota(jnp.int32, (experts, count), 0)
    chosen = (ids == routes_row).astype(F32)
    earlier = lax.broadcasted_iota(jnp.int32, (count, count), 0) <= lax.broadcasted_iota(jnp.int32, (count, count), 1)
    running = dot(chosen.astype(BF), earlier.astype(F32).astype(BF))
    rank = jnp.sum(running * chosen, axis=0, keepdims=True) - 1.0
    place = routes_row * slots + rank.astype(jnp.int32)
    rows = lax.broadcasted_iota(jnp.int32, (experts * slots, count), 0)
    return chosen.astype(BF), (rows == place).astype(F32).astype(BF)


def allowed_pairs(ends, docs, count):
    row = lax.broadcasted_iota(jnp.int32, (count, count), 0)
    col = lax.broadcasted_iota(jnp.int32, (count, count), 1)
    row_segment = jnp.zeros((count, count), jnp.int32)
    col_segment = jnp.zeros((count, count), jnp.int32)
    for d in range(docs):
        row_segment += (row >= ends[0, d]).astype(jnp.int32)
        col_segment += (col >= ends[0, d]).astype(jnp.int32)
    return (row_segment == col_segment) & (col <= row)


def half_marks(half):
    lane = lax.broadcasted_iota(jnp.int32, (1, 128), 1)
    inside = (lane >= 64 * half) & (lane < 64 * half + 64)
    return inside.astype(F32).astype(BF)


def head_shares(query_pair, key_pair, allowed, half):
    raw = dot(query_pair * half_marks(half), key_pair, ((1,), (1,)))
    scores = jnp.where(allowed, raw * 0.125, MASKED)
    raised = jnp.exp(scores - jnp.max(scores, axis=-1, keepdims=True))
    return raised * (1.0 / jnp.sum(raised, axis=-1, keepdims=True))


def join_halves(first, second):
    lane = lax.broadcasted_iota(jnp.int32, first.shape, 1)
    return jnp.where(lane < 64, first, second)


def enter_kernel(
    experts, slots, docs,
    ends, routes, tokens, cotangent, gain, cents, w_query, w_key, w_value, w_output,
    normed, queries, keys, values, mixed, hidden, out_rows,
    w_held, sems,
):
    copies = [
        pltpu.make_async_copy(w, w_held.at[i], sems.at[i])
        for i, w in enumerate((w_query, w_key, w_value, w_output))
    ]
    for copy in copies:
        copy.start()
    count, wide = tokens.shape
    unit, _ = norm_parts(tokens[...].astype(F32))
    normed[...] = (unit * gain[...]).astype(BF)
    for i, result in enumerate((queries, keys, values)):
        copies[i].wait()
        result[...] = dot(normed[...], w_held[i]).astype(BF)
    allowed = allowed_pairs(ends, docs, count)

    def one_pair(j, carry):
        cols = pl.ds(pl.multiple_of(j * 128, 128), 128)
        query_pair, key_pair, value_pair = queries[:, cols], keys[:, cols], values[:, cols]
        halves = [
            dot(head_shares(query_pair, key_pair, allowed, half).astype(BF), value_pair) for half in range(2)
        ]
        mixed[:, cols] = join_halves(*halves).astype(BF)
        return carry

    lax.fori_loop(0, wide // 128, one_pair, 0)
    copies[3].wait()
    hidden[...] = tokens[...].astype(F32) + dot(mixed[...], w_held[3])
    chosen, dispatch = route_marks(routes[...], experts, slots)
    own = select_rows(chosen, cents[...], ((0,), (0,)))
    gating = jax.nn.sigmoid(jnp.sum(hidden[...] * own, axis=-1, keepdims=True))
    live = (lax.broadcasted_iota(jnp.int32, (count, 1), 0) < ends[0, docs - 1]).astype(F32)
    grad_sent = (gating * (live * cotangent[...].astype(F32))).astype(BF)
    out_rows[0] = dot(dispatch, hidden[...].astype(BF)).astype(BF)
    out_rows[1] = dot(dispatch, grad_sent).astype(BF)


def enter(ends, routes_row, tokens, cotangent, gain, cents, weights, slots):
    count, wide = tokens.shape
    experts, docs = cents.shape[0], ends.shape[1]
    vmem = pl.BlockSpec(memory_space=pltpu.VMEM)
    anys = pl.BlockSpec(memory_space=pl.ANY)
    low = jax.ShapeDtypeStruct((count, wide), BF)
    return pl.pallas_call(
        functools.partial(enter_kernel, experts, slots, docs),
        out_shape=(low,) * 5 + (
            jax.ShapeDtypeStruct((count, wide), F32),
            jax.ShapeDtypeStruct((2, experts * slots, wide), BF),
        ),
        in_specs=[pl.BlockSpec(memory_space=pltpu.SMEM)] + [vmem] * 5 + [anys] * 4,
        out_specs=(vmem,) * 7,
        scratch_shapes=[pltpu.VMEM((4, wide, wide), BF), pltpu.SemaphoreType.DMA((4,))],
        compiler_params=pltpu.CompilerParams(vmem_limit_bytes=48 * 1024 * 1024),
        name="enter",
    )(ends, routes_row, tokens, cotangent, gain, cents, *weights)


def leave_kernel(
    experts, slots, docs, grid_like,
    ends, routes, tokens, cotangent, gain, cents, normed, queries, keys, values, mixed, hidden, came,
    w_query, w_key, w_value, w_output,
    block_out, grad_tokens, dense, small,
    w_held, grad_low, grad_three, normed_turned, grad_hidden, sems,
):
    copies = [
        pltpu.make_async_copy(w, w_held.at[i], sems.at[i])
        for i, w in enumerate((w_query, w_key, w_value, w_output))
    ]
    for i in (3, 0, 1, 2):
        copies[i].start()
    count, wide = tokens.shape
    chosen, dispatch = route_marks(routes[...], experts, slots)
    own = select_rows(chosen, cents[...], ((0,), (0,)))
    gating = jax.nn.sigmoid(jnp.sum(hidden[...] * own, axis=-1, keepdims=True))
    live = (lax.broadcasted_iota(jnp.int32, (count, 1), 0) < ends[0, docs - 1]).astype(F32)
    returned = dot(dispatch, came[0], ((0,), (0,)))
    block_out[...] = (live * (gating * returned + (1.0 - gating) * hidden[...])).astype(BF)
    grad_block = live * cotangent[...].astype(F32)
    grad_score = jnp.sum(grad_block * (returned - hidden[...]), axis=-1, keepdims=True) * gating * (1.0 - gating)
    grad_hidden[...] = (1.0 - gating) * grad_block + dot(dispatch, came[1], ((0,), (0,))) + grad_score * own
    small[pl.ds(8, experts), :] = select_rows(chosen, grad_score * hidden[...], ((1,), (0,)))
    grad_low[...] = grad_hidden[...].astype(BF)
    copies[3].wait()
    grad_mixed = dot(grad_low[...], w_held[3], ((1,), (1,))).astype(BF)
    dense_product(grid_like, dense, 3, mixed[...].T, grad_low)
    grad_low[...] = grad_mixed
    allowed = allowed_pairs(ends, docs, count)

    def one_pair(j, carry):
        cols = pl.ds(pl.multiple_of(j * 128, 128), 128)
        query_pair, key_pair, value_pair = queries[:, cols], keys[:, cols], values[:, cols]
        grad_pair = grad_low[:, cols]
        parts = []
        for half in range(2):
            shares = head_shares(query_pair, key_pair, allowed, half)
            grad_shares = dot(grad_pair * half_marks(half), value_pair, ((1,), (1,)))
            inner = jnp.sum(shares * grad_shares, axis=-1, keepdims=True)
            raw = (shares * (grad_shares - inner) * 0.125).astype(BF)
            parts.append((
                dot(raw, key_pair),
                dot(raw, query_pair, ((0,), (0,))),
                dot(shares.astype(BF), grad_pair, ((0,), (0,))),
            ))
        for i in range(3):
            grad_three[i, :, cols] = join_halves(parts[0][i], parts[1][i]).astype(BF)
        return carry

    lax.fori_loop(0, wide // 128, one_pair, 0)
    normed_turned[...] = normed[...].T
    for i in range(3):
        dense_product(grid_like, dense, i, normed_turned[...], grad_three.at[i])
    for i in range(3):
        copies[i].wait()
    grad_normed = sum(dot(grad_three[i], w_held[i], ((1,), (1,))) for i in range(3))
    pulled, grad_gain = norm_pull(grad_normed, tokens[...].astype(F32), gain[...])
    grad_tokens[...] = grad_hidden[...] + pulled
    small[pl.ds(0, 8), :] = jnp.broadcast_to(grad_gain, (8, wide))


def dense_product(grid_like, dense, which, turned, right):
    wide = turned.shape[0]
    if not grid_like:
        dense[which] = dot(turned, right[...]).astype(BF)
        return
    block = wide // 32
    for g in range(4):
        product = dot(turned[g * 8 * block:(g + 1) * 8 * block], right[...]).astype(BF)
        for e in range(8):
            dense[e % 2, which, (e // 2) % 2, e // 4, g] = product[e * block:(e + 1) * block]


def leave(ends, routes_row, tokens, cotangent, gain, cents, kept, came, weights, slots, grid_like):
    count, wide = tokens.shape
    experts, docs = cents.shape[0], ends.shape[1]
    vmem = pl.BlockSpec(memory_space=pltpu.VMEM)
    anys = pl.BlockSpec(memory_space=pl.ANY)
    dense_shape = (2, 4, 2, 2, 4, wide // 32, wide) if grid_like else (4, wide, wide)
    return pl.pallas_call(
        functools.partial(leave_kernel, experts, slots, docs, grid_like),
        out_shape=(
            jax.ShapeDtypeStruct((count, wide), BF),
            jax.ShapeDtypeStruct((count, wide), F32),
            jax.ShapeDtypeStruct(dense_shape, BF),
            jax.ShapeDtypeStruct((8 + experts, wide), F32),
        ),
        in_specs=[pl.BlockSpec(memory_space=pltpu.SMEM)] + [vmem] * 12 + [anys] * 4,
        out_specs=(vmem,) * 4,
        scratch_shapes=[
            pltpu.VMEM((4, wide, wide), BF),
            pltpu.VMEM((count, wide), BF),
            pltpu.VMEM((3, count, wide), BF),
            pltpu.VMEM((wide, count), BF),
            pltpu.VMEM((count, wide), F32),
            pltpu.SemaphoreType.DMA((4,)),
        ],
        compiler_params=pltpu.CompilerParams(vmem_limit_bytes=56 * 1024 * 1024),
        name="leave",
    )(ends, routes_row, tokens, cotangent, gain, cents, *kept, came, *weights)


def pack_marks(experts, slots, capacity):
    shape = (experts * capacity, experts * slots)
    row = lax.broadcasted_iota(jnp.int32, (shape[0], 1), 0)
    block = sum((row >= s * capacity).astype(jnp.int32) for s in range(1, experts))
    column = lax.broadcasted_iota(jnp.int32, shape, 1)
    return (column == row + (slots - capacity) * block).astype(F32).astype(BF)


def chain_kernel(
    experts, slots, capacity, tiles,
    came, up_first, down_first, up_second, down_second, gain_first, gain_second,
    back, rows, gains,
    up_tile, down_tile, pre, stream, total, sems,
):
    tile = up_tile.shape[2]
    ups, downs = (up_first, up_second), (down_first, down_second)
    gain_refs = (gain_first, gain_second)

    def fetch(s, c, slot):
        cols = pl.ds(pl.multiple_of(c * tile, tile), tile)
        return (
            pltpu.make_async_copy(ups[s].at[0, :, cols], up_tile.at[slot], sems.at[0, slot]),
            pltpu.make_async_copy(downs[s].at[0, cols, :], down_tile.at[slot], sems.at[1, slot]),
        )

    order = ((0, True), (1, True), (1, False), (0, False))

    def run(phase, body):
        s = order[phase][0]

        def step(c, carry):
            slot = lax.rem(c, 2)
            for copy in fetch(s, c, slot):
                copy.wait()

            @pl.when(c + 1 < tiles)
            def _():
                for copy in fetch(s, c + 1, 1 - slot):
                    copy.start()

            if phase < 3:
                @pl.when(c + 1 == tiles)
                def _():
                    for copy in fetch(order[phase + 1][0], 0, 1 - slot):
                        copy.start()

            body(s, pl.ds(pl.multiple_of(c * tile, tile), tile), slot)
            return carry

        lax.fori_loop(0, tiles, step, 0)

    for copy in fetch(0, 0, 0):
        copy.start()
    gains[...] = jnp.zeros_like(gains)
    packing = pack_marks(experts, slots, capacity)
    stream[0] = dot(packing, came[0])
    rows[1, 1] = dot(packing, came[1]).astype(BF)

    def forward(s, cols, slot):
        made = dot(rows[0, s], up_tile[slot])
        pre[s, :, cols] = made
        mid = gelu_pair(made)[0].astype(BF)
        total[...] += dot(mid, down_tile[slot])

    def backward(s, cols, slot):
        grad_mid = dot(rows[1, s], down_tile[slot], ((1,), (1,)))
        grad_pre = (gelu_pair(pre[s, :, cols])[1] * grad_mid).astype(BF)
        total[...] += dot(grad_pre, up_tile[slot], ((1,), (1,)))

    for s in range(2):
        unit, _ = norm_parts(stream[s])
        rows[0, s] = (unit * gain_refs[s][...]).astype(BF)
        total[...] = stream[s]
        run(s, forward)
        if s == 0:
            stream[1] = total[...]
    back[0] = dot(packing, total[...].astype(BF), ((0,), (0,))).astype(BF)

    for phase, s in ((2, 1), (3, 0)):
        total[...] = jnp.zeros_like(total)
        run(phase, backward)
        pulled, grad_gain = norm_pull(total[...], stream[s], gain_refs[s][...])
        gains[pl.ds(s, 1), :] = grad_gain
        if s == 1:
            grad_stream = rows[1, 1].astype(F32) + pulled
            stream[1] = grad_stream
            rows[1, 0] = grad_stream.astype(BF)
        else:
            grad_rows = (stream[1] + pulled).astype(BF)
            back[1] = dot(packing, grad_rows, ((0,), (0,))).astype(BF)


def chain(came, up_first, down_first, up_second, down_second, gain_first, gain_second, slots, capacity):
    wide, hidden = up_first.shape[1:]
    experts = came.shape[1] // slots
    count = experts * capacity
    tile = 512
    vmem = pl.BlockSpec(memory_space=pltpu.VMEM)
    anys = pl.BlockSpec(memory_space=pl.ANY)
    return pl.pallas_call(
        functools.partial(chain_kernel, experts, slots, capacity, hidden // tile),
        out_shape=(
            jax.ShapeDtypeStruct(came.shape, BF),
            jax.ShapeDtypeStruct((2, 2, count, wide), BF),
            jax.ShapeDtypeStruct((8, wide), F32),
        ),
        in_specs=[vmem] + [anys] * 4 + [vmem] * 2,
        out_specs=(vmem,) * 3,
        scratch_shapes=[
            pltpu.VMEM((2, wide, tile), BF),
            pltpu.VMEM((2, tile, wide), BF),
            pltpu.VMEM((2, count, hidden), F32),
            pltpu.VMEM((2, count, wide), F32),
            pltpu.VMEM((count, wide), F32),
            pltpu.SemaphoreType.DMA((2, 2)),
        ],
        compiler_params=pltpu.CompilerParams(vmem_limit_bytes=56 * 1024 * 1024),
        name="chain",
    )(came, up_first, down_first, up_second, down_second, gain_first, gain_second)


def ring_rows(rows, axis):
    count = lax.axis_size(axis)
    back = [(i, (i - 1) % count) for i in range(count)]
    held = [rows]
    for _ in range(count - 1):
        held.append(lax.ppermute(held[-1], axis, back))
    return jnp.concatenate(held, axis=0)


def weight_grads(normed_rows, grad_rows, up_proj, down_proj):
    count = lax.axis_size("batch")
    width = up_proj.shape[1] // count
    first = lax.axis_index("batch") * width
    up_part = lax.dynamic_slice_in_dim(up_proj, first, width, 1)
    down_part = lax.dynamic_slice_in_dim(down_proj, first, width, 0)
    pre_act = jnp.dot(normed_rows, up_part, preferred_element_type=jnp.float32)
    middle, gelu_pull = jax.vjp(jax.nn.gelu, pre_act)
    grad_middle = jnp.einsum("rd,fd->rf", grad_rows, down_part, preferred_element_type=jnp.float32)
    grad_pre = gelu_pull(grad_middle)[0].astype(jnp.bfloat16)
    grad_down = jnp.einsum(
        "rf,rd->fd", middle.astype(jnp.bfloat16), grad_rows, preferred_element_type=jnp.float32
    )
    grad_up = jnp.einsum("rd,rf->df", normed_rows, grad_pre, preferred_element_type=jnp.float32)
    return grad_up, grad_down


def halve(blocks, axis, bit, dim):
    count = lax.axis_size(axis)
    mine = (lax.axis_index(axis) // bit) % 2
    kept = lax.dynamic_index_in_dim(blocks, mine, dim, keepdims=False)
    sent = lax.dynamic_index_in_dim(blocks, 1 - mine, dim, keepdims=False)
    got = lax.ppermute(sent, axis, [(i, i ^ bit) for i in range(count)])
    return (kept.astype(jnp.float32) + got.astype(jnp.float32)).astype(blocks.dtype)


def scatter_sum(parts):
    experts, groups = lax.axis_size("expert"), lax.axis_size("batch")
    kinds, rows, width = parts.shape
    bits_e = experts.bit_length() - 1
    bits_b = groups.bit_length() - 1
    shape = (kinds,) + (2,) * (bits_b + bits_e) + (rows // (experts * groups), width)
    blocks = parts.reshape(shape)
    for k in range(bits_e):
        blocks = halve(blocks, "expert", 1 << k, bits_b + bits_e - k)
    for k in range(bits_b):
        blocks = halve(blocks, "batch", 1 << k, bits_b - k)
    return blocks


def all_sum(value):
    for axis in ("expert", "batch"):
        count = lax.axis_size(axis)
        bit = 1
        while bit < count:
            value = value + lax.ppermute(value, axis, [(i, i ^ bit) for i in range(count)])
            bit *= 2
    return value


def per_device(
    tokens, doc_ends, routes, w_query, w_key, w_value, w_output, attn_gain, centroids,
    up_first, down_first, gain_first, up_second, down_second, gain_second, cotangent,
):
    count, wide = tokens.shape
    experts, groups = lax.axis_size("expert"), lax.axis_size("batch")
    capacity = 11 * count // (8 * experts)
    slots = -(-capacity // 16) * 16
    fits = groups == 4 and experts == 8
    routes_row = routes.reshape(1, count)
    gain = attn_gain[None]
    weights = (w_query, w_key, w_value, w_output)
    *kept, out_rows = enter(doc_ends, routes_row, tokens, cotangent, gain, centroids, weights, slots)

    def exchange(rows):
        blocks = rows.reshape(2, experts, slots, wide)
        return lax.all_to_all(blocks, "expert", split_axis=1, concat_axis=1, tiled=True).reshape(rows.shape)

    back, rows, gains = chain(
        exchange(out_rows), up_first, down_first, up_second, down_second, gain_first, gain_second, slots, capacity
    )
    block_out, grad_tokens, dense, small = leave(
        doc_ends, routes_row, tokens, cotangent, gain, centroids, kept, exchange(back), weights, slots, fits
    )
    if fits:
        *parts, dense, small, gains = finish(
            rows, up_first, down_first, up_second, down_second, dense, small, gains
        )
        gains = gains[:2]
    else:
        dense = scatter_sum(dense).astype(F32)
        small = all_sum(small)
        parts = []
        for s, (up, down) in enumerate(((up_first, down_first), (up_second, down_second))):
            for part in weight_grads(ring_rows(rows[0, s], "batch"), ring_rows(rows[1, s], "batch"), up[0], down[0]):
                parts.append(part[None])
        gains = jnp.sum(lax.all_gather(gains[:2], "batch"), axis=0)
    gain_part = wide // groups
    gains = lax.dynamic_slice_in_dim(gains, lax.axis_index("batch") * gain_part, gain_part, 1)
    return (
        block_out, grad_tokens, dense[0], dense[1], dense[2], dense[3], small[0], small[8:],
        parts[0], parts[1], gains[0:1], parts[2], parts[3], gains[1:2],
    )


def solution(mesh):
    return jax.shard_map(
        per_device,
        mesh=mesh,
        in_specs=(
            P(("batch", "expert"), None),
            P(("batch", "expert"), None),
            P(("batch", "expert"), None),
            P(),
            P(),
            P(),
            P(),
            P(),
            P(),
            P("expert", None, None),
            P("expert", None, None),
            P("expert", None),
            P("expert", None, None),
            P("expert", None, None),
            P("expert", None),
            P(("batch", "expert"), None),
        ),
        out_specs=(
            P(("batch", "expert"), None),
            P(("batch", "expert"), None),
            P(("batch", "expert"), None),
            P(("batch", "expert"), None),
            P(("batch", "expert"), None),
            P(("batch", "expert"), None),
            P(),
            P(),
            P("expert", None, "batch"),
            P("expert", "batch", None),
            P("expert", "batch"),
            P("expert", None, "batch"),
            P("expert", "batch", None),
            P("expert", "batch"),
        ),
        check_vma=False,
    )
```

time: 480 us -> 420 us (0.88); the launches traced: 474 us -> 419 us
  matrix products: 103 us -> 0 us
  Pallas kernels: 242 us -> 336 us
  other arithmetic: 34.9 us -> 0 us
  starting transfers between devices: 15.9 us -> 4.95 us
  blocking collectives: 15.3 us -> 23.6 us
  local copies, waits for them, and re-layouts: 39.3 us -> 33.3 us
    dot_general x27 -> x0, matrix products: 103 us -> none  [the longest x2 30.5 us: sublayer_backward(): jnp.einsum('rf,df->rd', grad_pre, up_proj, preferred_element_type=jnp.flo...]
    pallas_call x0 -> x3, Pallas kernels: none -> 94.4 us  [the longest x1 55.8 us: chain(): pl.pallas_call(functools.partial(chain_kernel, experts, slots, capacity,...]
    unnamed x54 -> x34, local copies, waits for them, and re-layouts: 5.94 us -> 19.2 us
    slice x4 -> x2, local copies, waits for them, and re-layouts: 14.7 us -> 2.13 us  [the longest x1 1.37 us: per_device(): small[8:]]
    reduce_sum x12 -> x0, other arithmetic: 12 us -> none  [the longest x2 5.62 us: layer_norm(): centred = stream - average]
    all_to_all x3 -> x1, starting transfers between devices: 15.9 us -> 4.95 us  [exchange(): lax.all_to_all(blocks, 'expert', split_axis=1, concat_axis=1, tiled=True)]
    all_to_all x1, blocking collectives: 15.3 us -> 23.6 us  [exchange(): lax.all_to_all(blocks, 'expert', split_axis=1, concat_axis=1, tiled=True)]
    convert_element_type x7 -> x0, other arithmetic: 7.53 us -> none  [the longest x2 2.78 us: sublayer_forward(): normed = layer_norm(stream, gain_vec).astype(jnp.bfloat16)]
  transfers between devices with their start and end apart: 3 -> 1, of which waited for: 3 -> 1; matrix products, arithmetic and copies ran while one was open for 3% -> 0% of each run, Pallas kernels for 0% -> 0%
where the time goes in v3:
time: 420 us; the launch traced here: 419 us
  Pallas kernels  336 us (80%)
  local copies, waits for them, and re-layouts  33.3 us (8%)
  blocking collectives  23.6 us (6%)
  waiting for transfers between devices  19.5 us (5%)
  starting transfers between devices  4.95 us (1%)
    pallas_call x1, Pallas kernels, finish(): pl.pallas_call(functools.partial(finish_kernel, groups, width), out_shape...  242 us
    pallas_call x1, Pallas kernels, chain(): pl.pallas_call(functools.partial(chain_kernel, experts, slots, capacity,...  55.8 us
    pallas_call x1, Pallas kernels, leave(): pl.pallas_call(functools.partial(leave_kernel, experts, slots, docs, grid...  24.1 us
    all_to_all x1, blocking collectives, exchange(): lax.all_to_all(blocks, 'expert', split_axis=1, concat_axis=1, tiled=True)  23.6 us
    all_to_all x1, waiting for transfers between devices, exchange(): lax.all_to_all(blocks, 'expert', split_axis=1, concat_axis=1, tiled=True)  19.5 us
    unnamed x34, local copies, waits for them, and re-layouts  19.2 us
    pallas_call x1, Pallas kernels, enter(): pl.pallas_call(functools.partial(enter_kernel, experts, slots, docs), out...  14.5 us
  transfers between devices with their start and end apart: 1, of which 1 were waited for; matrix products, arithmetic and copies ran while one was open for 0% of the time, Pallas kernels for 0%

profile of v3, /device:TPU:26, one launch (start us, length us, event | category | flops | bytes accessed | tf_op | source)
XLA Modules:
  0.0 418.6 jit_solution(12653768346510147086)
XLA Ops:
  0.6 0.0 copy-start
  0.7 1.0 copy-done
  1.7 0.0 copy-start.1
  1.7 1.0 copy-done.1
  2.7 0.0 copy-start.8
  2.7 0.8 copy-done.8
  3.5 0.0 copy-start.9
  3.5 0.7 copy-done.9
  4.2 0.0 copy-start.10
  4.2 0.7 copy-done.10
  4.9 0.0 copy-start.11
  4.9 0.7 copy-done.11
  5.5 14.5 %enter.1 = (bf16[256,1024]{1,0:T(8,128)(2,1)S(1)}, bf16[256,1024]{1,0:T(8,128)(2,1)S(1)}, bf16[256,1024]{1,0:T(8,128)(2,1)S(1)}, bf16[256,1024]{1,0:T(8,128)(2,1...) custom-call(s32[1,4]{1,0:T(1,128)S(1)} %copy-done.11, ...), custom_call_target="tpu_custom_call" | custom-call | tf_op jit(solution)/shard_map/enter/pallas_call | solution.py:404
  20.0 0.0 copy-start.2
  20.1 0.0 copy-start.3
  20.1 0.0 copy-start.4
  20.1 0.0 copy-start.5
  20.1 0.0 copy-start.6
  20.1 0.0 copy-start.7
  20.1 2.7 copy.30
  22.8 23.6 %all_to_all.10 = bf16[2,8,48,1024]{3,2,0,1:T(8,128)(2,1)S(1)} all-to-all(bf16[2,8,48,1024]{3,2,0,1:T(8,128)(2,1)S(1)} %copy.30), channel_id=1, replica_groups=mesh['batch'=4,'expert'=8] {'expert'}, dimensions={1} | all-to-all | bytes 3145728 | tf_op jit(solution)/shard_map/all_to_all | solution.py:717
  46.4 1.3 copy.31
  47.7 0.0 copy-done.2
  47.7 0.0 copy-done.3
  47.7 0.0 copy-done.4
  47.7 0.0 copy-done.5
  47.7 0.0 copy-done.6
  47.7 0.0 copy-done.7
  47.8 55.8 %chain.1 = (bf16[2,384,1024]{2,1,0:T(8,128)(2,1)}, bf16[2,2,352,1024]{3,2,1,0:T(8,128)(2,1)}, f32[8,1024]{1,0:T(8,128)}) custom-call(bf16[2,384,1024]{2,1,0:T(8,128)(2,1)} %bitcast.19, bf16[1,1024,4096]{2,1,0:T(8,128)(2,1)} %up_first.3, bf16[1,4096,1024]{2,1,0:T(8,128)(2,1)} %down_first.3, bf16[1,1024,4096]{2,1,0:T(8,128)(2,1)} %up_second.3, ...), custom_call_target="tpu_custom_call" | custom-call | tf_op jit(solution)/shard_map/chain/pallas_call | solution.py:620
  103.5 2.7 copy.32
  106.3 5.0 %all-to-all-start.1 = ((bf16[2,8,48,1024]{3,2,0,1:T(8,128)(2,1)}), bf16[2,8,48,1024]{3,2,0,1:T(8,128)(2,1)S(1)}, u32[]{:S(2)}, u32[]{:S(2)}) async-start(bf16[2,8,48,1024]{3,2,0,1:T(8,128)(2,1)} %copy.32), calls=%async_computation.1 | async-start | bytes 3145728 | tf_op jit(solution)/shard_map/all_to_all | solution.py:717
  111.2 19.5 %all-to-all-done.1 = bf16[2,8,48,1024]{3,2,0,1:T(8,128)(2,1)S(1)} async-done(((bf16[2,8,48,1024]{3,2,0,1:T(8,128)(2,1)}), bf16[2,8,48,1024]{3,2,0,1:T(8,128)(2,1)S(1)}, u32[]{:S(2)}, u32[]{:S(2)}) %all-to-all-start.1) | async-done | bytes 1572896 | tf_op jit(solution)/shard_map/all_to_all | solution.py:717
  130.8 1.3 copy.33
  132.1 24.1 %leave.1 = (bf16[256,1024]{1,0:T(8,128)(2,1)}, f32[256,1024]{1,0:T(8,128)}, bf16[2,4,2,2,4,32,1024]{6,5,4,3,2,1,0:T(8,128)(2,1)}, f32[16,1024]{1,0:T(8,128)}) custom-call(s32[1,4]{1,0:T(1,128)} %ends.3, s32[1,256]{1,0:T(1,128)} %bitcast.17, bf16[256,1024]{1,0:T(8,128)(2,1)} %tokens.3, bf16[256,1024]{1,0:T(8,128)(2,1)} %cotangent.3, f32[1,1024]{1,0:T(1,128)} %bitcast.15, ...), custom_call_target="tpu_custom_call" | custom-call | tf_op jit(solution)/shard_map/leave/pallas_call | solution.py:498
  156.2 242.0 %finish.1 = (f32[1,1024,1024]{2,1,0:T(8,128)}, f32[1,1024,1024]{2,1,0:T(8,128)}, f32[1,1024,1024]{2,1,0:T(8,128)}, f32[1,1024,1024]{2,1,0:T(8,128)}, f32[4,32,10...) custom-call(bf16[2,2,352,1024]{3,2,1,0:T(8,128)(2,1)} %get-tuple-element.45.rows_in, ...), custom_call_target="tpu_custom_call" | custom-call | tf_op jit(solution)/shard_map/finish/pallas_call | solution.py:238
  398.2 1.4 slice.31
  399.6 1.4 slice.32
  400.9 1.9 slice_bitcast_fusion
  402.8 0.8 slice.33
  403.6 0.6 fusion
  404.2 0.0 copy-start.14
  404.2 4.9 %copy.38 = f32[1,1024,1024]{2,1,0:T(8,128)} copy(f32[1,1024,1024]{2,1,0:T(8,128)} %get-tuple-element.84) | data formatting | bytes 8388608
  409.2 0.0 copy-done.14
  409.2 0.0 copy-start.13
  409.2 2.1 copy.39
  411.3 1.6 copy-done.13
  412.9 0.0 copy-start.12
  412.9 2.1 copy.40
  415.0 1.6 copy-done.12
  416.6 2.0 copy.41
Async XLA Ops:
  0.6 1.0 copy-start
  1.7 1.0 copy-start.1
  2.7 0.8 copy-start.8
  3.5 0.7 copy-start.9
  4.2 0.7 copy-start.10
  4.9 0.7 copy-start.11
  20.0 27.7 %copy-start.2 = (f32[256,1024]{1,0:T(8,128)}, f32[256,1024]{1,0:T(8,128)S(1)}, u32[]{:S(2)}) copy-start(f32[256,1024]{1,0:T(8,128)S(1)} %get-tuple-element.40.hidden) | copy-start | bytes 3145732
  20.1 27.7 %copy-start.3 = (bf16[256,1024]{1,0:T(8,128)(2,1)}, bf16[256,1024]{1,0:T(8,128)(2,1)S(1)}, u32[]{:S(2)}) copy-start(bf16[256,1024]{1,0:T(8,128)(2,1)S(1)} %get-tuple-element.35.normed) | copy-start | bytes 1572868
  20.1 27.7 %copy-start.4 = (bf16[256,1024]{1,0:T(8,128)(2,1)}, bf16[256,1024]{1,0:T(8,128)(2,1)S(1)}, u32[]{:S(2)}) copy-start(bf16[256,1024]{1,0:T(8,128)(2,1)S(1)} %get-tuple-element.36.queries) | copy-start | bytes 1572868
  20.1 27.7 %copy-start.5 = (bf16[256,1024]{1,0:T(8,128)(2,1)}, bf16[256,1024]{1,0:T(8,128)(2,1)S(1)}, u32[]{:S(2)}) copy-start(bf16[256,1024]{1,0:T(8,128)(2,1)S(1)} %get-tuple-element.37.keys) | copy-start | bytes 1572868
  20.1 27.7 %copy-start.6 = (bf16[256,1024]{1,0:T(8,128)(2,1)}, bf16[256,1024]{1,0:T(8,128)(2,1)S(1)}, u32[]{:S(2)}) copy-start(bf16[256,1024]{1,0:T(8,128)(2,1)S(1)} %get-tuple-element.38.values) | copy-start | bytes 1572868
  20.1 27.7 %copy-start.7 = (bf16[256,1024]{1,0:T(8,128)(2,1)}, bf16[256,1024]{1,0:T(8,128)(2,1)S(1)}, u32[]{:S(2)}) copy-start(bf16[256,1024]{1,0:T(8,128)(2,1)S(1)} %get-tuple-element.39.mixed) | copy-start | bytes 1572868
  106.3 24.5 %all-to-all-start.1 = ((bf16[2,8,48,1024]{3,2,0,1:T(8,128)(2,1)}), bf16[2,8,48,1024]{3,2,0,1:T(8,128)(2,1)S(1)}, u32[]{:S(2)}, u32[]{:S(2)}) async-start(bf16[2,8,48,1024]{3,2,0,1:T(8,128)(2,1)} %copy.32), calls=%async_computation.1 | async-start | bytes 3145728 | tf_op jit(solution)/shard_map/all_to_all | solution.py:717
  404.2 4.9 %copy-start.14 = (f32[1,1024,1024]{2,1,0:T(8,128)S(1)}, f32[1,1024,1024]{2,1,0:T(8,128)}, u32[]{:S(2)}) copy-start(f32[1,1024,1024]{2,1,0:T(8,128)} %get-tuple-element.85) | copy-start | bytes 12582916
  409.2 3.7 copy-start.13
  412.9 3.7 copy-start.12

commit v4 on v3

--- a/solution.py
+++ b/solution.py
@@ -23,263 +23,6 @@
 
 def dot(a, b, dims=((1,), (0,))):
     return lax.dot_general(a, b, (dims, ((), ())), preferred_element_type=F32)
-
-
-def finish_kernel(
-    groups, width,
-    rows_in, up_first, down_first, up_second, down_second, dense_in, small_in, gains_in,
-    up_one, down_one, up_two, down_two, dense_out, small_out, gains_out,
-    rows, ups, downs, up_acc, down_acc, turned, part, d_one, d_two, d_three, d_four, d_five, keep, s_got, g_got,
-    ring_send, ring_recv, dense_send, dense_recv, small_send, small_recv, gain_send, gain_recv, local_sem, out_sem,
-):
-    b, e = lax.axis_index("batch"), lax.axis_index("expert")
-    steps = 2 * groups
-    before = lax.rem(b + groups - 1, groups)
-    after = lax.rem(b + 1, groups)
-    core, x, y = lax.rem(e, 2), lax.rem(e // 2, 2), lax.rem(e // 4, 2)
-    b0, b1 = lax.rem(b, 2), lax.rem(b // 2, 2)
-    e_core = e + 1 - 2 * core
-    e_x = e + 2 - 4 * x
-    e_y = e + 4 - 8 * y
-    b_lo = b + 1 - 2 * b0
-    b_hi = b + 2 - 4 * b1
-    peers = [(b, e_core), (b, e_x), (b, e_y), (before, e), (after, e), (b_hi, e)]
-    barrier = pltpu.get_barrier_semaphore()
-    for peer in peers:
-        pl.semaphore_signal(barrier, inc=1, device_id=peer, device_id_type=MESH)
-
-    loads = []
-    col = pl.multiple_of(b * width, width)
-    for s, (up, down) in enumerate(((up_first, down_first), (up_second, down_second))):
-        loads.append(pltpu.make_async_copy(up.at[0, :, pl.ds(col, width)], ups.at[s], local_sem.at[0, s]))
-        loads.append(pltpu.make_async_copy(down.at[0, pl.ds(col, width), :], downs.at[s], local_sem.at[1, s]))
-    for s in range(2):
-        for kind in range(2):
-            loads.append(pltpu.make_async_copy(rows_in.at[kind, s], rows.at[kind, s, 0], local_sem.at[2 + kind, s]))
-    mine = pltpu.make_async_copy(dense_in.at[core], part, local_sem.at[4, 0])
-    for load in loads:
-        load.start()
-    mine.start()
-    pl.semaphore_wait(barrier, len(peers))
-
-    def remote(src, dst, send, recv, peer):
-        return pltpu.make_async_remote_copy(
-            src_ref=src, dst_ref=dst, send_sem=send, recv_sem=recv, device_id=peer, device_id_type=MESH
-        )
-
-    first_dense = remote(dense_in.at[1 - core], d_one, dense_send.at[0], dense_recv.at[0], (b, e_core))
-    first_dense.start()
-
-    def ring(kind, s, k):
-        return remote(
-            rows.at[kind, s, k - 1], rows.at[kind, s, k], ring_send.at[kind, s, k], ring_recv.at[kind, s, k], (before, e)
-        )
-
-    for s in (1, 0):
-        for kind in range(2):
-            pltpu.make_async_copy(rows_in.at[kind, s], rows.at[kind, s, 0], local_sem.at[2 + kind, s]).wait()
-            ring(kind, s, 1).start()
-    for s in range(2):
-        loads[2 * s].wait()
-        loads[2 * s + 1].wait()
-    up_acc[...] = jnp.zeros_like(up_acc)
-    down_acc[...] = jnp.zeros_like(down_acc)
-
-    def small_step(level, peer):
-        return remote(keep.at[level], s_got.at[level], small_send.at[level], small_recv.at[level], peer)
-
-    def gain_step(level, peer):
-        return remote(
-            keep.at[5 + level, pl.ds(0, 8)], g_got.at[level], gain_send.at[level], gain_recv.at[level], peer
-        )
-
-    def second(m):
-        if m < 2:
-            return remote(part.at[m, 1 - x], d_two.at[m], dense_send.at[1 + m], dense_recv.at[1 + m], (b, e_x))
-        return remote(part.at[m, :, 1 - y], d_two.at[m], dense_send.at[1 + m], dense_recv.at[1 + m], (b, e_y))
-
-    def third(m):
-        if m < 2:
-            return remote(part.at[m, x, 1 - y], d_three.at[m], dense_send.at[5 + m], dense_recv.at[5 + m], (b, e_y))
-        return remote(part.at[m, 1 - x, y], d_three.at[m], dense_send.at[5 + m], dense_recv.at[5 + m], (b, e_x))
-
-    fourth = remote(d_four.at[:, 1 - b0], d_four.at[:, 2], dense_send.at[9], dense_recv.at[9], (b_lo, e))
-    fifth = remote(d_five.at[:, 1 - b1], d_five.at[:, 2], dense_send.at[10], dense_recv.at[10], (b_hi, e))
-
-    keep[0] = small_in[...]
-    keep[5, pl.ds(0, 8)] = gains_in[...]
-    small_step(0, (b, e_core)).start()
-    gain_step(0, (b_lo, e)).start()
-
-    def results(s):
-        up_out, down_out = ((up_one, down_one), (up_two, down_two))[s]
-        return (
-            pltpu.make_async_copy(up_acc.at[s], up_out.at[0], out_sem.at[0, s]),
-            pltpu.make_async_copy(down_acc.at[s], down_out.at[0], out_sem.at[1, s]),
-        )
-
-    def weight_step(i, carry):
-        k, s = i // 2, 1 - lax.rem(i, 2)
-
-        @pl.when(k > 0)
-        def _():
-            for kind in range(2):
-                ring(kind, s, k).wait_recv()
-
-        @pl.when((k > 0) & (k < groups - 1))
-        def _():
-            for kind in range(2):
-                ring(kind, s, k + 1).start()
-
-        turned[...] = rows[0, s, k].T
-
-        def chunk(c, carry):
-            cols = pl.ds(pl.multiple_of(c * 256, 256), 256)
-            pre = dot(rows[0, s, k], ups[s, :, cols])
-            grad_mid = dot(rows[1, s, k], downs[s, cols, :], ((1,), (1,)))
-            mid, slope = gelu_pair(pre)
-            down_acc[s, cols, :] += dot(mid.astype(BF), rows[1, s, k], ((0,), (0,)))
-            up_acc[s, :, cols] += dot(turned[...], (grad_mid * slope).astype(BF))
-            return carry
-
-        lax.fori_loop(0, width // 256, chunk, 0)
-
-        @pl.when(i == 0)
-        def _():
-            mine.wait()
-            first_dense.wait()
-            small_step(0, (b, e_core)).wait()
-            gain_step(0, (b_lo, e)).wait()
-            keep[1] = keep[0] + s_got[0]
-            keep[6, pl.ds(0, 8)] = keep[5, pl.ds(0, 8)] + g_got[0]
-            small_step(1, (b, e_x)).start()
-            gain_step(1, (b_hi, e)).start()
-            for m in range(4):
-                for xx in range(2):
-                    part[m, xx] = (part[m, xx].astype(F32) + d_one[m, xx].astype(F32)).astype(BF)
-            for m in range(4):
-                second(m).start()
-
-        @pl.when(i == 2)
-        def _():
-            small_step(1, (b, e_x)).wait()
-            gain_step(1, (b_hi, e)).wait()
-            gains_out[...] = keep[6, pl.ds(0, 8)] + g_got[1]
-            keep[2] = keep[1] + s_got[1]
-            small_step(2, (b, e_y)).start()
-            for m in range(4):
-                second(m).wait()
-            for m in range(4):
-                if m < 2:
-                    part[m, x] = (part[m, x].astype(F32) + d_two[m].astype(F32)).astype(BF)
-                else:
-                    for xx in range(2):
-                        part[m, xx, y] = (part[m, xx, y].astype(F32) + d_two[m, xx].astype(F32)).astype(BF)
-            for m in range(4):
-                third(m).start()
-
-        @pl.when(i == 3)
-        def _():
-            small_step(2, (b, e_y)).wait()
-            keep[3] = keep[2] + s_got[2]
-            small_step(3, (b_lo, e)).start()
-            for m in range(4):
-                third(m).wait()
-            for m in range(4):
-                for g in range(4):
-                    d_four[m, g % 2, g // 2] = (part[m, x, y, g].astype(F32) + d_three[m, g].astype(F32)).astype(BF)
-            fourth.start()
-
-        @pl.when(i == 4)
-        def _():
-            small_step(3, (b_lo, e)).wait()
-            keep[4] = keep[3] + s_got[3]
-            small_step(4, (b_hi, e)).start()
-            fourth.wait()
-            for m in range(4):
-                for g in range(2):
-                    d_five[m, g] = (d_four[m, b0, g].astype(F32) + d_four[m, 2, g].astype(F32)).astype(BF)
-            fifth.start()
-
-        @pl.when(i == 5)
-        def _():
-            small_step(4, (b_hi, e)).wait()
-            small_out[...] = keep[4] + s_got[4]
-            fifth.wait()
-            for m in range(4):
-                dense_out[m] = d_five[m, b1].astype(F32) + d_five[m, 2].astype(F32)
-
-        @pl.when(i == steps - 2)
-        def _():
-            for copy in results(1):
-                copy.start()
-
-        return carry
-
-    lax.fori_loop(0, steps, weight_step, 0)
-    for s in range(2):
-        for kind in range(2):
-            for k in range(1, groups):
-                ring(kind, s, k).wait_send()
-    for copy in results(0):
-        copy.start()
-    for copy in results(1) + results(0):
-        copy.wait()
-
-
-def finish(rows, up_first, down_first, up_second, down_second, dense, small, gains):
-    groups = lax.axis_size("batch")
-    count, width_all = rows.shape[2], rows.shape[3]
-    width = up_first.shape[2] // groups
-    block = dense.shape[5]
-    any_spec = pl.BlockSpec(memory_space=pl.ANY)
-    vmem = pl.BlockSpec(memory_space=pltpu.VMEM)
-    wide = width_all
-    return pl.pallas_call(
-        functools.partial(finish_kernel, groups, width),
-        out_shape=(
-            jax.ShapeDtypeStruct((1, wide, width), F32),
-            jax.ShapeDtypeStruct((1, width, wide), F32),
-            jax.ShapeDtypeStruct((1, wide, width), F32),
-            jax.ShapeDtypeStruct((1, width, wide), F32),
-            jax.ShapeDtypeStruct((4, block, wide), F32),
-            jax.ShapeDtypeStruct(small.shape, F32),
-            jax.ShapeDtypeStruct(gains.shape, F32),
-        ),
-        in_specs=[any_spec] * 6 + [vmem] * 2,
-        out_specs=(any_spec,) * 4 + (vmem,) * 3,
-        scratch_shapes=[
-            pltpu.VMEM((2, 2, groups, count, wide), BF),
-            pltpu.VMEM((2, wide, width), BF),
-            pltpu.VMEM((2, width, wide), BF),
-            pltpu.VMEM((2, wide, width), F32),
-            pltpu.VMEM((2, width, wide), F32),
-            pltpu.VMEM((wide, count), BF),
-            pltpu.VMEM((4, 2, 2, 4, block, wide), BF),
-            pltpu.VMEM((4, 2, 2, 4, block, wide), BF),
-            pltpu.VMEM((4, 2, 4, block, wide), BF),
-            pltpu.VMEM((4, 4, block, wide), BF),
-            pltpu.VMEM((4, 3, 2, block, wide), BF),
-            pltpu.VMEM((4, 3, block, wide), BF),
-            pltpu.VMEM((7,) + small.shape, F32),
-            pltpu.VMEM((5,) + small.shape, F32),
-            pltpu.VMEM((2,) + gains.shape, F32),
-            pltpu.SemaphoreType.DMA((2, 2, groups)),
-            pltpu.SemaphoreType.DMA((2, 2, groups)),
-            pltpu.SemaphoreType.DMA((11,)),
-            pltpu.SemaphoreType.DMA((11,)),
-            pltpu.SemaphoreType.DMA((5,)),
-            pltpu.SemaphoreType.DMA((5,)),
-            pltpu.SemaphoreType.DMA((2,)),
-            pltpu.SemaphoreType.DMA((2,)),
-            pltpu.SemaphoreType.DMA((5, 2)),
-            pltpu.SemaphoreType.DMA((2, 2)),
-        ],
-        compiler_params=pltpu.CompilerParams(
-            collective_id=1, has_side_effects=True, vmem_limit_bytes=64 * 1024 * 1024 - 65536
-        ),
-        name="finish",
-    )(rows, up_first, down_first, up_second, down_second, dense, small, gains)
 
 
 MASKED = -1e30
@@ -391,8 +134,8 @@
     gating = jax.nn.sigmoid(jnp.sum(hidden[...] * own, axis=-1, keepdims=True))
     live = (lax.broadcasted_iota(jnp.int32, (count, 1), 0) < ends[0, docs - 1]).astype(F32)
     grad_sent = (gating * (live * cotangent[...].astype(F32))).astype(BF)
-    out_rows[0] = dot(dispatch, hidden[...].astype(BF)).astype(BF)
-    out_rows[1] = dot(dispatch, grad_sent).astype(BF)
+    for kind, rows in enumerate((hidden[...].astype(BF), grad_sent)):
+        out_rows[kind] = dot(dispatch, rows).astype(BF).reshape(experts, slots, wide)
 
 
 def enter(ends, routes_row, tokens, cotangent, gain, cents, weights, slots):
@@ -405,7 +148,7 @@
         functools.partial(enter_kernel, experts, slots, docs),
         out_shape=(low,) * 5 + (
             jax.ShapeDtypeStruct((count, wide), F32),
-            jax.ShapeDtypeStruct((2, experts * slots, wide), BF),
+            jax.ShapeDtypeStruct((2, experts, slots, wide), BF),
         ),
         in_specs=[pl.BlockSpec(memory_space=pltpu.SMEM)] + [vmem] * 5 + [anys] * 4,
         out_specs=(vmem,) * 7,
@@ -415,8 +158,28 @@
     )(ends, routes_row, tokens, cotangent, gain, cents, *weights)
 
 
+def backward_pair(allowed, queries, keys, values, grad_low, grad_three, j, carry):
+    cols = pl.ds(pl.multiple_of(j * 128, 128), 128)
+    query_pair, key_pair, value_pair = queries[:, cols], keys[:, cols], values[:, cols]
+    grad_pair = grad_low[:, cols]
+    parts = []
+    for half in range(2):
+        shares = head_shares(query_pair, key_pair, allowed, half)
+        grad_shares = dot(grad_pair * half_marks(half), value_pair, ((1,), (1,)))
+        inner = jnp.sum(shares * grad_shares, axis=-1, keepdims=True)
+        raw = (shares * (grad_shares - inner) * 0.125).astype(BF)
+        parts.append((
+            dot(raw, key_pair),
+            dot(raw, query_pair, ((0,), (0,))),
+            dot(shares.astype(BF), grad_pair, ((0,), (0,))),
+        ))
+    for i in range(3):
+        grad_three[i][:, cols] = join_halves(parts[0][i], parts[1][i]).astype(BF)
+    return carry
+
+
 def leave_kernel(
-    experts, slots, docs, grid_like,
+    experts, slots, docs,
     ends, routes, tokens, cotangent, gain, cents, normed, queries, keys, values, mixed, hidden, came,
     w_query, w_key, w_value, w_output,
     block_out, grad_tokens, dense, small,
@@ -442,33 +205,18 @@
     grad_low[...] = grad_hidden[...].astype(BF)
     copies[3].wait()
     grad_mixed = dot(grad_low[...], w_held[3], ((1,), (1,))).astype(BF)
-    dense_product(grid_like, dense, 3, mixed[...].T, grad_low)
+    dense[3] = dot(mixed[...].T, grad_low[...]).astype(BF)
     grad_low[...] = grad_mixed
     allowed = allowed_pairs(ends, docs, count)
 
-    def one_pair(j, carry):
-        cols = pl.ds(pl.multiple_of(j * 128, 128), 128)
-        query_pair, key_pair, value_pair = queries[:, cols], keys[:, cols], values[:, cols]
-        grad_pair = grad_low[:, cols]
-        parts = []
-        for half in range(2):
-            shares = head_shares(query_pair, key_pair, allowed, half)
-            grad_shares = dot(grad_pair * half_marks(half), value_pair, ((1,), (1,)))
-            inner = jnp.sum(shares * grad_shares, axis=-1, keepdims=True)
-            raw = (shares * (grad_shares - inner) * 0.125).astype(BF)
-            parts.append((
-                dot(raw, key_pair),
-                dot(raw, query_pair, ((0,), (0,))),
-                dot(shares.astype(BF), grad_pair, ((0,), (0,))),
-            ))
-        for i in range(3):
-            grad_three[i, :, cols] = join_halves(parts[0][i], parts[1][i]).astype(BF)
-        return carry
-
-    lax.fori_loop(0, wide // 128, one_pair, 0)
+    lax.fori_loop(
+        0, wide // 128, functools.partial(
+            backward_pair, allowed, queries, keys, values, grad_low, [grad_three.at[i] for i in range(3)]
+        ), 0
+    )
     normed_turned[...] = normed[...].T
     for i in range(3):
-        dense_product(grid_like, dense, i, normed_turned[...], grad_three.at[i])
+        dense[i] = dot(normed_turned[...], grad_three[i]).astype(BF)
     for i in range(3):
         copies[i].wait()
     grad_normed = sum(dot(grad_three[i], w_held[i], ((1,), (1,))) for i in range(3))
@@ -477,30 +225,17 @@
     small[pl.ds(0, 8), :] = jnp.broadcast_to(grad_gain, (8, wide))
 
 
-def dense_product(grid_like, dense, which, turned, right):
-    wide = turned.shape[0]
-    if not grid_like:
-        dense[which] = dot(turned, right[...]).astype(BF)
-        return
-    block = wide // 32
-    for g in range(4):
-        product = dot(turned[g * 8 * block:(g + 1) * 8 * block], right[...]).astype(BF)
-        for e in range(8):
-            dense[e % 2, which, (e // 2) % 2, e // 4, g] = product[e * block:(e + 1) * block]
-
-
-def leave(ends, routes_row, tokens, cotangent, gain, cents, kept, came, weights, slots, grid_like):
+def leave(ends, routes_row, tokens, cotangent, gain, cents, kept, came, weights, slots):
     count, wide = tokens.shape
     experts, docs = cents.shape[0], ends.shape[1]
     vmem = pl.BlockSpec(memory_space=pltpu.VMEM)
     anys = pl.BlockSpec(memory_space=pl.ANY)
-    dense_shape = (2, 4, 2, 2, 4, wide // 32, wide) if grid_like else (4, wide, wide)
     return pl.pallas_call(
-        functools.partial(leave_kernel, experts, slots, docs, grid_like),
+        functools.partial(leave_kernel, experts, slots, docs),
         out_shape=(
             jax.ShapeDtypeStruct((count, wide), BF),
             jax.ShapeDtypeStruct((count, wide), F32),
-            jax.ShapeDtypeStruct(dense_shape, BF),
+            jax.ShapeDtypeStruct((4, wide, wide), BF),
             jax.ShapeDtypeStruct((8 + experts, wide), F32),
         ),
         in_specs=[pl.BlockSpec(memory_space=pltpu.SMEM)] + [vmem] * 12 + [anys] * 4,
@@ -614,7 +349,7 @@
     wide, hidden = up_first.shape[1:]
     experts = came.shape[1] // slots
     count = experts * capacity
-    tile = 512
+    tile = 1024
     vmem = pl.BlockSpec(memory_space=pltpu.VMEM)
     anys = pl.BlockSpec(memory_space=pl.ANY)
     return pl.pallas_call(
@@ -698,6 +433,473 @@
     return value
 
 
+def layer_kernel(
+    experts, groups, slots, capacity, docs, width, tiles,
+    ends, routes, tokens, cotangent, gain, cents, normed, queries, keys, values, mixed, hidden, gain_first, gain_second,
+    out_rows, w_query, w_key, w_value, w_output, up_first, down_first, up_second, down_second,
+    block_out, grad_tokens, dense_out, small_out, gains_out, up_one, down_one, up_two, down_two, ring_held,
+    w_held, acc, stream, total, norms, grads, cur, inbox, outbox, dense, turned,
+    keep, s_got, g_got,
+    w_sems, row_sems, a2a_send, a2a_recv, ring_send, ring_recv, dense_send, dense_recv, small_send, small_recv,
+    gain_send, gain_recv, ready, out_sem,
+):
+    b, e = lax.axis_index("batch"), lax.axis_index("expert")
+    count, wide = tokens.shape
+    many = experts * capacity
+    before, after = lax.rem(b + groups - 1, groups), lax.rem(b + 1, groups)
+    core, x, y = lax.rem(e, 2), lax.rem(e // 2, 2), lax.rem(e // 4, 2)
+    b0, b1 = lax.rem(b, 2), lax.rem(b // 2, 2)
+    other = 1 - core
+    to_core, to_x, to_y = (b, e + 1 - 2 * core), (b, e + 2 - 4 * x), (b, e + 4 - 8 * y)
+    to_low, to_high = (b + 1 - 2 * b0, e), (b + 2 - 4 * b1, e)
+
+    def remote(src, dst, send, recv, peer):
+        return pltpu.make_async_remote_copy(
+            src_ref=src, dst_ref=dst, send_sem=send, recv_sem=recv, device_id=peer, device_id_type=MESH
+        )
+
+    barrier = pltpu.get_barrier_semaphore()
+
+    def greet(p, carry):
+        peer = (b, lax.rem(e + p, experts))
+        pl.semaphore_signal(barrier, inc=1, device_id=peer, device_id_type=MESH)
+        return carry
+
+    lax.fori_loop(1, experts, greet, 0)
+    for peer in ((before, e), (after, e), to_high):
+        pl.semaphore_signal(barrier, inc=1, device_id=peer, device_id_type=MESH)
+
+    tile = wide
+    ups, downs = (up_first, up_second), (down_first, down_second)
+    gain_refs = (gain_first, gain_second)
+
+    def fetch(s, c, slot):
+        cols = pl.ds(pl.multiple_of(c * tile, tile), tile)
+        return (
+            pltpu.make_async_copy(ups[s].at[0, :, cols], w_held.at[slot], w_sems.at[slot]),
+            pltpu.make_async_copy(downs[s].at[0, cols, :], w_held.at[2 + slot], w_sems.at[2 + slot]),
+        )
+
+    def stream_tiles(s, follow, body):
+        def step(c, carry):
+            slot = lax.rem(c, 2)
+            for copy in fetch(s, c, slot):
+                copy.wait()
+
+            @pl.when(c + 1 < tiles)
+            def _():
+                for copy in fetch(s, c + 1, 1 - slot):
+                    copy.start()
+
+            if follow is not None:
+                @pl.when(c + 1 == tiles)
+                def _():
+                    for copy in fetch(follow, 0, 1 - slot):
+                        copy.start()
+
+            body(c, slot)
+            return carry
+
+        lax.fori_loop(0, tiles, step, 0)
+
+    def exchange(phase, kind, block):
+        def copy(p):
+            target = lax.rem(e + p, experts)
+            return remote(
+                block(target), inbox.at[phase, kind, e],
+                a2a_send.at[phase, kind, p], a2a_recv.at[phase, kind, p], (b, target),
+            )
+        own = pltpu.make_async_copy(block(e), inbox.at[phase, kind, e], a2a_recv.at[phase, kind, 0])
+
+        def start():
+            own.start()
+            lax.fori_loop(1, experts, lambda p, carry: (copy(p).start(), carry)[1], 0)
+
+        def wait():
+            own.wait()
+            lax.fori_loop(1, experts, lambda p, carry: (copy(p).wait(), carry)[1], 0)
+
+        return start, wait
+
+    ring_sources = (cur, grads.at[1], grads.at[0])
+
+    def ring(t, j):
+        source = ring_sources[t] if j == 1 else ring_held.at[t, j - 1]
+        return remote(source, ring_held.at[t, j], ring_send.at[t, j], ring_recv.at[t, j], (before, e))
+
+    def advance(t, j):
+        ring(t, j - 1).wait_recv()
+        ring(t, j).start()
+
+    for copy in fetch(0, 0, 0):
+        copy.start()
+    packing = pack_marks(experts, slots, capacity)
+    gains_out[...] = jnp.zeros_like(gains_out)
+    pl.semaphore_wait(barrier, experts + 2)
+
+    def out_block(kind, p):
+        return outbox.at[pl.ds(pl.multiple_of((kind * experts + p) * slots, 16), slots)]
+
+    send_routed, get_routed = exchange(0, 0, lambda p: out_rows.at[0, p])
+    send_grads, get_grads = exchange(0, 1, lambda p: out_rows.at[1, p])
+    send_result, get_result = exchange(1, 0, functools.partial(out_block, 0))
+    send_back, get_back = exchange(1, 1, functools.partial(out_block, 1))
+    send_routed()
+    send_grads()
+    get_routed()
+    arrived = dot(packing, inbox[0, 0].reshape(experts * slots, wide))
+    stream[0] = arrived
+    cur[...] = arrived.astype(BF)
+    ring(0, 1).start()
+
+    def slab(s, c):
+        return pl.ds(pl.multiple_of((s * tiles + c) * many, 8), many)
+
+    for s in range(2):
+        unit, _ = norm_parts(stream[s])
+        norms[s, 0] = (unit * gain_refs[s][...]).astype(BF)
+        total[...] = stream[s]
+
+        def forward(c, slot, s=s):
+            made = dot(norms[s, 0], w_held[slot])
+            acc[slab(s, c), :] = made
+            total[...] += dot(gelu_pair(made)[0].astype(BF), w_held[2 + slot])
+
+        stream_tiles(s, 1, forward)
+        if s == 0:
+            stream[1] = total[...]
+            get_grads()
+            grads[1] = dot(packing, inbox[0, 1].reshape(experts * slots, wide)).astype(BF)
+
+    def put_back(kind, value):
+        start = kind * experts * slots
+        outbox[start:start + experts * slots, :] = dot(packing, value, ((0,), (0,))).astype(BF)
+
+    put_back(0, total[...].astype(BF))
+    send_result()
+    advance(0, 2)
+    for s in (1, 0):
+        total[...] = jnp.zeros_like(total)
+
+        def backward(c, slot, s=s):
+            grad_mid = dot(grads[s], w_held[2 + slot], ((1,), (1,)))
+            grad_pre = (gelu_pair(acc[slab(s, c), :])[1] * grad_mid).astype(BF)
+            total[...] += dot(grad_pre, w_held[slot], ((1,), (1,)))
+
+        stream_tiles(s, 0 if s == 1 else None, backward)
+        pulled, grad_gain = norm_pull(total[...], stream[s], gain_refs[s][...])
+        gains_out[pl.ds(s, 1), :] = grad_gain
+        if s == 1:
+            grad_stream = grads[1].astype(F32) + pulled
+            stream[1] = grad_stream
+            grads[0] = grad_stream.astype(BF)
+        else:
+            put_back(1, (stream[1] + pulled).astype(BF))
+    send_back()
+    attention_weights = [
+        pltpu.make_async_copy(w, w_held.at[i], w_sems.at[i])
+        for i, w in enumerate((w_query, w_key, w_value, w_output))
+    ]
+    for i in (3, 0, 1, 2):
+        attention_weights[i].start()
+    advance(0, 3)
+    ring(1, 1).start()
+
+    def small_step(level, peer):
+        return remote(keep.at[level], s_got.at[level], small_send.at[level], small_recv.at[level], peer)
+
+    def gain_step(level, peer):
+        return remote(keep.at[5 + level, pl.ds(0, 8)], g_got.at[level], gain_send.at[level], gain_recv.at[level], peer)
+
+    keep[5, pl.ds(0, 8)] = gains_out[...]
+    gain_step(0, to_low).start()
+
+    chosen, dispatch = route_marks(routes[...], experts, slots)
+    own = select_rows(chosen, cents[...], ((0,), (0,)))
+    gating = jax.nn.sigmoid(jnp.sum(hidden[...] * own, axis=-1, keepdims=True))
+    live = (lax.broadcasted_iota(jnp.int32, (count, 1), 0) < ends[0, docs - 1]).astype(F32)
+    get_result()
+    returned = dot(dispatch, inbox[1, 0].reshape(experts * slots, wide), ((0,), (0,)))
+    block_out[...] = (live * (gating * returned + (1.0 - gating) * hidden[...])).astype(BF)
+    grad_block = live * cotangent[...].astype(F32)
+    grad_score = jnp.sum(grad_block * (returned - hidden[...]), axis=-1, keepdims=True) * gating * (1.0 - gating)
+    grad_hidden = stream.at[0, pl.ds(0, count)]
+    grad_hidden[...] = (1.0 - gating) * grad_block + grad_score * own
+    keep[0, pl.ds(8, experts)] = select_rows(chosen, grad_score * hidden[...], ((1,), (0,)))
+    normed_turned = turned.at[:, pl.ds(0, count)]
+    normed_turned[...] = normed[...].T
+    ring(0, 1).wait_send()
+    grad_low = cur.at[pl.ds(0, count)]
+    get_back()
+    grad_hidden[...] += dot(dispatch, inbox[1, 1].reshape(experts * slots, wide), ((0,), (0,)))
+    grad_low[...] = grad_hidden[...].astype(BF)
+    attention_weights[3].wait()
+    grad_mixed = dot(grad_low[...], w_held[3], ((1,), (1,))).astype(BF)
+    dense_product(dense, 3, mixed[...].T, grad_low)
+    grad_low[...] = grad_mixed
+    allowed = allowed_pairs(ends, docs, count)
+    grad_three = [outbox.at[pl.ds(i * count, count)] for i in range(3)]
+    lax.fori_loop(
+        0, wide // 128, functools.partial(backward_pair, allowed, queries, keys, values, grad_low, grad_three), 0
+    )
+    for i in range(3):
+        dense_product(dense, i, normed_turned[...], grad_three[i])
+    for i in range(3):
+        attention_weights[i].wait()
+    grad_normed = sum(dot(grad_three[i][...], w_held[i], ((1,), (1,))) for i in range(3))
+    pl.semaphore_signal(ready.at[0], inc=1, device_id=to_core, device_id_type=MESH)
+    pulled, grad_gain = norm_pull(grad_normed, tokens[...].astype(F32), gain[...])
+    grad_tokens[...] = grad_hidden[...] + pulled
+    keep[0, pl.ds(0, 8)] = jnp.broadcast_to(grad_gain, (8, wide))
+
+    def rows_at(start, size):
+        return pl.ds(pl.multiple_of(start, 32), size)
+
+    def level_copies(level):
+        copies = []
+        for m in range(4):
+            mine, theirs = dense.at[core, m], dense.at[other, m]
+            if level == 0:
+                parts = ((theirs, w_held.at[m // 2, pl.ds(m % 2 * 512, 512)], to_core),)
+            elif level == 1 and m < 2:
+                parts = ((mine.at[rows_at((1 - x) * 256, 256)], theirs.at[pl.ds(0, 256)], to_x),)
+            elif level == 1:
+                parts = tuple(
+                    (mine.at[rows_at(xx * 256 + (1 - y) * 128, 128)], theirs.at[pl.ds(xx * 128, 128)], to_y)
+                    for xx in range(2)
+                )
+            elif level == 2 and m < 2:
+                parts = ((mine.at[rows_at(x * 256 + (1 - y) * 128, 128)], theirs.at[pl.ds(256, 128)], to_y),)
+            elif level == 2:
+                parts = ((mine.at[rows_at((1 - x) * 256 + y * 128, 128)], theirs.at[pl.ds(256, 128)], to_x),)
+            elif level == 3:
+                start = x * 256 + y * 128 + (1 - b0) * 64
+                parts = ((mine.at[rows_at(start, 64)], theirs.at[pl.ds(384, 64)], to_low),)
+            else:
+                start = x * 256 + y * 128 + b0 * 64 + (1 - b1) * 32
+                parts = ((mine.at[rows_at(start, 32)], theirs.at[pl.ds(448, 32)], to_high),)
+            for n, (src, dst, peer) in enumerate(parts):
+                copies.append(remote(src, dst, dense_send.at[level, m, n], dense_recv.at[level, m, n], peer))
+        return copies
+
+    small_peers = (to_core, to_x, to_y, to_low, to_high)
+
+    def begin(level):
+        for sem in {0: (0,), 1: (1, 2), 2: (), 3: (3,), 4: (4,)}[level]:
+            pl.semaphore_wait(ready.at[sem], 1)
+        for copy in level_copies(level):
+            copy.start()
+        small_step(level, small_peers[level]).start()
+
+    def add_rows(m, start, size, got):
+        where = rows_at(start, size)
+        dense[core, m, where, :] = (dense[core, m, where, :].astype(F32) + got.astype(F32)).astype(BF)
+
+    def end(level):
+        for copy in level_copies(level):
+            copy.wait()
+        small_step(level, small_peers[level]).wait()
+        if level < 4:
+            keep[level + 1] = keep[level] + s_got[level]
+        for m in range(4):
+            if level == 0:
+                for h in range(2):
+                    add_rows(m, h * 256, 256, w_held[m // 2, m % 2 * 512 + h * 256:m % 2 * 512 + h * 256 + 256])
+            elif level == 1 and m < 2:
+                add_rows(m, x * 256, 256, dense[other, m, 0:256])
+            elif level == 1:
+                for xx in range(2):
+                    add_rows(m, xx * 256 + y * 128, 128, dense[other, m, xx * 128:xx * 128 + 128])
+            elif level == 2:
+                add_rows(m, x * 256 + y * 128, 128, dense[other, m, 256:384])
+            elif level == 3:
+                add_rows(m, x * 256 + y * 128 + b0 * 64, 64, dense[other, m, 384:448])
+            else:
+                where = rows_at(x * 256 + y * 128 + b0 * 64 + b1 * 32, 32)
+                dense_out[m] = dense[core, m, where, :].astype(F32) + dense[other, m, 448:480].astype(F32)
+        if level == 0:
+            for sem, peer in enumerate(small_peers[1:], 1):
+                pl.semaphore_signal(ready.at[sem], inc=1, device_id=peer, device_id_type=MESH)
+        if level == 4:
+            small_out[...] = keep[4] + s_got[4]
+
+    begin(0)
+    advance(1, 2)
+    ring(2, 1).start()
+    gain_step(0, to_low).wait()
+    keep[6, pl.ds(0, 8)] = keep[5, pl.ds(0, 8)] + g_got[0]
+    gain_step(1, to_high).start()
+    ring(0, 3).wait_recv()
+    for k in range(1, groups):
+        load = pltpu.make_async_copy(ring_held.at[0, k], cur, row_sems.at[0])
+        load.start()
+        load.wait()
+        routed = cur[...].astype(F32)
+        acc[(k - 1) * many:k * many, :] = routed
+        norms[0, k] = (norm_parts(routed)[0] * gain_first[...]).astype(BF)
+    end(0)
+    begin(1)
+    for copy in fetch(0, 0, 0):
+        copy.start()
+
+    def forward_others(c, slot):
+        def one_group(k, carry):
+            where = pl.ds(pl.multiple_of(k * many, 8), many)
+            mid = gelu_pair(dot(norms[0, k + 1], w_held[slot]))[0].astype(BF)
+            acc[where, :] += dot(mid, w_held[2 + slot])
+            return carry
+
+        lax.fori_loop(0, groups - 1, one_group, 0)
+
+        @pl.when(c == tiles - 2)
+        def _():
+            end(1)
+            begin(2)
+
+    stream_tiles(0, None, forward_others)
+    col = pl.multiple_of(b * width, width)
+    shards = []
+    for i, s in enumerate((1, 0)):
+        shards.append((
+            pltpu.make_async_copy(ups[s].at[0, :, pl.ds(col, width)], w_held.at[2 * i], w_sems.at[2 * i]),
+            pltpu.make_async_copy(downs[s].at[0, pl.ds(col, width), :], w_held.at[2 * i + 1], w_sems.at[2 * i + 1]),
+        ))
+    for pair in shards:
+        for copy in pair:
+            copy.start()
+    for k in range(1, groups):
+        norms[1, k] = (norm_parts(acc[(k - 1) * many:k * many, :])[0] * gain_second[...]).astype(BF)
+    advance(1, 3)
+    advance(2, 2)
+    gain_step(1, to_high).wait()
+    gains_out[...] = keep[6, pl.ds(0, 8)] + g_got[1]
+
+    def weight_phase(i, s, t, hooks):
+        for copy in shards[i]:
+            copy.wait()
+        acc[0:wide + width, :] = jnp.zeros((wide + width, wide), F32)
+
+        def step(k, carry):
+            for at, hook in hooks.items():
+                pl.when(k == at)(hook)
+
+            @pl.when(k == 0)
+            def _():
+                load = pltpu.make_async_copy(grads.at[s], cur, row_sems.at[0])
+                load.start()
+                load.wait()
+
+            @pl.when(k > 0)
+            def _():
+                load = pltpu.make_async_copy(ring_held.at[t, k], cur, row_sems.at[0])
+                load.start()
+                load.wait()
+
+            turned[...] = norms[s, k].T
+
+            def chunk(c, carry):
+                cols = pl.ds(pl.multiple_of(c * 256, 256), 256)
+                mid, slope = gelu_pair(dot(norms[s, k], w_held[2 * i, :, cols]))
+                grad_mid = dot(cur[...], w_held[2 * i + 1, cols, :], ((1,), (1,)))
+                below = pl.ds(pl.multiple_of(wide + c * 256, 256), 256)
+                acc[below, :] += dot(mid.astype(BF), cur[...], ((0,), (0,)))
+                acc[0:wide, cols] += dot(turned[...], (grad_mid * slope).astype(BF))
+                return carry
+
+            lax.fori_loop(0, width // 256, chunk, 0)
+            return carry
+
+        lax.fori_loop(0, groups, step, 0)
+        results = (
+            pltpu.make_async_copy(acc.at[pl.ds(0, wide)], (up_one, up_two)[s].at[0], out_sem.at[0, s]),
+            pltpu.make_async_copy(acc.at[pl.ds(wide, width)], (down_one, down_two)[s].at[0], out_sem.at[1, s]),
+        )
+        for copy in results:
+            copy.start()
+        for copy in results:
+            copy.wait()
+
+    def next_level(level):
+        def hook():
+            end(level)
+            begin(level + 1)
+        return hook
+
+    def late():
+        ring(1, 3).wait_recv()
+        advance(2, 3)
+
+    weight_phase(0, 1, 1, {1: next_level(2), 2: next_level(3), 3: late})
+    weight_phase(1, 0, 2, {1: lambda: end(4), 3: lambda: ring(2, 3).wait_recv()})
+    for t in range(3):
+        for j in range(1, groups):
+            if (t, j) != (0, 1):
+                ring(t, j).wait_send()
+
+
+def dense_product(dense, which, turned, right):
+    block = 32
+    for g in range(4):
+        product = dot(turned[g * 8 * block:(g + 1) * 8 * block], right[...]).astype(BF)
+        for e in range(8):
+            place = (((e // 2) % 2 * 2 + e // 4) * 4 + g % 2 * 2 + g // 2) * block
+            dense[e % 2, which, place:place + block] = product[e * block:(e + 1) * block]
+
+
+def layer(
+    ends, routes_row, tokens, cotangent, gain, cents, kept, gain_first, gain_second, out_rows, weights, expert_weights,
+    slots, capacity,
+):
+    count, wide = tokens.shape
+    experts, docs, groups = cents.shape[0], ends.shape[1], lax.axis_size("batch")
+    many, ff = experts * capacity, expert_weights[0].shape[2]
+    width, tiles = ff // groups, ff // wide
+    vmem = pl.BlockSpec(memory_space=pltpu.VMEM)
+    anys = pl.BlockSpec(memory_space=pl.ANY)
+    f32_out = jax.ShapeDtypeStruct((1, wide, width), F32)
+    dma = pltpu.SemaphoreType.DMA
+    return pl.pallas_call(
+        functools.partial(layer_kernel, experts, groups, slots, capacity, docs, width, tiles),
+        out_shape=(
+            jax.ShapeDtypeStruct((count, wide), BF),
+            jax.ShapeDtypeStruct((count, wide), F32),
+            jax.ShapeDtypeStruct((4, 32, wide), F32),
+            jax.ShapeDtypeStruct((8 + experts, wide), F32),
+            jax.ShapeDtypeStruct((8, wide), F32),
+            f32_out, f32_out, f32_out, f32_out,
+            jax.ShapeDtypeStruct((3, groups, many, wide), BF),
+        ),
+        in_specs=[pl.BlockSpec(memory_space=pltpu.SMEM)] + [vmem] * 13 + [anys] * 9,
+        out_specs=(vmem,) * 5 + (anys,) * 5,
+        scratch_shapes=[
+            pltpu.VMEM((4, wide, wide), BF),
+            pltpu.VMEM((2 * tiles * many, wide), F32),
+            pltpu.VMEM((2, many, wide), F32),
+            pltpu.VMEM((many, wide), F32),
+            pltpu.VMEM((2, groups, many, wide), BF),
+            pltpu.VMEM((2, many, wide), BF),
+            pltpu.VMEM((many, wide), BF),
+            pltpu.VMEM((2, 2, experts, slots, wide), BF),
+            pltpu.VMEM((max(2 * experts * slots, 3 * count), wide), BF),
+            pltpu.VMEM((2, 4, wide // 2, wide), BF),
+            pltpu.VMEM((wide, many), BF),
+            pltpu.VMEM((7, 16, wide), F32),
+            pltpu.VMEM((5, 16, wide), F32),
+            pltpu.VMEM((2, 8, wide), F32),
+            dma((4,)), dma((1,)), dma((2, 2, experts)), dma((2, 2, experts)),
+            dma((3, groups)), dma((3, groups)), dma((5, 4, 2)), dma((5, 4, 2)), dma((5,)), dma((5,)),
+            dma((2,)), dma((2,)), pltpu.SemaphoreType.REGULAR((5,)), dma((2, 2)),
+        ],
+        compiler_params=pltpu.CompilerParams(
+            collective_id=1, has_side_effects=True, vmem_limit_bytes=64 * 1024 * 1024 - 65536
+        ),
+        name="layer",
+    )(
+        ends, routes_row, tokens, cotangent, gain, cents, *kept, gain_first, gain_second, out_rows, *weights,
+        *expert_weights,
+    )
+
+
 def per_device(
     tokens, doc_ends, routes, w_query, w_key, w_value, w_output, attn_gain, centroids,
     up_first, down_first, gain_first, up_second, down_second, gain_second, cotangent,
@@ -706,28 +908,27 @@
     experts, groups = lax.axis_size("expert"), lax.axis_size("batch")
     capacity = 11 * count // (8 * experts)
     slots = -(-capacity // 16) * 16
-    fits = groups == 4 and experts == 8
     routes_row = routes.reshape(1, count)
     gain = attn_gain[None]
     weights = (w_query, w_key, w_value, w_output)
+    expert_weights = (up_first, down_first, up_second, down_second)
     *kept, out_rows = enter(doc_ends, routes_row, tokens, cotangent, gain, centroids, weights, slots)
-
-    def exchange(rows):
-        blocks = rows.reshape(2, experts, slots, wide)
-        return lax.all_to_all(blocks, "expert", split_axis=1, concat_axis=1, tiled=True).reshape(rows.shape)
-
-    back, rows, gains = chain(
-        exchange(out_rows), up_first, down_first, up_second, down_second, gain_first, gain_second, slots, capacity
-    )
-    block_out, grad_tokens, dense, small = leave(
-        doc_ends, routes_row, tokens, cotangent, gain, centroids, kept, exchange(back), weights, slots, fits
-    )
-    if fits:
-        *parts, dense, small, gains = finish(
-            rows, up_first, down_first, up_second, down_second, dense, small, gains
+    if groups == 4 and experts == 8:
+        block_out, grad_tokens, dense, small, gains, *parts = layer(
+            doc_ends, routes_row, tokens, cotangent, gain, centroids, kept, gain_first, gain_second, out_rows,
+            weights, expert_weights, slots, capacity,
         )
         gains = gains[:2]
     else:
+        def exchange(blocks):
+            return lax.all_to_all(blocks, "expert", split_axis=1, concat_axis=1, tiled=True)
+
+        came = exchange(out_rows).reshape(2, experts * slots, wide)
+        back, rows, gains = chain(came, *expert_weights, gain_first, gain_second, slots, capacity)
+        came_back = exchange(back.reshape(out_rows.shape)).reshape(back.shape)
+        block_out, grad_tokens, dense, small = leave(
+            doc_ends, routes_row, tokens, cotangent, gain, centroids, kept, came_back, weights, slots
+        )
         dense = scatter_sum(dense).astype(F32)
         small = all_sum(small)
         parts = []

time: 420 us -> 282 us (0.67)
  the two profiles are of different devices: /device:TPU:26 before, /device:TPU:0 now
where the time goes in v4:
time: 282 us; the launch traced here: 276 us
  Pallas kernels  241 us (85%)
  local copies, waits for them, and re-layouts  34.3 us (12%)
    pallas_call x1, Pallas kernels, layer(): pl.pallas_call(functools.partial(layer_kernel, experts, groups, slots, ca...  227 us
    unnamed x36, local copies, waits for them, and re-layouts  28.3 us
    pallas_call x1, Pallas kernels, enter(): pl.pallas_call(functools.partial(enter_kernel, experts, slots, docs), out...  14.5 us

profile of v4, /device:TPU:0, one launch (start us, length us, event | category | flops | bytes accessed | tf_op | source)
XLA Modules:
  0.0 276.4 jit_solution(4261669048028561813)
XLA Ops:
  0.6 0.0 copy-start
  0.7 1.0 copy-done
  1.7 0.0 copy-start.1
  1.7 1.0 copy-done.1
  2.7 0.0 copy-start.8
  2.7 0.8 copy-done.8
  3.5 0.0 copy-start.9
  3.5 0.7 copy-done.9
  4.2 0.0 copy-start.10
  4.2 0.7 copy-done.10
  4.9 0.0 copy-start.11
  4.9 0.7 copy-done.11
  5.5 14.5 %enter.1 = (bf16[256,1024]{1,0:T(8,128)(2,1)S(1)}, bf16[256,1024]{1,0:T(8,128)(2,1)S(1)}, bf16[256,1024]{1,0:T(8,128)(2,1)S(1)}, bf16[256,1024]{1,0:T(8,128)(2,1...) custom-call(s32[1,4]{1,0:T(1,128)S(1)} %copy-done.11, ...), custom_call_target="tpu_custom_call" | custom-call | tf_op jit(solution)/shard_map/enter/pallas_call | solution.py:147
  20.0 0.0 copy-start.2
  20.1 1.0 copy-done.2
  21.0 0.0 copy-start.3
  21.0 0.8 copy-done.3
  21.8 0.0 copy-start.4
  21.8 0.8 copy-done.4
  22.6 0.0 copy-start.5
  22.6 0.8 copy-done.5
  23.4 0.0 copy-start.6
  23.4 0.8 copy-done.6
  24.2 0.0 copy-start.7
  24.2 0.8 copy-done.7
  25.0 226.9 %layer.1 = (bf16[256,1024]{1,0:T(8,128)(2,1)}, f32[256,1024]{1,0:T(8,128)}, f32[4,32,1024]{2,1,0:T(8,128)}, f32[16,1024]{1,0:T(8,128)}, f32[8,1024]{1,0:T(8,128)...) custom-call(s32[1,4]{1,0:T(1,128)} %ends.3, ...), custom_call_target="tpu_custom_call" | custom-call | tf_op jit(solution)/shard_map/layer/pallas_call | solution.py:861
  251.8 1.9 slice_bitcast_fusion
  253.7 0.8 slice.33
  254.5 0.6 fusion
  255.1 1.4 slice.32
  256.5 1.4 slice.31
  257.8 1.9 copy.36
  259.7 2.3 copy.37
  262.0 0.0 copy-start.14
  262.0 4.9 %copy.38 = f32[1,1024,1024]{2,1,0:T(8,128)} copy(f32[1,1024,1024]{2,1,0:T(8,128)} %get-tuple-element.74) | data formatting | bytes 8388608
  267.0 0.0 copy-done.14
  267.0 0.0 copy-start.13
  267.0 2.1 copy.39
  269.1 1.6 copy-done.13
  270.7 0.0 copy-start.12
  270.7 2.1 copy.40
  272.8 1.6 copy-done.12
  274.4 2.0 copy.41
Async XLA Ops:
  0.6 1.0 copy-start
  1.7 1.0 copy-start.1
  2.7 0.8 copy-start.8
  3.5 0.7 copy-start.9
  4.2 0.7 copy-start.10
  4.9 0.7 copy-start.11
  20.0 1.0 copy-start.2
  21.0 0.8 copy-start.3
  21.8 0.8 copy-start.4
  22.6 0.8 copy-start.5
  23.4 0.8 copy-start.6
  24.2 0.8 copy-start.7
  262.0 4.9 %copy-start.14 = (f32[1,1024,1024]{2,1,0:T(8,128)S(1)}, f32[1,1024,1024]{2,1,0:T(8,128)}, u32[]{:S(2)}) copy-start(f32[1,1024,1024]{2,1,0:T(8,128)} %get-tuple-element.75) | copy-start | bytes 12582916
  267.0 3.7 %copy-start.13 = (f32[1,1024,1024]{2,1,0:T(8,128)S(1)}, f32[1,1024,1024]{2,1,0:T(8,128)}, u32[]{:S(2)}) copy-start(f32[1,1024,1024]{2,1,0:T(8,128)} %get-tuple-element.77) | copy-start | bytes 12582916
  270.7 3.7 %copy-start.12 = (f32[1,1024,1024]{2,1,0:T(8,128)S(1)}, f32[1,1024,1024]{2,1,0:T(8,128)}, u32[]{:S(2)}) copy-start(f32[1,1024,1024]{2,1,0:T(8,128)} %get-tuple-element.78) | copy-start | bytes 12582916

commit v5 on v4

--- a/solution.py
+++ b/solution.py
@@ -95,6 +95,14 @@
 def join_halves(first, second):
     lane = lax.broadcasted_iota(jnp.int32, first.shape, 1)
     return jnp.where(lane < 64, first, second)
+
+
+def forward_pair(allowed, queries, keys, values, mixed, j, carry):
+    cols = pl.ds(pl.multiple_of(j * 128, 128), 128)
+    query_pair, key_pair, value_pair = queries[:, cols], keys[:, cols], values[:, cols]
+    halves = [dot(head_shares(query_pair, key_pair, allowed, half).astype(BF), value_pair) for half in range(2)]
+    mixed[:, cols] = join_halves(*halves).astype(BF)
+    return carry
 
 
 def enter_kernel(
@@ -117,16 +125,7 @@
         result[...] = dot(normed[...], w_held[i]).astype(BF)
     allowed = allowed_pairs(ends, docs, count)
 
-    def one_pair(j, carry):
-        cols = pl.ds(pl.multiple_of(j * 128, 128), 128)
-        query_pair, key_pair, value_pair = queries[:, cols], keys[:, cols], values[:, cols]
-        halves = [
-            dot(head_shares(query_pair, key_pair, allowed, half).astype(BF), value_pair) for half in range(2)
-        ]
-        mixed[:, cols] = join_halves(*halves).astype(BF)
-        return carry
-
-    lax.fori_loop(0, wide // 128, one_pair, 0)
+    lax.fori_loop(0, wide // 128, functools.partial(forward_pair, allowed, queries, keys, values, mixed), 0)
     copies[3].wait()
     hidden[...] = tokens[...].astype(F32) + dot(mixed[...], w_held[3])
     chosen, dispatch = route_marks(routes[...], experts, slots)
@@ -435,12 +434,12 @@
 
 def layer_kernel(
     experts, groups, slots, capacity, docs, width, tiles,
-    ends, routes, tokens, cotangent, gain, cents, normed, queries, keys, values, mixed, hidden, gain_first, gain_second,
-    out_rows, w_query, w_key, w_value, w_output, up_first, down_first, up_second, down_second,
+    ends, routes, tokens, cotangent, gain, cents, gain_first, gain_second,
+    w_query, w_key, w_value, w_output, up_first, down_first, up_second, down_second,
     block_out, grad_tokens, dense_out, small_out, gains_out, up_one, down_one, up_two, down_two, ring_held,
-    w_held, acc, stream, total, norms, grads, cur, inbox, outbox, dense, turned,
+    w_held, slopes, stream, norms, grads, cur, attention, hidden, dispatch, inbox, outbox, dense, turned, middles,
     keep, s_got, g_got,
-    w_sems, row_sems, a2a_send, a2a_recv, ring_send, ring_recv, dense_send, dense_recv, small_send, small_recv,
+    w_sems, row_sem, a2a_send, a2a_recv, ring_send, ring_recv, dense_send, dense_recv, small_send, small_recv,
     gain_send, gain_recv, ready, out_sem,
 ):
     b, e = lax.axis_index("batch"), lax.axis_index("expert")
@@ -521,39 +520,68 @@
 
         return start, wait
 
-    ring_sources = (cur, grads.at[1], grads.at[0])
 
     def ring(t, j):
-        source = ring_sources[t] if j == 1 else ring_held.at[t, j - 1]
-        return remote(source, ring_held.at[t, j], ring_send.at[t, j], ring_recv.at[t, j], (before, e))
+        if t == 0:
+            source, target = cur if j == 1 else ring_held.at[j - 1], ring_held.at[j]
+        else:
+            source, target = grads.at[2 - t, j - 1], grads.at[2 - t, j]
+        return remote(source, target, ring_send.at[t, j], ring_recv.at[t, j], (before, e))
 
     def advance(t, j):
         ring(t, j - 1).wait_recv()
         ring(t, j).start()
 
+    attention_weights = [
+        pltpu.make_async_copy(w, w_held.at[i], w_sems.at[i])
+        for i, w in enumerate((w_query, w_key, w_value, w_output))
+    ]
+    for copy in attention_weights:
+        copy.start()
+    normed, queries, keys, values, mixed = (attention.at[i] for i in range(5))
+    normed[...] = (norm_parts(tokens[...].astype(F32))[0] * gain[...]).astype(BF)
+    for i, result in enumerate((queries, keys, values)):
+        attention_weights[i].wait()
+        result[...] = dot(normed[...], w_held[i]).astype(BF)
     for copy in fetch(0, 0, 0):
         copy.start()
+    allowed = allowed_pairs(ends, docs, count)
+    lax.fori_loop(0, wide // 128, functools.partial(forward_pair, allowed, queries, keys, values, mixed), 0)
+    attention_weights[3].wait()
+    hidden[...] = tokens[...].astype(F32) + dot(mixed[...], w_held[3])
+    chosen, marks = route_marks(routes[...], experts, slots)
+    dispatch[...] = marks
+    own = select_rows(chosen, cents[...], ((0,), (0,)))
+    gating = jax.nn.sigmoid(jnp.sum(hidden[...] * own, axis=-1, keepdims=True))
+    live = (lax.broadcasted_iota(jnp.int32, (count, 1), 0) < ends[0, docs - 1]).astype(F32)
+
+    def out_block(kind, p):
+        return outbox.at[pl.ds(pl.multiple_of((kind * experts + p) * slots, 16), slots)]
+
+    def put_out(kind, marks, value, dims):
+        start = kind * experts * slots
+        outbox[start:start + experts * slots, :] = dot(marks, value, dims).astype(BF)
+
+    send_routed, get_routed = exchange(0, 0, functools.partial(out_block, 0))
+    send_grads, get_grads = exchange(0, 1, functools.partial(out_block, 1))
+    send_result, get_result = exchange(1, 0, functools.partial(out_block, 0))
+    send_back, get_back = exchange(1, 1, functools.partial(out_block, 1))
+    put_out(0, dispatch[...], hidden[...].astype(BF), ((1,), (0,)))
+    pl.semaphore_wait(barrier, experts + 2)
+    send_routed()
+    put_out(1, dispatch[...], (gating * (live * cotangent[...].astype(F32))).astype(BF), ((1,), (0,)))
+    send_grads()
     packing = pack_marks(experts, slots, capacity)
     gains_out[...] = jnp.zeros_like(gains_out)
-    pl.semaphore_wait(barrier, experts + 2)
-
-    def out_block(kind, p):
-        return outbox.at[pl.ds(pl.multiple_of((kind * experts + p) * slots, 16), slots)]
-
-    send_routed, get_routed = exchange(0, 0, lambda p: out_rows.at[0, p])
-    send_grads, get_grads = exchange(0, 1, lambda p: out_rows.at[1, p])
-    send_result, get_result = exchange(1, 0, functools.partial(out_block, 0))
-    send_back, get_back = exchange(1, 1, functools.partial(out_block, 1))
-    send_routed()
-    send_grads()
     get_routed()
     arrived = dot(packing, inbox[0, 0].reshape(experts * slots, wide))
     stream[0] = arrived
     cur[...] = arrived.astype(BF)
     ring(0, 1).start()
+    total = stream.at[2]
 
     def slab(s, c):
-        return pl.ds(pl.multiple_of((s * tiles + c) * many, 8), many)
+        return pl.ds(pl.multiple_of((s * tiles + c) * many, 16), many)
 
     for s in range(2):
         unit, _ = norm_parts(stream[s])
@@ -562,44 +590,38 @@
 
         def forward(c, slot, s=s):
             made = dot(norms[s, 0], w_held[slot])
-            acc[slab(s, c), :] = made
-            total[...] += dot(gelu_pair(made)[0].astype(BF), w_held[2 + slot])
+            value, slope = gelu_pair(made)
+            slopes[slab(s, c), :] = slope.astype(BF)
+            total[...] += dot(value.astype(BF), w_held[2 + slot])
 
         stream_tiles(s, 1, forward)
         if s == 0:
             stream[1] = total[...]
             get_grads()
-            grads[1] = dot(packing, inbox[0, 1].reshape(experts * slots, wide)).astype(BF)
-
-    def put_back(kind, value):
-        start = kind * experts * slots
-        outbox[start:start + experts * slots, :] = dot(packing, value, ((0,), (0,))).astype(BF)
-
-    put_back(0, total[...].astype(BF))
+            grads[1, 0] = dot(packing, inbox[0, 1].reshape(experts * slots, wide)).astype(BF)
+
+    put_out(0, packing, total[...].astype(BF), ((0,), (0,)))
     send_result()
     advance(0, 2)
     for s in (1, 0):
         total[...] = jnp.zeros_like(total)
 
         def backward(c, slot, s=s):
-            grad_mid = dot(grads[s], w_held[2 + slot], ((1,), (1,)))
-            grad_pre = (gelu_pair(acc[slab(s, c), :])[1] * grad_mid).astype(BF)
+            grad_mid = dot(grads[s, 0], w_held[2 + slot], ((1,), (1,)))
+            grad_pre = (slopes[slab(s, c), :].astype(F32) * grad_mid).astype(BF)
             total[...] += dot(grad_pre, w_held[slot], ((1,), (1,)))
 
         stream_tiles(s, 0 if s == 1 else None, backward)
         pulled, grad_gain = norm_pull(total[...], stream[s], gain_refs[s][...])
         gains_out[pl.ds(s, 1), :] = grad_gain
         if s == 1:
-            grad_stream = grads[1].astype(F32) + pulled
+            grad_stream = grads[1, 0].astype(F32) + pulled
             stream[1] = grad_stream
-            grads[0] = grad_stream.astype(BF)
+            grads[0, 0] = grad_stream.astype(BF)
         else:
-            put_back(1, (stream[1] + pulled).astype(BF))
+            put_out(1, packing, (stream[1] + pulled).astype(BF), ((0,), (0,)))
     send_back()
-    attention_weights = [
-        pltpu.make_async_copy(w, w_held.at[i], w_sems.at[i])
-        for i, w in enumerate((w_query, w_key, w_value, w_output))
-    ]
+    pl.semaphore_signal(ready.at[0], inc=1, device_id=to_core, device_id_type=MESH)
     for i in (3, 0, 1, 2):
         attention_weights[i].start()
     advance(0, 3)
@@ -614,16 +636,13 @@
     keep[5, pl.ds(0, 8)] = gains_out[...]
     gain_step(0, to_low).start()
 
-    chosen, dispatch = route_marks(routes[...], experts, slots)
-    own = select_rows(chosen, cents[...], ((0,), (0,)))
-    gating = jax.nn.sigmoid(jnp.sum(hidden[...] * own, axis=-1, keepdims=True))
-    live = (lax.broadcasted_iota(jnp.int32, (count, 1), 0) < ends[0, docs - 1]).astype(F32)
     get_result()
-    returned = dot(dispatch, inbox[1, 0].reshape(experts * slots, wide), ((0,), (0,)))
+    returned = dot(dispatch[...], inbox[1, 0].reshape(experts * slots, wide), ((0,), (0,)))
     block_out[...] = (live * (gating * returned + (1.0 - gating) * hidden[...])).astype(BF)
     grad_block = live * cotangent[...].astype(F32)
     grad_score = jnp.sum(grad_block * (returned - hidden[...]), axis=-1, keepdims=True) * gating * (1.0 - gating)
     grad_hidden = stream.at[0, pl.ds(0, count)]
+    own = select_rows(chosen, cents[...], ((0,), (0,)))
     grad_hidden[...] = (1.0 - gating) * grad_block + grad_score * own
     keep[0, pl.ds(8, experts)] = select_rows(chosen, grad_score * hidden[...], ((1,), (0,)))
     normed_turned = turned.at[:, pl.ds(0, count)]
@@ -631,13 +650,12 @@
     ring(0, 1).wait_send()
     grad_low = cur.at[pl.ds(0, count)]
     get_back()
-    grad_hidden[...] += dot(dispatch, inbox[1, 1].reshape(experts * slots, wide), ((0,), (0,)))
+    grad_hidden[...] += dot(dispatch[...], inbox[1, 1].reshape(experts * slots, wide), ((0,), (0,)))
     grad_low[...] = grad_hidden[...].astype(BF)
     attention_weights[3].wait()
     grad_mixed = dot(grad_low[...], w_held[3], ((1,), (1,))).astype(BF)
     dense_product(dense, 3, mixed[...].T, grad_low)
     grad_low[...] = grad_mixed
-    allowed = allowed_pairs(ends, docs, count)
     grad_three = [outbox.at[pl.ds(i * count, count)] for i in range(3)]
     lax.fori_loop(
         0, wide // 128, functools.partial(backward_pair, allowed, queries, keys, values, grad_low, grad_three), 0
@@ -647,7 +665,6 @@
     for i in range(3):
         attention_weights[i].wait()
     grad_normed = sum(dot(grad_three[i][...], w_held[i], ((1,), (1,))) for i in range(3))
-    pl.semaphore_signal(ready.at[0], inc=1, device_id=to_core, device_id_type=MESH)
     pulled, grad_gain = norm_pull(grad_normed, tokens[...].astype(F32), gain[...])
     grad_tokens[...] = grad_hidden[...] + pulled
     keep[0, pl.ds(0, 8)] = jnp.broadcast_to(grad_gain, (8, wide))
@@ -660,7 +677,7 @@
         for m in range(4):
             mine, theirs = dense.at[core, m], dense.at[other, m]
             if level == 0:
-                parts = ((theirs, w_held.at[m // 2, pl.ds(m % 2 * 512, 512)], to_core),)
+                parts = ((theirs, slopes.at[pl.ds(m * 512, 512)], to_core),)
             elif level == 1 and m < 2:
                 parts = ((mine.at[rows_at((1 - x) * 256, 256)], theirs.at[pl.ds(0, 256)], to_x),)
             elif level == 1:
@@ -704,7 +721,7 @@
         for m in range(4):
             if level == 0:
                 for h in range(2):
-                    add_rows(m, h * 256, 256, w_held[m // 2, m % 2 * 512 + h * 256:m % 2 * 512 + h * 256 + 256])
+                    add_rows(m, h * 256, 256, slopes[m * 512 + h * 256:m * 512 + h * 256 + 256])
             elif level == 1 and m < 2:
                 add_rows(m, x * 256, 256, dense[other, m, 0:256])
             elif level == 1:
@@ -730,31 +747,28 @@
     keep[6, pl.ds(0, 8)] = keep[5, pl.ds(0, 8)] + g_got[0]
     gain_step(1, to_high).start()
     ring(0, 3).wait_recv()
+    for copy in fetch(0, 0, 0):
+        copy.start()
     for k in range(1, groups):
-        load = pltpu.make_async_copy(ring_held.at[0, k], cur, row_sems.at[0])
+        load = pltpu.make_async_copy(ring_held.at[k], cur, row_sem.at[0])
         load.start()
         load.wait()
         routed = cur[...].astype(F32)
-        acc[(k - 1) * many:k * many, :] = routed
+        stream[k - 1] = routed
         norms[0, k] = (norm_parts(routed)[0] * gain_first[...]).astype(BF)
-    end(0)
-    begin(1)
-    for copy in fetch(0, 0, 0):
-        copy.start()
 
     def forward_others(c, slot):
         def one_group(k, carry):
-            where = pl.ds(pl.multiple_of(k * many, 8), many)
             mid = gelu_pair(dot(norms[0, k + 1], w_held[slot]))[0].astype(BF)
-            acc[where, :] += dot(mid, w_held[2 + slot])
+            stream[k] += dot(mid, w_held[2 + slot])
             return carry
 
         lax.fori_loop(0, groups - 1, one_group, 0)
 
-        @pl.when(c == tiles - 2)
+        @pl.when(c == 1)
         def _():
-            end(1)
-            begin(2)
+            end(0)
+            begin(1)
 
     stream_tiles(0, None, forward_others)
     col = pl.multiple_of(b * width, width)
@@ -768,55 +782,82 @@
         for copy in pair:
             copy.start()
     for k in range(1, groups):
-        norms[1, k] = (norm_parts(acc[(k - 1) * many:k * many, :])[0] * gain_second[...]).astype(BF)
+        norms[1, k] = (norm_parts(stream[k - 1])[0] * gain_second[...]).astype(BF)
     advance(1, 3)
     advance(2, 2)
     gain_step(1, to_high).wait()
     gains_out[...] = keep[6, pl.ds(0, 8)] + g_got[1]
 
-    def weight_phase(i, s, t, hooks):
+    quarter = wide // 4
+    every = groups * many
+
+    def stage_copies(n, s, c, slot):
+        stage = stream.at[slot]
+        cols = pl.ds(pl.multiple_of(c * quarter, quarter), quarter)
+        if n == 0:
+            return (pltpu.make_async_copy(stage.at[pl.ds(0, quarter)], (down_one, down_two)[s].at[0, cols], out_sem.at[slot, 0]),)
+        return tuple(
+            pltpu.make_async_copy(
+                stage.at[pl.ds(0, quarter), pl.ds(r * quarter, quarter)],
+                (up_one, up_two)[s].at[0, pl.ds(r * quarter, quarter), cols], out_sem.at[slot, 1 + r],
+            )
+            for r in range(4)
+        )
+
+    def weight_phase(i, s, hooks):
         for copy in shards[i]:
             copy.wait()
-        acc[0:wide + width, :] = jnp.zeros((wide + width, wide), F32)
-
-        def step(k, carry):
+
+        def turn(d, carry):
+            cols = pl.ds(pl.multiple_of(d * 128, 128), 128)
+            turned[cols, :] = norms[s, :, :, cols].reshape(every, 128).T
+            return carry
+
+        lax.fori_loop(0, wide // 128, turn, 0)
+
+        def chunk(c, carry):
+            cols = pl.ds(pl.multiple_of(c * quarter, quarter), quarter)
+
+            def one_group(k, carry):
+                where = pl.ds(pl.multiple_of(k * many, 16), many)
+                mid, slope = gelu_pair(dot(norms[s, k], w_held[2 * i, :, cols]))
+                middles[0, where, :] = mid.astype(BF)
+                grad_mid = dot(grads[s, k], w_held[2 * i + 1, cols, :], ((1,), (1,)))
+                middles[1, where, :] = (grad_mid * slope).astype(BF)
+                return carry
+
+            lax.fori_loop(0, groups, one_group, 0)
+            slot = lax.rem(c, 2)
+
+            @pl.when(c > 1)
+            def _():
+                for copy in stage_copies(0, s, c - 2, slot):
+                    copy.wait()
+
+            stream[slot, 0:quarter, :] = dot(middles[0], grads[s].reshape(every, wide), ((0,), (0,)))
+            for copy in stage_copies(0, s, c, slot):
+                copy.start()
+
+            @pl.when(c > 0)
+            def _():
+                for copy in stage_copies(1, s, c - 1, 2):
+                    copy.wait()
+
+            product = dot(turned[...], middles[1])
+            for r in range(4):
+                stream[2, 0:quarter, r * quarter:(r + 1) * quarter] = product[r * quarter:(r + 1) * quarter]
+            for copy in stage_copies(1, s, c, 2):
+                copy.start()
             for at, hook in hooks.items():
-                pl.when(k == at)(hook)
-
-            @pl.when(k == 0)
-            def _():
-                load = pltpu.make_async_copy(grads.at[s], cur, row_sems.at[0])
-                load.start()
-                load.wait()
-
-            @pl.when(k > 0)
-            def _():
-                load = pltpu.make_async_copy(ring_held.at[t, k], cur, row_sems.at[0])
-                load.start()
-                load.wait()
-
-            turned[...] = norms[s, k].T
-
-            def chunk(c, carry):
-                cols = pl.ds(pl.multiple_of(c * 256, 256), 256)
-                mid, slope = gelu_pair(dot(norms[s, k], w_held[2 * i, :, cols]))
-                grad_mid = dot(cur[...], w_held[2 * i + 1, cols, :], ((1,), (1,)))
-                below = pl.ds(pl.multiple_of(wide + c * 256, 256), 256)
-                acc[below, :] += dot(mid.astype(BF), cur[...], ((0,), (0,)))
-                acc[0:wide, cols] += dot(turned[...], (grad_mid * slope).astype(BF))
-                return carry
-
-            lax.fori_loop(0, width // 256, chunk, 0)
+                pl.when(c == at)(hook)
             return carry
 
-        lax.fori_loop(0, groups, step, 0)
-        results = (
-            pltpu.make_async_copy(acc.at[pl.ds(0, wide)], (up_one, up_two)[s].at[0], out_sem.at[0, s]),
-            pltpu.make_async_copy(acc.at[pl.ds(wide, width)], (down_one, down_two)[s].at[0], out_sem.at[1, s]),
-        )
-        for copy in results:
-            copy.start()
-        for copy in results:
+        chunks = width // quarter
+        lax.fori_loop(0, chunks, chunk, 0)
+        for c in (chunks - 2, chunks - 1):
+            for copy in stage_copies(0, s, c, c % 2):
+                copy.wait()
+        for copy in stage_copies(1, s, chunks - 1, 2):
             copy.wait()
 
     def next_level(level):
@@ -825,12 +866,11 @@
             begin(level + 1)
         return hook
 
-    def late():
-        ring(1, 3).wait_recv()
-        advance(2, 3)
-
-    weight_phase(0, 1, 1, {1: next_level(2), 2: next_level(3), 3: late})
-    weight_phase(1, 0, 2, {1: lambda: end(4), 3: lambda: ring(2, 3).wait_recv()})
+    ring(1, 3).wait_recv()
+    advance(2, 3)
+    weight_phase(0, 1, {1: next_level(1), 3: next_level(2)})
+    ring(2, 3).wait_recv()
+    weight_phase(1, 0, {1: next_level(3), 3: lambda: end(4)})
     for t in range(3):
         for j in range(1, groups):
             if (t, j) != (0, 1):
@@ -847,8 +887,7 @@
 
 
 def layer(
-    ends, routes_row, tokens, cotangent, gain, cents, kept, gain_first, gain_second, out_rows, weights, expert_weights,
-    slots, capacity,
+    ends, routes_row, tokens, cotangent, gain, cents, gain_first, gain_second, weights, expert_weights, slots, capacity,
 ):
     count, wide = tokens.shape
     experts, docs, groups = cents.shape[0], ends.shape[1], lax.axis_size("batch")
@@ -867,36 +906,38 @@
             jax.ShapeDtypeStruct((8 + experts, wide), F32),
             jax.ShapeDtypeStruct((8, wide), F32),
             f32_out, f32_out, f32_out, f32_out,
-            jax.ShapeDtypeStruct((3, groups, many, wide), BF),
+            jax.ShapeDtypeStruct((groups, many, wide), BF),
         ),
-        in_specs=[pl.BlockSpec(memory_space=pltpu.SMEM)] + [vmem] * 13 + [anys] * 9,
+        in_specs=[pl.BlockSpec(memory_space=pltpu.SMEM)] + [vmem] * 7 + [anys] * 8,
         out_specs=(vmem,) * 5 + (anys,) * 5,
         scratch_shapes=[
             pltpu.VMEM((4, wide, wide), BF),
-            pltpu.VMEM((2 * tiles * many, wide), F32),
-            pltpu.VMEM((2, many, wide), F32),
-            pltpu.VMEM((many, wide), F32),
+            pltpu.VMEM((2 * tiles * many, wide), BF),
+            pltpu.VMEM((3, many, wide), F32),
             pltpu.VMEM((2, groups, many, wide), BF),
-            pltpu.VMEM((2, many, wide), BF),
+            pltpu.VMEM((2, groups, many, wide), BF),
             pltpu.VMEM((many, wide), BF),
+            pltpu.VMEM((5, count, wide), BF),
+            pltpu.VMEM((count, wide), F32),
+            pltpu.VMEM((experts * slots, count), BF),
             pltpu.VMEM((2, 2, experts, slots, wide), BF),
             pltpu.VMEM((max(2 * experts * slots, 3 * count), wide), BF),
             pltpu.VMEM((2, 4, wide // 2, wide), BF),
-            pltpu.VMEM((wide, many), BF),
+            pltpu.VMEM((wide, groups * many), BF),
+            pltpu.VMEM((2, groups * many, wide // 4), BF),
             pltpu.VMEM((7, 16, wide), F32),
             pltpu.VMEM((5, 16, wide), F32),
             pltpu.VMEM((2, 8, wide), F32),
             dma((4,)), dma((1,)), dma((2, 2, experts)), dma((2, 2, experts)),
             dma((3, groups)), dma((3, groups)), dma((5, 4, 2)), dma((5, 4, 2)), dma((5,)), dma((5,)),
-            dma((2,)), dma((2,)), pltpu.SemaphoreType.REGULAR((5,)), dma((2, 2)),
+            dma((2,)), dma((2,)), pltpu.SemaphoreType.REGULAR((5,)), dma((3, 5)),
         ],
         compiler_params=pltpu.CompilerParams(
             collective_id=1, has_side_effects=True, vmem_limit_bytes=64 * 1024 * 1024 - 65536
         ),
         name="layer",
     )(
-        ends, routes_row, tokens, cotangent, gain, cents, *kept, gain_first, gain_second, out_rows, *weights,
-        *expert_weights,
+        ends, routes_row, tokens, cotangent, gain, cents, gain_first, gain_second, *weights, *expert_weights,
     )
 
 
@@ -912,14 +953,15 @@
     gain = attn_gain[None]
     weights = (w_query, w_key, w_value, w_output)
     expert_weights = (up_first, down_first, up_second, down_second)
-    *kept, out_rows = enter(doc_ends, routes_row, tokens, cotangent, gain, centroids, weights, slots)
     if groups == 4 and experts == 8:
         block_out, grad_tokens, dense, small, gains, *parts = layer(
-            doc_ends, routes_row, tokens, cotangent, gain, centroids, kept, gain_first, gain_second, out_rows,
-            weights, expert_weights, slots, capacity,
+            doc_ends, routes_row, tokens, cotangent, gain, centroids, gain_first, gain_second, weights, expert_weights,
+            slots, capacity,
         )
         gains = gains[:2]
     else:
+        *kept, out_rows = enter(doc_ends, routes_row, tokens, cotangent, gain, centroids, weights, slots)
+
         def exchange(blocks):
             return lax.all_to_all(blocks, "expert", split_axis=1, concat_axis=1, tiled=True)
 

time: 282 us -> 250 us (0.89); the launches traced: 276 us -> 249 us
  Pallas kernels: 241 us -> 225 us
  local copies, waits for them, and re-layouts: 34.3 us -> 23.5 us
    pallas_call x1 -> x0, Pallas kernels: 14.5 us -> none  [enter(): pl.pallas_call(functools.partial(enter_kernel, experts, slots, docs), out...]
    unnamed x36 -> x14, local copies, waits for them, and re-layouts: 28.3 us -> 17.3 us
where the time goes in v5:
time: 250 us; the launch traced here: 249 us
  Pallas kernels  225 us (90%)
  local copies, waits for them, and re-layouts  23.5 us (9%)
    pallas_call x1, Pallas kernels, layer(): pl.pallas_call(functools.partial(layer_kernel, experts, groups, slots, ca...  225 us
    unnamed x14, local copies, waits for them, and re-layouts  17.3 us

profile of v5, /device:TPU:0, one launch (start us, length us, event | category | flops | bytes accessed | tf_op | source)
XLA Modules:
  0.0 249.4 jit_solution(15949780912463756964)
XLA Ops:
  0.7 225.3 %layer.1 = (bf16[256,1024]{1,0:T(8,128)(2,1)}, f32[256,1024]{1,0:T(8,128)}, f32[4,32,1024]{2,1,0:T(8,128)}, f32[16,1024]{1,0:T(8,128)}, f32[8,1024]{1,0:T(8,128)...) custom-call(s32[1,4]{1,0:T(1,128)} %ends.1, ...), custom_call_target="tpu_custom_call" | custom-call | tf_op jit(solution)/shard_map/layer/pallas_call | solution.py:900
  225.9 0.0 copy-start.3
  225.9 1.5 slice.31
  227.4 1.4 slice.32
  228.8 0.8 slice.33
  229.6 0.6 fusion
  230.2 1.9 slice_bitcast_fusion
  232.1 1.9 copy.36
  234.0 2.3 copy.37
  236.3 0.0 copy-done.3
  236.3 0.0 copy-start.2
  236.3 2.1 copy.38
  238.4 1.6 copy-done.2
  240.0 0.0 copy-start.1
  240.0 2.1 copy.39
  242.1 1.6 copy-done.1
  243.7 0.0 copy-start
  243.7 2.1 copy.40
  245.8 1.6 copy-done
  247.4 2.0 copy.41
Async XLA Ops:
  225.9 10.4 %copy-start.3 = (f32[1,1024,1024]{2,1,0:T(8,128)S(1)}, f32[1,1024,1024]{2,1,0:T(8,128)}, u32[]{:S(2)}) copy-start(f32[1,1024,1024]{2,1,0:T(8,128)} %get-tuple-element.60) | copy-start | bytes 12582916
  236.3 3.7 %copy-start.2 = (f32[1,1024,1024]{2,1,0:T(8,128)S(1)}, f32[1,1024,1024]{2,1,0:T(8,128)}, u32[]{:S(2)}) copy-start(f32[1,1024,1024]{2,1,0:T(8,128)} %get-tuple-element.61) | copy-start | bytes 12582916
  240.0 3.7 %copy-start.1 = (f32[1,1024,1024]{2,1,0:T(8,128)S(1)}, f32[1,1024,1024]{2,1,0:T(8,128)}, u32[]{:S(2)}) copy-start(f32[1,1024,1024]{2,1,0:T(8,128)} %get-tuple-element.63) | copy-start | bytes 12582916
  243.7 3.7 %copy-start = (f32[1,1024,1024]{2,1,0:T(8,128)S(1)}, f32[1,1024,1024]{2,1,0:T(8,128)}, u32[]{:S(2)}) copy-start(f32[1,1024,1024]{2,1,0:T(8,128)} %get-tuple-element.64) | copy-start | bytes 12582916
